TPU v7x, 256 devices: a whole 4x4x8 slice. The times are simulated.
256 devices in a mesh: dp: 8 (over z_lo, core), mp: 16 (over x, y), group: 2 (over z_hi).
Axes of the slice: x: 4, y: 4, z: 8 (z_hi: 2, z_lo: 4; z = z_hi * 4 + z_lo), core: 2. Of those that a mesh axis runs over, the one named last changes fastest.
Arguments:
- hidden: bfloat16 [1024, 8192], P('dp', 'mp'), may hold values from -6 to 6
- neighbour_ids: int32 [16, 2, 128], P('dp', 'group'), may hold values from 0 to 65535, as said below
- counts: int32 [16], P('dp'), may hold values from 0 to 2
- embed_table: bfloat16 [65536, 8192], P(('dp', 'group'), 'mp'), may hold values from -6 to 6
- w_query: bfloat16 [8192, 4096], P('group', 'mp'), may hold values from -0.0625 to 0.0625
- w_key: bfloat16 [8192, 4096], P('group', 'mp'), may hold values from -0.0625 to 0.0625
- w_value: bfloat16 [8192, 4096], P('group', 'mp'), may hold values from -0.0625 to 0.0625
- w_out: bfloat16 [4096, 8192], P('mp', 'group'), may hold values from -0.09375 to 0.09375
- grad_out: bfloat16 [1024, 8192], P('dp', 'mp'), may hold values from -6 to 6
Outputs:
- output: float32 [1024, 8192], P('dp', 'mp')
- grad_hidden: float32 [1024, 8192], P('dp', 'mp')
- grad_neighbours: float32 [16, 2, 128, 8192], P('dp', 'group', None, 'mp')
Inputs may be any that keep to these rules, and one draw needn't show every extreme that they name: `neighbour_ids`: token ids of the retrieved neighbours; the ids are split into 16 owners of 4096 consecutive ids each; of the 256 ids of one window's neighbour k (blocks of one window, one k), at most 64 belong to one owner, and exactly 64 belong to some owner. neighbours k < counts[c] of block c are used, the others are masked.
All inputs are finite; a program needn't handle non-finite values.
Results may differ from a plain program's by a relative error of at most 0.019.
Values may be sent and summed in bfloat16 or wider, within the bound.
A program may use at most 128 MiB of HBM per device.

v0:
```python
import math

import jax
import jax.numpy as jnp
from jax import lax
from jax.sharding import PartitionSpec as P

HD = 128
BLOCK = 64
RET = 128


def contract(left, right):
    return lax.dot_general(
        left, right, (((1,), (1,)), ((), ())), preferred_element_type=jnp.float32
    )


def per_device(
    hidden, neighbour_ids, counts, embed_table, w_query, w_key, w_value, w_out, grad_out
):
    tail_rows = BLOCK - 1
    rows_here = hidden.shape[0]
    blocks_here = rows_here // BLOCK
    heads_here = w_query.shape[1] // HD
    inv_root = 1.0 / math.sqrt(HD)
    keep_rows = rows_here - tail_rows
    pad_rows = jnp.zeros((tail_rows, hidden.shape[1]), jnp.bfloat16)
    query_rows = jnp.concatenate([hidden[tail_rows:], pad_rows], 0)
    grad_rows = jnp.concatenate([grad_out[tail_rows:], pad_rows], 0)
    full_query, full_grad = (
        lax.all_gather(query_rows, "mp", axis=1, tiled=True),
        lax.all_gather(grad_rows, "mp", axis=1, tiled=True),
    )
    flat_ids = neighbour_ids.reshape(-1)
    block_rows = embed_table.shape[0]
    every_id = lax.all_gather(flat_ids, ("dp", "group"), axis=0, tiled=True)
    owner = lax.axis_index("dp") * lax.axis_size("group") + lax.axis_index("group")
    local_ids = every_id - owner * block_rows
    inside = (local_ids >= 0) & (local_ids < block_rows)
    picked = embed_table[jnp.clip(local_ids, 0, block_rows - 1)]
    picked = jnp.where(inside[:, None], picked, jnp.zeros_like(picked))
    own_cols = (
        lax.psum_scatter(picked, ("dp", "group"), scatter_dimension=0, tiled=True)
        .astype(jnp.float32)
        .astype(jnp.bfloat16)
    )
    neighbours = lax.all_gather(own_cols, "mp", axis=1, tiled=True)
    wq_full, wk_full, wv_full = (
        lax.all_gather(w_query, "group", axis=0, tiled=True),
        lax.all_gather(w_key, "group", axis=0, tiled=True),
        lax.all_gather(w_value, "group", axis=0, tiled=True),
    )
    query_sum = jnp.dot(full_query, wq_full, preferred_element_type=jnp.float32)
    query = query_sum.astype(jnp.bfloat16)
    wo_full = lax.all_gather(w_out, "group", axis=1, tiled=True)
    keys = jnp.dot(neighbours, wk_full, preferred_element_type=jnp.float32).astype(jnp.bfloat16)
    values = jnp.dot(neighbours, wv_full, preferred_element_type=jnp.float32).astype(jnp.bfloat16)
    key_block = keys.reshape(blocks_here, RET, heads_here, HD)
    value_block = values.reshape(blocks_here, RET, heads_here, HD)
    query_block = query.reshape(blocks_here, BLOCK, heads_here, HD)
    live = (counts > lax.axis_index("group")).astype(jnp.float32)
    scores = (
        jnp.einsum("cqhd,ckhd->chqk", query_block, key_block, preferred_element_type=jnp.float32)
        * inv_root
    )
    weights = jnp.exp(scores) * live[:, None, None, None]
    numer = jnp.einsum(
        "chqk,ckhd->cqhd",
        weights.astype(jnp.bfloat16),
        value_block,
        preferred_element_type=jnp.float32,
    )
    partial_total = jnp.sum(weights, -1)
    numer, partial_total = lax.psum((numer, partial_total), "group")
    total = partial_total + 1.0
    attn = numer / jnp.transpose(total, (0, 2, 1))[..., None]
    attn_bf = attn.reshape(rows_here, heads_here * HD).astype(jnp.bfloat16)
    out_term = jnp.dot(attn_bf, wo_full, preferred_element_type=jnp.float32)
    d_attn = contract(full_grad, wo_full).astype(jnp.bfloat16)
    d_block = d_attn.reshape(blocks_here, BLOCK, heads_here, HD)
    prob = weights / total[..., None]
    d_prob = jnp.einsum("cqhd,ckhd->chqk", d_block, value_block, preferred_element_type=jnp.float32)
    delta = jnp.sum(d_block.astype(jnp.float32) * attn, -1)
    d_score = (prob * (d_prob - jnp.transpose(delta, (0, 2, 1))[..., None])).astype(jnp.bfloat16)
    query_part = jnp.einsum(
        "chqk,ckhd->cqhd", d_score, key_block, preferred_element_type=jnp.float32
    )
    query_grad = lax.psum(query_part, "group")
    d_query = (query_grad * inv_root).astype(jnp.bfloat16).reshape(rows_here, heads_here * HD)
    d_keys = (
        jnp.einsum("chqk,cqhd->ckhd", d_score, query_block, preferred_element_type=jnp.float32)
        * inv_root
    ).astype(jnp.bfloat16)
    d_values = jnp.einsum(
        "chqk,cqhd->ckhd", prob.astype(jnp.bfloat16), d_block, preferred_element_type=jnp.float32
    ).astype(jnp.bfloat16)
    d_keys = d_keys.reshape(blocks_here * RET, heads_here * HD)
    d_values = d_values.reshape(blocks_here * RET, heads_here * HD)
    hid_term = contract(d_query, wq_full)
    out_cols, hid_cols = (
        lax.psum_scatter(
            out_term.astype(jnp.bfloat16), "mp", scatter_dimension=1, tiled=True
        ).astype(jnp.float32),
        lax.psum_scatter(
            hid_term.astype(jnp.bfloat16), "mp", scatter_dimension=1, tiled=True
        ).astype(jnp.float32),
    )
    zero_rows = jnp.zeros((tail_rows, out_cols.shape[1]), jnp.float32)
    output = jnp.concatenate([zero_rows, out_cols[:keep_rows]], 0)
    grad_hidden = jnp.concatenate([zero_rows, hid_cols[:keep_rows]], 0)
    neigh_term = contract(d_keys, wk_full) + contract(d_values, wv_full)
    neigh_cols = lax.psum_scatter(
        neigh_term.astype(jnp.bfloat16), "mp", scatter_dimension=1, tiled=True
    ).astype(jnp.float32)
    grad_neighbours = neigh_cols.reshape(blocks_here, 1, RET, neigh_cols.shape[1])
    return (output, grad_hidden, grad_neighbours)


def solution(mesh):
    return jax.shard_map(
        per_device,
        mesh=mesh,
        in_specs=(
            P("dp", "mp"),
            P("dp", "group", None),
            P("dp"),
            P(("dp", "group"), "mp"),
            P("group", "mp"),
            P("group", "mp"),
            P("group", "mp"),
            P("mp", "group"),
            P("dp", "mp"),
        ),
        out_specs=(P("dp", "mp"), P("dp", "mp"), P("dp", "group", None, "mp")),
        check_vma=False,
    )
```

profile of v0, /device:TPU:192, one launch (start us, length us, event | category | flops | bytes accessed | tf_op | source)
XLA Modules:
  0.0 1069.4 jit_solution(10892111256990667614)
XLA Ops:
  8.0 37.5 %all-gather = s32[16,1,256]{2,1,0:T(1,128)S(1)} all-gather(s32[1,1,256]{2,1,0:T(1,128)} %bitcast.59), channel_id=1, replica_groups=mesh['dp'=8,'mp'=16,'group'=2] {'dp','group'}, dimensions={0}, use_global_device_ids=true | all-gather | bytes 17408 | tf_op jit(solution)/shard_map/all_gather | solution.py:37
  45.7 20.2 %gather_fusion = bf16[4096,512]{1,0:T(8,128)(2,1)} fusion(bf16[4096,512]{1,0:T(8,128)(2,1)} %param.12, s32[4096]{0:T(1024)S(1)} %fusion.28), kind=kCustom, calls=%fused_computation | custom fusion | bytes 8404992 | tf_op jit(solution)/shard_map/gather | solution.py:41
  65.9 3.9 broadcast_select_fusion
  69.9 0.8 copy-done.1
  72.9 0.7 all-gather.19.cloned.1.call-update
  73.6 0.7 all-gather.11.cloned.1.call-update
  74.4 479.4 %reduce-scatter.5.cloned.1.call-done = bf16[256,512]{1,0:T(8,128)(2,1)} async-done(((bf16[4096,512]{1,0:T(8,128)(2,1)}), bf16[256,512]{1,0:T(8,128)(2,1)}) %reduce-scatter.5.cloned.1.call-update) | async-done | bytes 262160 | tf_op jit(solution)/shard_map/reduce_scatter | solution.py:44
  554.5 3.5 convolution_convert_fusion.6
  558.1 4.4 convolution_convert_fusion.5
  562.5 58.7 %all-gather.9.cloned.1.call-done = bf16[256,8192]{1,0:T(8,128)(2,1)} async-done(((bf16[256,512]{1,0:T(8,128)(2,1)}), bf16[256,8192]{1,0:T(8,128)(2,1)}) %all-gather.9.cloned.1.call-update) | async-done | bytes 4194320 | tf_op jit(solution)/shard_map/all_gather | solution.py:48
  621.2 4.7 convolution_convert_fusion.4
  626.0 103.6 %all-gather.17.cloned.1.call-done = bf16[8192,256]{1,0:T(8,128)(2,1)} async-done(((bf16[4096,256]{1,0:T(8,128)(2,1)}), bf16[8192,256]{1,0:T(8,128)(2,1)}) %all-gather.17.cloned.1.call-update) | async-done | bytes 4194320 | tf_op jit(solution)/shard_map/all_gather | solution.py:51
  729.5 4.7 convolution_convert_fusion.3
  734.6 0.8 convolution_bitcast_fusion.1
  735.5 8.9 psum.22
  744.4 26.5 %all-reduce.7.cloned.1.call-done = f32[2,64,2,128]{3,1,2,0:T(8,128)} async-done(((f32[2,64,2,128]{3,1,2,0:T(8,128)}), f32[2,64,2,128]{3,1,2,0:T(8,128)}) %all-reduce.7.cloned.1.call-update) | async-done | bytes 131088 | tf_op jit(solution)/shard_map/psum | solution.py:75
  770.9 1.1 multiply_reduce_fusion
  772.2 0.8 convolution_bitcast_fusion
  773.1 4.2 convolution_convert_fusion.1
  777.5 31.1 %all-reduce.9.cloned.1.call-done = f32[2,64,2,128]{3,1,2,0:T(8,128)} async-done(((f32[2,64,2,128]{3,1,2,0:T(8,128)}), f32[2,64,2,128]{3,1,2,0:T(8,128)}) %all-reduce.9.cloned.1.call-update) | async-done | bytes 131088 | tf_op jit(solution)/shard_map/psum | solution.py:89
  808.6 0.9 multiply_convert_fusion
  809.6 5.0 convolution_convert_fusion
  815.7 3.6 fusion.10
  819.3 3.3 fusion
  822.6 69.0 %reduce-scatter.7.cloned.1.call-done = bf16[128,512]{1,0:T(8,128)(2,1)} async-done(((bf16[128,8192]{1,0:T(8,128)(2,1)}), bf16[128,512]{1,0:T(8,128)(2,1)}) %reduce-scatter.7.cloned.1.call-update) | async-done | bytes 131088 | tf_op jit(solution)/shard_map/reduce_scatter | solution.py:102
  891.7 0.9 slice.20
  892.6 0.7 pad_convert_fusion.1
  893.3 81.0 %reduce-scatter.9.cloned.1.call-done = bf16[128,512]{1,0:T(8,128)(2,1)} async-done(((bf16[128,8192]{1,0:T(8,128)(2,1)}), bf16[128,512]{1,0:T(8,128)(2,1)}) %reduce-scatter.9.cloned.1.call-update) | async-done | bytes 131088 | tf_op jit(solution)/shard_map/reduce_scatter | solution.py:105
  974.3 0.9 slice.21
  975.2 0.7 pad_convert_fusion
  975.9 84.2 %reduce-scatter.11.cloned.1.call-done = bf16[256,512]{1,0:T(8,128)(2,1)} async-done(((bf16[256,8192]{1,0:T(8,128)(2,1)}), bf16[256,512]{1,0:T(8,128)(2,1)}) %reduce-scatter.11.cloned.1.call-update) | async-done | bytes 262160 | tf_op jit(solution)/shard_map/reduce_scatter | solution.py:113
  1060.1 1.8 convert.8
  (58 shorter events, 5.1 us)
Async XLA Ops:
  8.0 545.7 %reduce-scatter.5.cloned.1.call-start = ((), (), s32[]{:S(2)}) async-start(), calls=%async_computation.4 | async-start | bytes 4456448 | tf_op jit(solution)/shard_map/reduce_scatter | solution.py:44
  69.8 0.9 copy-start.1
  69.8 2.3 copy-start.2
  69.8 484.6 %all-gather.13.cloned.1.call-start = ((), (), s32[]{:S(2)}) async-start(), calls=%async_computation.7 | async-start | bytes 2228224 | tf_op jit(solution)/shard_map/all_gather | solution.py:32
  71.4 482.9 %copy-start.3 = (s32[2]{0:T(128)S(1)}, s32[2]{0:T(128)}, u32[]{:S(2)}) copy-start(s32[2]{0:T(128)} %param.11) | copy-start | bytes 28
  71.4 483.0 %all-gather.15.cloned.1.call-start = ((), (), s32[]{:S(2)}) async-start(), calls=%async_computation.8 | async-start | bytes 6291456 | tf_op jit(solution)/shard_map/all_gather | solution.py:50
  72.0 486.0 %all-gather.21.cloned.1.call-start = ((), (), s32[]{:S(2)}) async-start(), calls=%async_computation.13 | async-start | bytes 2228224 | tf_op jit(solution)/shard_map/all_gather | solution.py:33
  72.8 485.3 %all-gather.19.cloned.1.call-start = ((), (), s32[]{:S(2)}) async-start(), calls=%async_computation.11 | async-start | bytes 6291456 | tf_op jit(solution)/shard_map/all_gather | solution.py:56
  73.6 489.0 %all-gather.11.cloned.1.call-start = ((), (), s32[]{:S(2)}) async-start(), calls=%async_computation.6 | async-start | bytes 6291456 | tf_op jit(solution)/shard_map/all_gather | solution.py:52
  74.3 546.9 %all-gather.9.cloned.1.call-start = ((), (), s32[]{:S(2)}) async-start(), calls=%async_computation.5 | async-start | bytes 4456448 | tf_op jit(solution)/shard_map/all_gather | solution.py:48
  553.7 175.8 %all-gather.17.cloned.1.call-start = ((), (), s32[]{:S(2)}) async-start(), calls=%async_computation.9 | async-start | bytes 6291456 | tf_op jit(solution)/shard_map/all_gather | solution.py:51
  554.3 216.5 %all-reduce.7.cloned.1.call-start = ((), (), s32[]{:S(2)}) async-start(), calls=%async_computation.10 | async-start | bytes 262144 | tf_op jit(solution)/shard_map/psum | solution.py:75
  735.4 73.2 %all-reduce.9.cloned.1.call-start = ((), (), s32[]{:S(2)}) async-start(), calls=%async_computation.14 | async-start | bytes 262144 | tf_op jit(solution)/shard_map/psum | solution.py:89
  773.1 118.6 %reduce-scatter.7.cloned.1.call-start = ((), (), s32[]{:S(2)}) async-start(), calls=%async_computation.12 | async-start | bytes 2228224 | tf_op jit(solution)/shard_map/reduce_scatter | solution.py:102
  777.4 196.9 %reduce-scatter.9.cloned.1.call-start = ((), (), s32[]{:S(2)}) async-start(), calls=%async_computation.15 | async-start | bytes 2228224 | tf_op jit(solution)/shard_map/reduce_scatter | solution.py:105
  814.7 245.5 %reduce-scatter.11.cloned.1.call-start = ((), (), s32[]{:S(2)}) async-start(), calls=%async_computation.16 | async-start | bytes 4456448 | tf_op jit(solution)/shard_map/reduce_scatter | solution.py:113
  815.7 3.6 copy-start
Sparse Core Ops, SparseCore 0:
  70.0 483.7 reduce-scatter.4
Sparse Core Ops, SparseCore 1:
  73.3 53.8 all-gather.12
  128.8 115.2 all-gather.14
  246.9 53.6 all-gather.20
  302.4 78.6 all-gather.18
  382.9 155.3 all-gather.10
  553.8 67.3 all-gather.8
  622.9 106.6 all-gather.16
  735.5 35.3 all-reduce.6
  773.9 34.7 all-reduce.8
  812.2 79.4 reduce-scatter.6
  895.5 78.7 reduce-scatter.8
  978.0 82.1 reduce-scatter.10
where the time goes:
time: 1070 us
  waiting for transfers between devices  936 us (87%)
  blocking collectives  46.4 us (4%)
  matrix products  36.1 us (3%)
  local copies, waits for them, and re-layouts  24.7 us (2%)
  between operations  15.9 us (1%)
    reduce_scatter x1, waiting for transfers between devices, per_device(): lax.psum_scatter(picked, ('dp', 'group'), scatter_dimension=0, tiled=True)  479 us
    all_gather x1, waiting for transfers between devices, per_device(): lax.all_gather(w_key, 'group', axis=0, tiled=True)  104 us
    reduce_scatter x1, waiting for transfers between devices, per_device(): lax.psum_scatter(neigh_term.astype(jnp.bfloat16), 'mp', scatter_dimension...  84.2 us
    reduce_scatter x1, waiting for transfers between devices, per_device(): lax.psum_scatter(hid_term.astype(jnp.bfloat16), 'mp', scatter_dimension=1...  81 us
    reduce_scatter x1, waiting for transfers between devices, per_device(): lax.psum_scatter(out_term.astype(jnp.bfloat16), 'mp', scatter_dimension=1...  69 us
    all_gather x1, waiting for transfers between devices, per_device(): neighbours = lax.all_gather(own_cols, 'mp', axis=1, tiled=True)  58.7 us
    all_gather x1, blocking collectives, per_device(): every_id = lax.all_gather(flat_ids, ('dp', 'group'), axis=0, tiled=True)  37.5 us
    psum x1, waiting for transfers between devices, per_device(): query_grad = lax.psum(query_part, 'group')  31.1 us
  transfers between devices with their start and end apart: 13, of which 8 were waited for; matrix products, arithmetic and copies ran while one was open for 3% of the time, Pallas kernels for 0%

commit v1 on v0

--- a/solution.py
+++ b/solution.py
@@ -34,17 +34,25 @@
     )
     flat_ids = neighbour_ids.reshape(-1)
     block_rows = embed_table.shape[0]
-    every_id = lax.all_gather(flat_ids, ("dp", "group"), axis=0, tiled=True)
+    owners = lax.axis_size("dp") * lax.axis_size("group")
+    cap = flat_ids.shape[0] // 4
+    every_id = lax.all_gather(
+        flat_ids.astype(jnp.float32), ("dp", "group"), axis=0, tiled=True
+    ).astype(jnp.int32).reshape(owners, -1)
     owner = lax.axis_index("dp") * lax.axis_size("group") + lax.axis_index("group")
     local_ids = every_id - owner * block_rows
     inside = (local_ids >= 0) & (local_ids < block_rows)
-    picked = embed_table[jnp.clip(local_ids, 0, block_rows - 1)]
-    picked = jnp.where(inside[:, None], picked, jnp.zeros_like(picked))
-    own_cols = (
-        lax.psum_scatter(picked, ("dp", "group"), scatter_dimension=0, tiled=True)
-        .astype(jnp.float32)
-        .astype(jnp.bfloat16)
-    )
+    rank = jnp.cumsum(inside.astype(jnp.int32), axis=1) - 1
+    slot_hit = inside[:, :, None] & (rank[:, :, None] == jnp.arange(cap)[None, None, :])
+    send_rows = jnp.sum(jnp.where(slot_hit, local_ids[:, :, None], 0), axis=1)
+    send_buf = embed_table[send_rows.reshape(-1)].reshape(owners, cap, -1)
+    recv_buf = lax.all_to_all(send_buf, ("dp", "group"), 0, 0, tiled=True)
+    own_owner = flat_ids // block_rows
+    same_owner = own_owner[:, None] == jnp.arange(owners)[None, :]
+    own_rank = jnp.sum(
+        jnp.where(same_owner, jnp.cumsum(same_owner.astype(jnp.int32), axis=0), 0), axis=1
+    ) - 1
+    own_cols = recv_buf.reshape(owners * cap, -1)[own_owner * cap + own_rank]
     neighbours = lax.all_gather(own_cols, "mp", axis=1, tiled=True)
     wq_full, wk_full, wv_full = (
         lax.all_gather(w_query, "group", axis=0, tiled=True),

time: 1070 us -> 973 us (0.909)
  waiting for transfers between devices: 936 us -> 843 us
    reduce_scatter x1 -> x0, waiting for transfers between devices: 479 us -> none  [per_device(): lax.psum_scatter(picked, ('dp', 'group'), scatter_dimension=0, tiled=True)]
    all_gather x1, waiting for transfers between devices: 0.02 us -> 108 us  [per_device(): wo_full = lax.all_gather(w_out, 'group', axis=1, tiled=True)]
    all_gather x1, waiting for transfers between devices: 0.03 us -> 105 us  [per_device(): lax.all_gather(w_value, 'group', axis=0, tiled=True)]
    all_gather x1, waiting for transfers between devices: 0.02 us -> 82.6 us  [per_device(): lax.all_gather(w_query, 'group', axis=0, tiled=True)]
    all_gather x1, waiting for transfers between devices: 0.03 us -> 52 us  [per_device(): lax.all_gather(grad_rows, 'mp', axis=1, tiled=True)]
    all_to_all x0 -> x1, waiting for transfers between devices: none -> 29.8 us  [per_device(): recv_buf = lax.all_to_all(send_buf, ('dp', 'group'), 0, 0, tiled=True)]
  transfers between devices with their start and end apart: 13 -> 13, of which waited for: 8 -> 12; matrix products, arithmetic and copies ran while one was open for 3% -> 5% of each run, Pallas kernels for 0% -> 0%
where the time goes in v1:
time: 973 us; the launch traced here: 971 us
  waiting for transfers between devices  843 us (87%)
  blocking collectives  46.2 us (5%)
  matrix products  36.1 us (4%)
  local copies, waits for them, and re-layouts  15.6 us (2%)
  between operations  14.5 us (1%)
    all_gather x1, waiting for transfers between devices, per_device(): wo_full = lax.all_gather(w_out, 'group', axis=1, tiled=True)  108 us
    all_gather x1, waiting for transfers between devices, per_device(): lax.all_gather(w_value, 'group', axis=0, tiled=True)  105 us
    all_gather x1, waiting for transfers between devices, per_device(): lax.all_gather(w_key, 'group', axis=0, tiled=True)  104 us
    reduce_scatter x1, waiting for transfers between devices, per_device(): lax.psum_scatter(neigh_term.astype(jnp.bfloat16), 'mp', scatter_dimension...  84 us
    all_gather x1, waiting for transfers between devices, per_device(): lax.all_gather(w_query, 'group', axis=0, tiled=True)  82.6 us
    reduce_scatter x1, waiting for transfers between devices, per_device(): lax.psum_scatter(hid_term.astype(jnp.bfloat16), 'mp', scatter_dimension=1...  81.1 us
    reduce_scatter x1, waiting for transfers between devices, per_device(): lax.psum_scatter(out_term.astype(jnp.bfloat16), 'mp', scatter_dimension=1...  69 us
    all_gather x1, waiting for transfers between devices, per_device(): neighbours = lax.all_gather(own_cols, 'mp', axis=1, tiled=True)  66.2 us
  transfers between devices with their start and end apart: 13, of which 12 were waited for; matrix products, arithmetic and copies ran while one was open for 5% of the time, Pallas kernels for 0%

profile of v1, /device:TPU:192, one launch (start us, length us, event | category | flops | bytes accessed | tf_op | source)
XLA Modules:
  0.0 970.9 jit_solution(12286093274936307989)
XLA Ops:
  7.2 0.9 slice.30
  9.6 0.9 slice.32
  12.4 37.3 %all-gather.1 = f32[16,1,256]{2,1,0:T(1,128)S(1)} all-gather(f32[1,1,256]{2,1,0:T(1,128)S(1)} %bitcast.107), channel_id=1, replica_groups=mesh['dp'=8,'mp'=16,'group'=2] {'dp','group'}, dimensions={0}, use_global_device_ids=true | all-gather | bytes 17408 | tf_op jit(solution)/shard_map/all_gather | solution.py:39
  51.2 7.8 gather_fusion
  59.1 7.4 all-to-all-start
  67.5 29.8 %all-to-all-done = bf16[16,64,512]{2,1,0:T(8,128)(2,1)S(1)} async-done(((bf16[16,64,512]{2,1,0:T(8,128)(2,1)}), bf16[16,64,512]{2,1,0:T(8,128)(2,1)S(1)}, u32[]{:S(2)}, u32[]{:S(2)}) %all-to-all-start) | async-done | bytes 1048608 | tf_op jit(solution)/shard_map/all_to_all | solution.py:49
  97.3 1.9 gather_fusion.1
  100.0 82.6 %all-gather.14.cloned.1.call-done = bf16[8192,256]{1,0:T(8,128)(2,1)} async-done(((bf16[4096,256]{1,0:T(8,128)(2,1)}), bf16[8192,256]{1,0:T(8,128)(2,1)}) %all-gather.14.cloned.1.call-update) | async-done | bytes 4194320 | tf_op jit(solution)/shard_map/all_gather | solution.py:58
  182.6 3.5 convolution_convert_fusion.6
  186.2 52.0 %all-gather.20.cloned.1.call-done = bf16[128,8192]{1,0:T(8,128)(2,1)} async-done(((bf16[128,512]{1,0:T(8,128)(2,1)}), bf16[128,8192]{1,0:T(8,128)(2,1)}) %all-gather.20.cloned.1.call-update) | async-done | bytes 2097168 | tf_op jit(solution)/shard_map/all_gather | solution.py:33
  238.2 108.5 %all-gather.18.cloned.1.call-done = bf16[256,8192]{1,0:T(8,128)(2,1)} async-done(((bf16[256,4096]{1,0:T(8,128)(2,1)}), bf16[256,8192]{1,0:T(8,128)(2,1)}) %all-gather.18.cloned.1.call-update) | async-done | bytes 4194320 | tf_op jit(solution)/shard_map/all_gather | solution.py:64
  346.6 4.4 convolution_convert_fusion.5
  351.0 105.4 %all-gather.10.cloned.1.call-done = bf16[8192,256]{1,0:T(8,128)(2,1)} async-done(((bf16[4096,256]{1,0:T(8,128)(2,1)}), bf16[8192,256]{1,0:T(8,128)(2,1)}) %all-gather.10.cloned.1.call-update) | async-done | bytes 4194320 | tf_op jit(solution)/shard_map/all_gather | solution.py:60
  456.4 66.2 %all-gather.22.cloned.1.call-done = bf16[256,8192]{1,0:T(8,128)(2,1)} async-done(((bf16[256,512]{1,0:T(8,128)(2,1)}), bf16[256,8192]{1,0:T(8,128)(2,1)}) %all-gather.22.cloned.1.call-update) | async-done | bytes 4194320 | tf_op jit(solution)/shard_map/all_gather | solution.py:56
  522.6 4.7 convolution_convert_fusion.4
  527.4 103.9 %all-gather.16.cloned.1.call-done = bf16[8192,256]{1,0:T(8,128)(2,1)} async-done(((bf16[4096,256]{1,0:T(8,128)(2,1)}), bf16[8192,256]{1,0:T(8,128)(2,1)}) %all-gather.16.cloned.1.call-update) | async-done | bytes 4194320 | tf_op jit(solution)/shard_map/all_gather | solution.py:59
  631.3 4.7 convolution_convert_fusion.3
  637.2 8.9 psum.22
  646.1 26.7 %all-reduce.7.cloned.1.call-done = f32[2,64,2,128]{3,1,2,0:T(8,128)} async-done(((f32[2,64,2,128]{3,1,2,0:T(8,128)}), f32[2,64,2,128]{3,1,2,0:T(8,128)}) %all-reduce.7.cloned.1.call-update) | async-done | bytes 131088 | tf_op jit(solution)/shard_map/psum | solution.py:83
  672.8 1.1 multiply_reduce_fusion
  675.1 4.3 convolution_convert_fusion.1
  679.4 31.5 %all-reduce.9.cloned.1.call-done = f32[2,64,2,128]{3,1,2,0:T(8,128)} async-done(((f32[2,64,2,128]{3,1,2,0:T(8,128)}), f32[2,64,2,128]{3,1,2,0:T(8,128)}) %all-reduce.9.cloned.1.call-update) | async-done | bytes 131088 | tf_op jit(solution)/shard_map/psum | solution.py:97
  711.0 0.9 multiply_convert_fusion
  712.0 5.0 convolution_convert_fusion
  718.1 3.6 fusion.11
  721.7 3.2 fusion
  725.0 69.0 %reduce-scatter.4.cloned.1.call-done = bf16[128,512]{1,0:T(8,128)(2,1)} async-done(((bf16[128,8192]{1,0:T(8,128)(2,1)}), bf16[128,512]{1,0:T(8,128)(2,1)}) %reduce-scatter.4.cloned.1.call-update) | async-done | bytes 131088 | tf_op jit(solution)/shard_map/reduce_scatter | solution.py:110
  793.9 0.9 slice.40
  795.6 81.1 %reduce-scatter.6.cloned.1.call-done = bf16[128,512]{1,0:T(8,128)(2,1)} async-done(((bf16[128,8192]{1,0:T(8,128)(2,1)}), bf16[128,512]{1,0:T(8,128)(2,1)}) %reduce-scatter.6.cloned.1.call-update) | async-done | bytes 131088 | tf_op jit(solution)/shard_map/reduce_scatter | solution.py:113
  876.7 0.9 slice.41
  878.3 84.0 %reduce-scatter.8.cloned.1.call-done = bf16[256,512]{1,0:T(8,128)(2,1)} async-done(((bf16[256,8192]{1,0:T(8,128)(2,1)}), bf16[256,512]{1,0:T(8,128)(2,1)}) %reduce-scatter.8.cloned.1.call-update) | async-done | bytes 262160 | tf_op jit(solution)/shard_map/reduce_scatter | solution.py:121
  962.3 1.8 convert.9
  (78 shorter events, 11.6 us)
Async XLA Ops:
  7.2 5.2 copy-start.1
  7.2 92.8 %all-gather.12.cloned.1.call-start = ((), (), s32[]{:S(2)}) async-start(), calls=%async_computation.5 | async-start | bytes 2228224 | tf_op jit(solution)/shard_map/all_gather | solution.py:32
  8.8 173.8 %all-gather.14.cloned.1.call-start = ((), (), s32[]{:S(2)}) async-start(), calls=%async_computation.6 | async-start | bytes 6291456 | tf_op jit(solution)/shard_map/all_gather | solution.py:58
  9.6 228.6 %all-gather.20.cloned.1.call-start = ((), (), s32[]{:S(2)}) async-start(), calls=%async_computation.11 | async-start | bytes 2228224 | tf_op jit(solution)/shard_map/all_gather | solution.py:33
  11.2 335.4 %all-gather.18.cloned.1.call-start = ((), (), s32[]{:S(2)}) async-start(), calls=%async_computation.9 | async-start | bytes 6291456 | tf_op jit(solution)/shard_map/all_gather | solution.py:64
  11.8 444.6 %all-gather.10.cloned.1.call-start = ((), (), s32[]{:S(2)}) async-start(), calls=%async_computation.4 | async-start | bytes 6291456 | tf_op jit(solution)/shard_map/all_gather | solution.py:60
  59.1 40.9 %copy-start.2 = (s32[2]{0:T(128)S(1)}, s32[2]{0:T(128)}, u32[]{:S(2)}) copy-start(s32[2]{0:T(128)} %param.11) | copy-start | bytes 28
  59.1 38.2 %all-to-all-start = ((bf16[16,64,512]{2,1,0:T(8,128)(2,1)}), bf16[16,64,512]{2,1,0:T(8,128)(2,1)S(1)}, u32[]{:S(2)}, u32[]{:S(2)}) async-start(bf16[16,64,512]{2,1,0:T(8,128)(2,1)} %bitcast.4), calls=%async_computation | async-start | bytes 2097152 | tf_op jit(solution)/shard_map/all_to_all | solution.py:49
  66.5 456.2 %all-gather.22.cloned.1.call-start = ((), (), s32[]{:S(2)}) async-start(), calls=%async_computation.15 | async-start | bytes 4456448 | tf_op jit(solution)/shard_map/all_gather | solution.py:56
  99.2 532.1 %all-gather.16.cloned.1.call-start = ((), (), s32[]{:S(2)}) async-start(), calls=%async_computation.7 | async-start | bytes 6291456 | tf_op jit(solution)/shard_map/all_gather | solution.py:59
  99.9 572.9 %all-reduce.7.cloned.1.call-start = ((), (), s32[]{:S(2)}) async-start(), calls=%async_computation.8 | async-start | bytes 262144 | tf_op jit(solution)/shard_map/psum | solution.py:83
  637.2 73.8 %all-reduce.9.cloned.1.call-start = ((), (), s32[]{:S(2)}) async-start(), calls=%async_computation.12 | async-start | bytes 262144 | tf_op jit(solution)/shard_map/psum | solution.py:97
  675.1 118.9 %reduce-scatter.4.cloned.1.call-start = ((), (), s32[]{:S(2)}) async-start(), calls=%async_computation.10 | async-start | bytes 2228224 | tf_op jit(solution)/shard_map/reduce_scatter | solution.py:110
  679.4 197.3 %reduce-scatter.6.cloned.1.call-start = ((), (), s32[]{:S(2)}) async-start(), calls=%async_computation.13 | async-start | bytes 2228224 | tf_op jit(solution)/shard_map/reduce_scatter | solution.py:113
  717.0 245.2 %reduce-scatter.8.cloned.1.call-start = ((), (), s32[]{:S(2)}) async-start(), calls=%async_computation.14 | async-start | bytes 4456448 | tf_op jit(solution)/shard_map/reduce_scatter | solution.py:121
  718.1 3.6 copy-start
Sparse Core Ops, SparseCore 0:
  11.0 53.4 all-gather.11
  66.3 116.3 all-gather.13
  185.6 52.4 all-gather.19
  239.8 106.7 all-gather.17
  348.3 108.0 all-gather.9
  459.3 63.3 all-gather.21
  524.4 106.7 all-gather.15
  637.3 35.4 all-reduce.6
  676.0 34.9 all-reduce.8
  714.4 79.5 reduce-scatter.3
  797.9 78.6 reduce-scatter.5
  880.1 82.0 reduce-scatter.7

commit v2 on v1

--- a/solution.py
+++ b/solution.py
@@ -25,6 +25,10 @@
     heads_here = w_query.shape[1] // HD
     inv_root = 1.0 / math.sqrt(HD)
     keep_rows = rows_here - tail_rows
+    half = w_query.shape[0]
+    me_group = lax.axis_index("group")
+    me_dp = lax.axis_index("dp")
+    swap = [(0, 1), (1, 0)]
     pad_rows = jnp.zeros((tail_rows, hidden.shape[1]), jnp.bfloat16)
     query_rows = jnp.concatenate([hidden[tail_rows:], pad_rows], 0)
     grad_rows = jnp.concatenate([grad_out[tail_rows:], pad_rows], 0)
@@ -32,14 +36,22 @@
         lax.all_gather(query_rows, "mp", axis=1, tiled=True),
         lax.all_gather(grad_rows, "mp", axis=1, tiled=True),
     )
+    piece_rows = half // lax.axis_size("dp")
+    kv_local = jnp.concatenate([w_key, w_value], axis=1)
+    kv_piece = lax.dynamic_slice_in_dim(kv_local, me_dp * piece_rows, piece_rows, 0)
+    kv_other = lax.all_gather(
+        lax.ppermute(kv_piece, "group", swap), "dp", axis=0, tiled=True
+    )
+    cols_kv = w_key.shape[1]
+    wk_other, wv_other = kv_other[:, :cols_kv], kv_other[:, cols_kv:]
+
     flat_ids = neighbour_ids.reshape(-1)
     block_rows = embed_table.shape[0]
     owners = lax.axis_size("dp") * lax.axis_size("group")
     cap = flat_ids.shape[0] // 4
-    every_id = lax.all_gather(
-        flat_ids.astype(jnp.float32), ("dp", "group"), axis=0, tiled=True
-    ).astype(jnp.int32).reshape(owners, -1)
-    owner = lax.axis_index("dp") * lax.axis_size("group") + lax.axis_index("group")
+    ids_f = lax.all_gather(flat_ids.astype(jnp.float32), "group", axis=0)
+    every_id = lax.all_gather(ids_f, "dp", axis=0).astype(jnp.int32).reshape(owners, -1)
+    owner = me_dp * lax.axis_size("group") + me_group
     local_ids = every_id - owner * block_rows
     inside = (local_ids >= 0) & (local_ids < block_rows)
     rank = jnp.cumsum(inside.astype(jnp.int32), axis=1) - 1
@@ -54,20 +66,28 @@
     ) - 1
     own_cols = recv_buf.reshape(owners * cap, -1)[own_owner * cap + own_rank]
     neighbours = lax.all_gather(own_cols, "mp", axis=1, tiled=True)
-    wq_full, wk_full, wv_full = (
-        lax.all_gather(w_query, "group", axis=0, tiled=True),
-        lax.all_gather(w_key, "group", axis=0, tiled=True),
-        lax.all_gather(w_value, "group", axis=0, tiled=True),
-    )
-    query_sum = jnp.dot(full_query, wq_full, preferred_element_type=jnp.float32)
-    query = query_sum.astype(jnp.bfloat16)
-    wo_full = lax.all_gather(w_out, "group", axis=1, tiled=True)
-    keys = jnp.dot(neighbours, wk_full, preferred_element_type=jnp.float32).astype(jnp.bfloat16)
-    values = jnp.dot(neighbours, wv_full, preferred_element_type=jnp.float32).astype(jnp.bfloat16)
+
+    def this_half(x):
+        return lax.dynamic_slice_in_dim(x, me_group * half, half, 1)
+
+    def other_half(x):
+        return lax.dynamic_slice_in_dim(x, (1 - me_group) * half, half, 1)
+
+    query_part = jnp.dot(this_half(full_query), w_query, preferred_element_type=jnp.float32)
+    query = lax.psum(query_part, "group").astype(jnp.bfloat16)
+    n_here, n_there = this_half(neighbours), other_half(neighbours)
+    keys = (
+        jnp.dot(n_here, w_key, preferred_element_type=jnp.float32)
+        + jnp.dot(n_there, wk_other, preferred_element_type=jnp.float32)
+    ).astype(jnp.bfloat16)
+    values = (
+        jnp.dot(n_here, w_value, preferred_element_type=jnp.float32)
+        + jnp.dot(n_there, wv_other, preferred_element_type=jnp.float32)
+    ).astype(jnp.bfloat16)
     key_block = keys.reshape(blocks_here, RET, heads_here, HD)
     value_block = values.reshape(blocks_here, RET, heads_here, HD)
     query_block = query.reshape(blocks_here, BLOCK, heads_here, HD)
-    live = (counts > lax.axis_index("group")).astype(jnp.float32)
+    live = (counts > me_group).astype(jnp.float32)
     scores = (
         jnp.einsum("cqhd,ckhd->chqk", query_block, key_block, preferred_element_type=jnp.float32)
         * inv_root
@@ -84,8 +104,16 @@
     total = partial_total + 1.0
     attn = numer / jnp.transpose(total, (0, 2, 1))[..., None]
     attn_bf = attn.reshape(rows_here, heads_here * HD).astype(jnp.bfloat16)
-    out_term = jnp.dot(attn_bf, wo_full, preferred_element_type=jnp.float32)
-    d_attn = contract(full_grad, wo_full).astype(jnp.bfloat16)
+
+    def place_half(x):
+        zeros = jnp.zeros_like(x)
+        return jnp.where(
+            me_group == 0, jnp.concatenate([x, zeros], 1), jnp.concatenate([zeros, x], 1)
+        )
+
+    out_term = jnp.dot(attn_bf, w_out, preferred_element_type=jnp.float32)
+    d_attn_part = contract(this_half(full_grad), w_out)
+    d_attn = lax.psum(d_attn_part, "group").astype(jnp.bfloat16)
     d_block = d_attn.reshape(blocks_here, BLOCK, heads_here, HD)
     prob = weights / total[..., None]
     d_prob = jnp.einsum("cqhd,ckhd->chqk", d_block, value_block, preferred_element_type=jnp.float32)
@@ -105,19 +133,26 @@
     ).astype(jnp.bfloat16)
     d_keys = d_keys.reshape(blocks_here * RET, heads_here * HD)
     d_values = d_values.reshape(blocks_here * RET, heads_here * HD)
-    hid_term = contract(d_query, wq_full)
+    hid_term = contract(d_query, w_query)
     out_cols, hid_cols = (
         lax.psum_scatter(
-            out_term.astype(jnp.bfloat16), "mp", scatter_dimension=1, tiled=True
+            place_half(out_term.astype(jnp.bfloat16)), "mp", scatter_dimension=1, tiled=True
         ).astype(jnp.float32),
         lax.psum_scatter(
-            hid_term.astype(jnp.bfloat16), "mp", scatter_dimension=1, tiled=True
+            place_half(hid_term.astype(jnp.bfloat16)), "mp", scatter_dimension=1, tiled=True
         ).astype(jnp.float32),
     )
+    out_cols, hid_cols = lax.psum((out_cols, hid_cols), "group")
     zero_rows = jnp.zeros((tail_rows, out_cols.shape[1]), jnp.float32)
     output = jnp.concatenate([zero_rows, out_cols[:keep_rows]], 0)
     grad_hidden = jnp.concatenate([zero_rows, hid_cols[:keep_rows]], 0)
-    neigh_term = contract(d_keys, wk_full) + contract(d_values, wv_full)
+    term_here = contract(d_keys, w_key) + contract(d_values, w_value)
+    term_there = contract(d_keys, wk_other) + contract(d_values, wv_other)
+    neigh_term = jnp.where(
+        me_group == 0,
+        jnp.concatenate([term_here, term_there], 1),
+        jnp.concatenate([term_there, term_here], 1),
+    )
     neigh_cols = lax.psum_scatter(
         neigh_term.astype(jnp.bfloat16), "mp", scatter_dimension=1, tiled=True
     ).astype(jnp.float32)

time: 973 us -> 586 us (0.60)
  waiting for transfers between devices: 843 us -> 407 us
  blocking collectives: 46.2 us -> 87.3 us
    all_gather x4 -> x1, waiting for transfers between devices: 400 us -> 50.5 us  [per_device(): lax.all_gather(lax.ppermute(kv_piece, 'group', swap), 'dp', axis=0, tiled...]
    psum x0 -> x2, blocking collectives: none -> 49.7 us  [the longest x1 32.2 us: per_device(): out_cols, hid_cols = lax.psum((out_cols, hid_cols), 'group')]
    all_gather x1, waiting for transfers between devices: 52 us -> 5.62 us  [per_device(): lax.all_gather(grad_rows, 'mp', axis=1, tiled=True)]
    reduce_scatter x1, waiting for transfers between devices: 84 us -> 52 us  [per_device(): lax.psum_scatter(neigh_term.astype(jnp.bfloat16), 'mp', scatter_dimension...]
    all_gather x1 -> x2, blocking collectives: 37.3 us -> 20.3 us  [the longest x1 12.1 us: per_device(): lax.all_gather(ids_f, 'dp', axis=0).astype(jnp.int32).reshape(owners, -1)]
    ppermute x0 -> x1, waiting for transfers between devices: none -> 14 us  [per_device(): lax.ppermute(kv_piece, 'group', swap)]
  transfers between devices with their start and end apart: 13 -> 11, of which waited for: 12 -> 10; matrix products, arithmetic and copies ran while one was open for 5% -> 7% of each run, Pallas kernels for 0% -> 0%
where the time goes in v2:
time: 586 us; the launch traced here: 584 us
  waiting for transfers between devices  407 us (69%)
  blocking collectives  87.3 us (15%)
  matrix products  30.3 us (5%)
  local copies, waits for them, and re-layouts  19.9 us (3%)
  between operations  14.3 us (2%)
  other arithmetic  13.4 us (2%)
  starting transfers between devices  12 us (2%)
    reduce_scatter x1, waiting for transfers between devices, per_device(): lax.psum_scatter(place_half(hid_term.astype(jnp.bfloat16)), 'mp', scatter...  82.7 us
    reduce_scatter x1, waiting for transfers between devices, per_device(): lax.psum_scatter(place_half(out_term.astype(jnp.bfloat16)), 'mp', scatter...  63.3 us
    all_gather x1, waiting for transfers between devices, per_device(): neighbours = lax.all_gather(own_cols, 'mp', axis=1, tiled=True)  63 us
    reduce_scatter x1, waiting for transfers between devices, per_device(): lax.psum_scatter(neigh_term.astype(jnp.bfloat16), 'mp', scatter_dimension...  52 us
    all_gather x1, waiting for transfers between devices, per_device(): lax.all_gather(lax.ppermute(kv_piece, 'group', swap), 'dp', axis=0, tiled...  50.5 us
    psum x1, waiting for transfers between devices, per_device(): query_grad = lax.psum(query_part, 'group')  33.2 us
    psum x1, blocking collectives, per_device(): out_cols, hid_cols = lax.psum((out_cols, hid_cols), 'group')  32.2 us
    all_to_all x1, waiting for transfers between devices, per_device(): recv_buf = lax.all_to_all(send_buf, ('dp', 'group'), 0, 0, tiled=True)  22.2 us
  transfers between devices with their start and end apart: 11, of which 10 were waited for; matrix products, arithmetic and copies ran while one was open for 7% of the time, Pallas kernels for 0%

profile of v2, /device:TPU:192, one launch (start us, length us, event | category | flops | bytes accessed | tf_op | source)
XLA Modules:
  0.0 583.8 jit_solution(987865017134909866)
XLA Ops:
  11.3 8.1 %all-gather.2 = f32[2,1,256]{2,1,0:T(1,128)S(1)} all-gather(f32[1,1,256]{2,1,0:T(1,128)S(1)} %convert_bitcast_fusion.1), channel_id=1, replica_groups=mesh['dp'=8,'mp'=16,'group'=2] {'group'}, dimensions={0}, use_global_device_ids=true | all-gather | bytes 3072 | tf_op jit(solution)/shard_map/all_gather | solution.py:52
  19.4 12.1 %all-gather.3 = f32[8,2,256]{2,1,0:T(2,128)S(1)} all-gather(f32[1,2,256]{2,1,0:T(2,128)S(1)} %copy.55), channel_id=2, replica_groups=mesh['dp'=8,'mp'=16,'group'=2] {'dp'}, dimensions={0}, use_global_device_ids=true | all-gather | bytes 18432 | tf_op jit(solution)/shard_map/all_gather | solution.py:53
  33.0 7.8 %gather_fusion = bf16[1024,512]{1,0:T(8,128)(2,1)} fusion(bf16[4096,512]{1,0:T(8,128)(2,1)} %param.12, s32[1024]{0:T(1024)S(1)} %broadcast_clamp_fusion), kind=kCustom, calls=%fused_computation | custom fusion | bytes 2101248 | tf_op jit(solution)/shard_map/gather | solution.py:60
  40.9 7.0 %all-to-all-start = ((bf16[16,64,512]{2,1,0:T(8,128)(2,1)}), bf16[16,64,512]{2,1,0:T(8,128)(2,1)S(1)}, u32[]{:S(2)}, u32[]{:S(2)}) async-start(bf16[16,64,512]{2,1,0:T(8,128)(2,1)} %bitcast.98), calls=%async_computation | async-start | bytes 2097152 | tf_op jit(solution)/shard_map/all_to_all | solution.py:61
  48.9 22.2 %all-to-all-done = bf16[16,64,512]{2,1,0:T(8,128)(2,1)S(1)} async-done(((bf16[16,64,512]{2,1,0:T(8,128)(2,1)}), bf16[16,64,512]{2,1,0:T(8,128)(2,1)S(1)}, u32[]{:S(2)}, u32[]{:S(2)}) %all-to-all-start) | async-done | bytes 1048608 | tf_op jit(solution)/shard_map/all_to_all | solution.py:61
  71.1 1.9 gather_fusion.1
  74.1 4.5 collective-permute-start
  78.6 14.0 %collective-permute-done = bf16[512,512]{1,0:T(8,128)(2,1)S(1)} collective-permute-done((bf16[512,512]{1,0:T(8,128)(2,1)S(1)}, bf16[512,512]{1,0:T(8,128)(2,1)S(1)}, u32[]{:S(2)}, u32[]{:S(2)}) %collective-permute-start) | collective-permute-done | bytes 524320 | tf_op jit(solution)/shard_map/ppermute | solution.py:43
  93.5 2.4 fusion.43
  95.9 17.5 %all-reduce.19 = bf16[128,256]{1,0:T(8,128)(2,1)S(1)} all-reduce(f32[128,256]{1,0:T(8,128)S(1)} %fusion.43), channel_id=1, replica_groups=mesh['dp'=8,'mp'=16,'group'=2] {'group'}, use_global_device_ids=true, to_apply=%region_6.7 | all-reduce | flops 32768 | bytes 196608 | tf_op jit(solution)/shard_map/psum | solution.py:77
  113.4 5.6 all-gather.13.cloned.1.call-done
  119.0 2.1 fusion.41
  121.1 63.0 %all-gather.15.cloned.1.call-done = bf16[256,8192]{1,0:T(8,128)(2,1)} async-done(((bf16[256,512]{1,0:T(8,128)(2,1)}), bf16[256,8192]{1,0:T(8,128)(2,1)}) %all-gather.15.cloned.1.call-update) | async-done | bytes 4194320 | tf_op jit(solution)/shard_map/all_gather | solution.py:68
  184.1 2.9 fusion.12
  187.0 50.5 %all-gather.9.cloned.1.call-done = bf16[4096,512]{1,0:T(8,128)(2,1)} async-done(((bf16[512,512]{1,0:T(8,128)(2,1)}), bf16[4096,512]{1,0:T(8,128)(2,1)}) %all-gather.9.cloned.1.call-update) | async-done | bytes 4194320 | tf_op jit(solution)/shard_map/all_gather | solution.py:42
  237.5 2.9 fusion.25
  240.5 3.1 fusion.10
  243.9 2.3 fusion.30
  247.5 17.3 %all-reduce.20 = (f32[2,2,64]{2,1,0:T(2,128)S(1)}, bf16[128,256]{1,0:T(8,128)(2,1)S(1)}) all-reduce(f32[2,2,64]{2,1,0:T(2,128)S(1)} %get-tuple-element.25, f32[128,256]{1,0:T(8,128)S(1)} %fusion.41), channel_id=1, replica_groups=mesh['dp'=8,'mp'=16,'group'=2] {'group'}, use_global_device_ids=true, to_apply=%region_9.10 | all-reduce | flops 33024 | bytes 198656 | tf_op jit(solution)/shard_map/psum | solution.py:103
  264.9 20.1 %all-reduce.16.cloned.1.call-done = f32[2,64,2,128]{3,1,2,0:T(8,128)} async-done(((f32[2,64,2,128]{3,1,2,0:T(8,128)}), f32[2,64,2,128]{3,1,2,0:T(8,128)}) %all-reduce.16.cloned.1.call-update) | async-done | bytes 131088 | tf_op jit(solution)/shard_map/psum | solution.py:103
  289.0 1.8 pad_select_fusion.1
  290.8 33.2 %all-reduce.18.cloned.1.call-done = f32[2,64,2,128]{3,1,2,0:T(8,128)} async-done(((f32[2,64,2,128]{3,1,2,0:T(8,128)}), f32[2,64,2,128]{3,1,2,0:T(8,128)}) %all-reduce.18.cloned.1.call-update) | async-done | bytes 131088 | tf_op jit(solution)/shard_map/psum | solution.py:125
  325.0 2.4 convolution_convert_fusion
  327.5 1.7 pad_select_fusion
  329.9 4.3 fusion.1
  334.6 2.5 fusion.50
  341.4 2.5 fusion
  343.9 63.3 %reduce-scatter.4.cloned.1.call-done = bf16[128,512]{1,0:T(8,128)(2,1)} async-done(((bf16[128,8192]{1,0:T(8,128)(2,1)}), bf16[128,512]{1,0:T(8,128)(2,1)}) %reduce-scatter.4.cloned.1.call-update) | async-done | bytes 131088 | tf_op jit(solution)/shard_map/reduce_scatter | solution.py:138
  407.1 82.7 %reduce-scatter.6.cloned.1.call-done = bf16[128,512]{1,0:T(8,128)(2,1)} async-done(((bf16[128,8192]{1,0:T(8,128)(2,1)}), bf16[128,512]{1,0:T(8,128)(2,1)}) %reduce-scatter.6.cloned.1.call-update) | async-done | bytes 131088 | tf_op jit(solution)/shard_map/reduce_scatter | solution.py:141
  489.8 32.2 %all-reduce.21 = (f32[128,512]{1,0:T(8,128)S(1)}, f32[128,512]{1,0:T(8,128)S(1)}) all-reduce(bf16[128,512]{1,0:T(8,128)(2,1)} %reduce-scatter.4.cloned.1.call-done, bf16[128,512]{1,0:T(8,128)(2,1)} %reduce-scatter.6.cloned.1.call-done), channel_id=1, replica_groups=mesh['dp'=8,'mp'=16,'group'=2] {'group'}, use_global_device_ids=true, to_apply=%region_11.12 | all-reduce | flops 131072 | bytes 786432 | tf_op jit(solution)/shard_map/psum | solution.py:145
  523.6 52.0 %reduce-scatter.8.cloned.1.call-done = bf16[256,512]{1,0:T(8,128)(2,1)} async-done(((bf16[256,8192]{1,0:T(8,128)(2,1)}), bf16[256,512]{1,0:T(8,128)(2,1)}) %reduce-scatter.8.cloned.1.call-update) | async-done | bytes 262160 | tf_op jit(solution)/shard_map/reduce_scatter | solution.py:156
  575.5 1.8 convert.3
  (101 shorter events, 21.9 us)
Async XLA Ops:
  7.2 111.9 %copy-start = (bf16[256,4096]{1,0:T(8,128)(2,1)S(1)}, bf16[256,4096]{1,0:T(8,128)(2,1)}, u32[]{:S(2)}) copy-start(bf16[256,4096]{1,0:T(8,128)(2,1)} %param.16) | copy-start | bytes 6291460
  7.2 86.3 %all-gather.11.cloned.1.call-start = ((), (), s32[]{:S(2)}) async-start(), calls=%async_computation.5 | async-start | bytes 2228224 | tf_op jit(solution)/shard_map/all_gather | solution.py:36
  9.0 110.1 %all-gather.13.cloned.1.call-start = ((), (), s32[]{:S(2)}) async-start(), calls=%async_computation.8 | async-start | bytes 2228224 | tf_op jit(solution)/shard_map/all_gather | solution.py:37
  40.9 7.0 %copy-start.11 = (s32[2,1,128]{2,1,0:T(1,128)S(1)}, s32[2,1,128]{2,1,0:T(1,128)}, u32[]{:S(2)}) copy-start(s32[2,1,128]{2,1,0:T(1,128)} %param.10) | copy-start | bytes 3076
  40.9 30.3 %all-to-all-start = ((bf16[16,64,512]{2,1,0:T(8,128)(2,1)}), bf16[16,64,512]{2,1,0:T(8,128)(2,1)S(1)}, u32[]{:S(2)}, u32[]{:S(2)}) async-start(bf16[16,64,512]{2,1,0:T(8,128)(2,1)} %bitcast.98), calls=%async_computation | async-start | bytes 2097152 | tf_op jit(solution)/shard_map/all_to_all | solution.py:61
  47.9 136.2 %all-gather.15.cloned.1.call-start = ((), (), s32[]{:S(2)}) async-start(), calls=%async_computation.12 | async-start | bytes 4456448 | tf_op jit(solution)/shard_map/all_gather | solution.py:68
  73.0 164.5 %all-gather.9.cloned.1.call-start = ((), (), s32[]{:S(2)}) async-start(), calls=%async_computation.4 | async-start | bytes 4718592 | tf_op jit(solution)/shard_map/all_gather | solution.py:42
  73.0 20.4 %copy-start.12 = (s32[2]{0:T(128)S(1)}, s32[2]{0:T(128)}, u32[]{:S(2)}) copy-start(s32[2]{0:T(128)} %param.11) | copy-start | bytes 28
  74.1 18.4 %collective-permute-start = (bf16[512,512]{1,0:T(8,128)(2,1)S(1)}, bf16[512,512]{1,0:T(8,128)(2,1)S(1)}, u32[]{:S(2)}, u32[]{:S(2)}) collective-permute-start(bf16[512,512]{1,0:T(8,128)(2,1)S(1)} %fusion.46), channel_id=1, source_target_pairs={{0,1},{1,0},{2,3},{3,2},{4,5},{5,4},{6,7},{7,6},{8,9},{9,8},{10,11... | collective-permute-start | bytes 1572872 | tf_op jit(solution)/shard_map/ppermute | solution.py:43
  92.6 0.8 copy-start.5
  93.4 191.5 %all-reduce.16.cloned.1.call-start = ((), (), s32[]{:S(2)}) async-start(), calls=%async_computation.6 | async-start | bytes 262144 | tf_op jit(solution)/shard_map/psum | solution.py:103
  240.5 3.5 copy-start.3
  246.6 39.5 %copy-start.8 = (f32[2,2,64,128]{3,2,1,0:T(8,128)}, f32[2,2,64,128]{3,2,1,0:T(8,128)S(1)}, u32[]{:S(2)}) copy-start(f32[2,2,64,128]{3,2,1,0:T(8,128)S(1)} %get-tuple-element.26) | copy-start | bytes 393220
  247.5 76.6 %all-reduce.18.cloned.1.call-start = ((), (), s32[]{:S(2)}) async-start(), calls=%async_computation.9 | async-start | bytes 262144 | tf_op jit(solution)/shard_map/psum | solution.py:125
  264.9 21.7 %copy-start.6 = (bf16[2,64,2,128]{3,2,1,0:T(2,128)(2,1)}, bf16[2,64,2,128]{3,2,1,0:T(2,128)(2,1)S(1)}, u32[]{:S(2)}) copy-start(bf16[2,64,2,128]{3,2,1,0:T(2,128)(2,1)S(1)} %reshape.275) | copy-start | bytes 196612
  286.1 0.9 copy-start.9
  288.9 118.2 %reduce-scatter.4.cloned.1.call-start = ((), (), s32[]{:S(2)}) async-start(), calls=%async_computation.7 | async-start | bytes 2228224 | tf_op jit(solution)/shard_map/reduce_scatter | solution.py:138
  290.8 199.1 %reduce-scatter.6.cloned.1.call-start = ((), (), s32[]{:S(2)}) async-start(), calls=%async_computation.10 | async-start | bytes 2228224 | tf_op jit(solution)/shard_map/reduce_scatter | solution.py:141
  327.4 2.0 copy-start.7
  327.5 2.0 copy-start.10
  329.2 246.3 %reduce-scatter.8.cloned.1.call-start = ((), (), s32[]{:S(2)}) async-start(), calls=%async_computation.11 | async-start | bytes 4456448 | tf_op jit(solution)/shard_map/reduce_scatter | solution.py:156
  334.5 2.5 copy-start.1
  337.0 2.2 copy-start.2
  337.1 3.6 copy-start.4
Sparse Core Ops, SparseCore 0:
  11.0 53.4 all-gather.10
  66.9 52.0 all-gather.12
  122.0 62.0 all-gather.14
  186.3 51.1 all-gather.8
  247.6 37.2 all-reduce.15
  289.0 34.9 all-reduce.17
  327.6 79.4 reduce-scatter.3
  411.1 78.6 reduce-scatter.5
  493.5 81.9 reduce-scatter.7

commit v3 on v2

--- a/solution.py
+++ b/solution.py
@@ -29,6 +29,10 @@
     me_group = lax.axis_index("group")
     me_dp = lax.axis_index("dp")
     swap = [(0, 1), (1, 0)]
+
+    def group_sum(x):
+        return x + lax.ppermute(x, "group", swap)
+
     pad_rows = jnp.zeros((tail_rows, hidden.shape[1]), jnp.bfloat16)
     query_rows = jnp.concatenate([hidden[tail_rows:], pad_rows], 0)
     grad_rows = jnp.concatenate([grad_out[tail_rows:], pad_rows], 0)
@@ -74,7 +78,7 @@
         return lax.dynamic_slice_in_dim(x, (1 - me_group) * half, half, 1)
 
     query_part = jnp.dot(this_half(full_query), w_query, preferred_element_type=jnp.float32)
-    query = lax.psum(query_part, "group").astype(jnp.bfloat16)
+    query = group_sum(query_part).astype(jnp.bfloat16)
     n_here, n_there = this_half(neighbours), other_half(neighbours)
     keys = (
         jnp.dot(n_here, w_key, preferred_element_type=jnp.float32)
@@ -100,7 +104,7 @@
         preferred_element_type=jnp.float32,
     )
     partial_total = jnp.sum(weights, -1)
-    numer, partial_total = lax.psum((numer, partial_total), "group")
+    numer, partial_total = group_sum(numer), group_sum(partial_total)
     total = partial_total + 1.0
     attn = numer / jnp.transpose(total, (0, 2, 1))[..., None]
     attn_bf = attn.reshape(rows_here, heads_here * HD).astype(jnp.bfloat16)
@@ -113,7 +117,7 @@
 
     out_term = jnp.dot(attn_bf, w_out, preferred_element_type=jnp.float32)
     d_attn_part = contract(this_half(full_grad), w_out)
-    d_attn = lax.psum(d_attn_part, "group").astype(jnp.bfloat16)
+    d_attn = group_sum(d_attn_part).astype(jnp.bfloat16)
     d_block = d_attn.reshape(blocks_here, BLOCK, heads_here, HD)
     prob = weights / total[..., None]
     d_prob = jnp.einsum("cqhd,ckhd->chqk", d_block, value_block, preferred_element_type=jnp.float32)
@@ -122,7 +126,7 @@
     query_part = jnp.einsum(
         "chqk,ckhd->cqhd", d_score, key_block, preferred_element_type=jnp.float32
     )
-    query_grad = lax.psum(query_part, "group")
+    query_grad = group_sum(query_part)
     d_query = (query_grad * inv_root).astype(jnp.bfloat16).reshape(rows_here, heads_here * HD)
     d_keys = (
         jnp.einsum("chqk,cqhd->ckhd", d_score, query_block, preferred_element_type=jnp.float32)
@@ -134,18 +138,6 @@
     d_keys = d_keys.reshape(blocks_here * RET, heads_here * HD)
     d_values = d_values.reshape(blocks_here * RET, heads_here * HD)
     hid_term = contract(d_query, w_query)
-    out_cols, hid_cols = (
-        lax.psum_scatter(
-            place_half(out_term.astype(jnp.bfloat16)), "mp", scatter_dimension=1, tiled=True
-        ).astype(jnp.float32),
-        lax.psum_scatter(
-            place_half(hid_term.astype(jnp.bfloat16)), "mp", scatter_dimension=1, tiled=True
-        ).astype(jnp.float32),
-    )
-    out_cols, hid_cols = lax.psum((out_cols, hid_cols), "group")
-    zero_rows = jnp.zeros((tail_rows, out_cols.shape[1]), jnp.float32)
-    output = jnp.concatenate([zero_rows, out_cols[:keep_rows]], 0)
-    grad_hidden = jnp.concatenate([zero_rows, hid_cols[:keep_rows]], 0)
     term_here = contract(d_keys, w_key) + contract(d_values, w_value)
     term_there = contract(d_keys, wk_other) + contract(d_values, wv_other)
     neigh_term = jnp.where(
@@ -153,9 +145,22 @@
         jnp.concatenate([term_here, term_there], 1),
         jnp.concatenate([term_there, term_here], 1),
     )
-    neigh_cols = lax.psum_scatter(
-        neigh_term.astype(jnp.bfloat16), "mp", scatter_dimension=1, tiled=True
-    ).astype(jnp.float32)
+    stacked = jnp.concatenate(
+        [
+            place_half(out_term.astype(jnp.bfloat16)),
+            place_half(hid_term.astype(jnp.bfloat16)),
+            neigh_term.astype(jnp.bfloat16),
+        ],
+        0,
+    )
+    reduced = lax.psum_scatter(stacked, "mp", scatter_dimension=1, tiled=True)
+    both_cols = reduced[: 2 * rows_here]
+    both_cols = (both_cols + lax.ppermute(both_cols, "group", swap)).astype(jnp.float32)
+    out_cols, hid_cols = both_cols[:rows_here], both_cols[rows_here:]
+    zero_rows = jnp.zeros((tail_rows, out_cols.shape[1]), jnp.float32)
+    output = jnp.concatenate([zero_rows, out_cols[:keep_rows]], 0)
+    grad_hidden = jnp.concatenate([zero_rows, hid_cols[:keep_rows]], 0)
+    neigh_cols = reduced[2 * rows_here :].astype(jnp.float32)
     grad_neighbours = neigh_cols.reshape(blocks_here, 1, RET, neigh_cols.shape[1])
     return (output, grad_hidden, grad_neighbours)
 

time: 586 us -> 402 us (0.69)
  waiting for transfers between devices: 407 us -> 280 us
  blocking collectives: 87.3 us -> 20.3 us
  starting transfers between devices: 12 us -> 29.1 us
    reduce_scatter x3 -> x1, waiting for transfers between devices: 198 us -> 90.3 us  [per_device(): reduced = lax.psum_scatter(stacked, 'mp', scatter_dimension=1, tiled=True)]
    psum x3 -> x0, blocking collectives: 67 us -> none  [the longest x1 32.2 us: per_device(): out_cols, hid_cols = lax.psum((out_cols, hid_cols), 'group')]
    psum x2 -> x0, waiting for transfers between devices: 53.3 us -> none  [the longest x1 33.2 us: per_device(): query_grad = lax.psum(query_part, 'group')]
    ppermute x0 -> x6, waiting for transfers between devices: none -> 31.7 us  [the longest x5 17.6 us: group_sum(): return x + lax.ppermute(x, 'group', swap)]
    ppermute x0 -> x6, starting transfers between devices: none -> 17.4 us  [the longest x5 15.3 us: group_sum(): return x + lax.ppermute(x, 'group', swap)]
    all_gather x1, waiting for transfers between devices: 5.62 us -> 19.9 us  [per_device(): lax.all_gather(grad_rows, 'mp', axis=1, tiled=True)]
    all_gather x1, waiting for transfers between devices: 63 us -> 51.8 us  [per_device(): neighbours = lax.all_gather(own_cols, 'mp', axis=1, tiled=True)]
  transfers between devices with their start and end apart: 11 -> 13, of which waited for: 10 -> 10; matrix products, arithmetic and copies ran while one was open for 7% -> 9% of each run, Pallas kernels for 0% -> 0%
where the time goes in v3:
time: 402 us; the launch traced here: 399 us
  waiting for transfers between devices  280 us (70%)
  starting transfers between devices  29.1 us (7%)
  matrix products  26.4 us (7%)
  blocking collectives  20.3 us (5%)
  local copies, waits for them, and re-layouts  17.2 us (4%)
  between operations  14.2 us (4%)
  other arithmetic  11.4 us (3%)
    reduce_scatter x1, waiting for transfers between devices, per_device(): reduced = lax.psum_scatter(stacked, 'mp', scatter_dimension=1, tiled=True)  90.3 us
    all_gather x1, waiting for transfers between devices, per_device(): neighbours = lax.all_gather(own_cols, 'mp', axis=1, tiled=True)  51.8 us
    all_gather x1, waiting for transfers between devices, per_device(): lax.all_gather(lax.ppermute(kv_piece, 'group', swap), 'dp', axis=0, tiled...  50.5 us
    all_to_all x1, waiting for transfers between devices, per_device(): recv_buf = lax.all_to_all(send_buf, ('dp', 'group'), 0, 0, tiled=True)  22.2 us
    all_gather x1, waiting for transfers between devices, per_device(): lax.all_gather(grad_rows, 'mp', axis=1, tiled=True)  19.9 us
    ppermute x5, waiting for transfers between devices, group_sum(): return x + lax.ppermute(x, 'group', swap)  17.6 us
    ppermute x5, starting transfers between devices, group_sum(): return x + lax.ppermute(x, 'group', swap)  15.3 us
    ppermute x1, waiting for transfers between devices, per_device(): lax.ppermute(both_cols, 'group', swap)  14 us
  transfers between devices with their start and end apart: 13, of which 10 were waited for; matrix products, arithmetic and copies ran while one was open for 9% of the time, Pallas kernels for 0%

profile of v3, /device:TPU:192, one launch (start us, length us, event | category | flops | bytes accessed | tf_op | source)
XLA Modules:
  0.0 399.1 jit_solution(2553404690957030191)
XLA Ops:
  11.3 8.1 %all-gather.2 = f32[2,1,256]{2,1,0:T(1,128)S(1)} all-gather(f32[1,1,256]{2,1,0:T(1,128)S(1)} %convert_bitcast_fusion.1), channel_id=1, replica_groups=mesh['dp'=8,'mp'=16,'group'=2] {'group'}, dimensions={0}, use_global_device_ids=true | all-gather | bytes 3072 | tf_op jit(solution)/shard_map/all_gather | solution.py:56
  19.4 12.1 %all-gather.3 = f32[8,2,256]{2,1,0:T(2,128)S(1)} all-gather(f32[1,2,256]{2,1,0:T(2,128)S(1)} %copy.55), channel_id=2, replica_groups=mesh['dp'=8,'mp'=16,'group'=2] {'dp'}, dimensions={0}, use_global_device_ids=true | all-gather | bytes 18432 | tf_op jit(solution)/shard_map/all_gather | solution.py:57
  33.0 7.8 %gather_fusion = bf16[1024,512]{1,0:T(8,128)(2,1)} fusion(bf16[4096,512]{1,0:T(8,128)(2,1)} %param.12, s32[1024]{0:T(1024)S(1)} %broadcast_clamp_fusion), kind=kCustom, calls=%fused_computation | custom fusion | bytes 2101248 | tf_op jit(solution)/shard_map/gather | solution.py:64
  40.8 7.0 %all-to-all-start = ((bf16[16,64,512]{2,1,0:T(8,128)(2,1)}), bf16[16,64,512]{2,1,0:T(8,128)(2,1)S(1)}, u32[]{:S(2)}, u32[]{:S(2)}) async-start(bf16[16,64,512]{2,1,0:T(8,128)(2,1)} %bitcast.97), calls=%async_computation | async-start | bytes 2097152 | tf_op jit(solution)/shard_map/all_to_all | solution.py:65
  48.9 22.2 %all-to-all-done = bf16[16,64,512]{2,1,0:T(8,128)(2,1)S(1)} async-done(((bf16[16,64,512]{2,1,0:T(8,128)(2,1)}), bf16[16,64,512]{2,1,0:T(8,128)(2,1)S(1)}, u32[]{:S(2)}, u32[]{:S(2)}) %all-to-all-start) | async-done | bytes 1048608 | tf_op jit(solution)/shard_map/all_to_all | solution.py:65
  71.1 1.9 gather_fusion.1
  74.1 4.5 %collective-permute-start = (bf16[512,512]{1,0:T(8,128)(2,1)S(1)}, bf16[512,512]{1,0:T(8,128)(2,1)S(1)}, u32[]{:S(2)}, u32[]{:S(2)}) collective-permute-start(bf16[512,512]{1,0:T(8,128)(2,1)S(1)} %fusion.46), channel_id=1, source_target_pairs={{0,1},{1,0},{2,3},{3,2},{4,5},{5,4},{6,7},{7,6},{8,9},{9,8},{10,11... | collective-permute-start | bytes 1572872 | tf_op jit(solution)/shard_map/ppermute | solution.py:47
  78.6 13.9 %collective-permute-done = bf16[512,512]{1,0:T(8,128)(2,1)S(1)} collective-permute-done((bf16[512,512]{1,0:T(8,128)(2,1)S(1)}, bf16[512,512]{1,0:T(8,128)(2,1)S(1)}, u32[]{:S(2)}, u32[]{:S(2)}) %collective-permute-start) | collective-permute-done | bytes 524320 | tf_op jit(solution)/shard_map/ppermute | solution.py:47
  93.5 2.4 fusion.43
  95.8 3.3 collective-permute-start.1
  99.1 19.9 %all-gather.13.cloned.1.call-done = bf16[128,8192]{1,0:T(8,128)(2,1)} async-done(((bf16[128,512]{1,0:T(8,128)(2,1)}), bf16[128,8192]{1,0:T(8,128)(2,1)}) %all-gather.13.cloned.1.call-update) | async-done | bytes 2097168 | tf_op jit(solution)/shard_map/all_gather | solution.py:41
  119.0 2.1 fusion.41
  121.1 2.1 collective-permute-start.4
  123.2 9.0 %collective-permute-done.4 = f32[128,256]{1,0:T(8,128)S(1)} collective-permute-done((f32[128,256]{1,0:T(8,128)S(1)}, f32[128,256]{1,0:T(8,128)S(1)}, u32[]{:S(2)}, u32[]{:S(2)}) %collective-permute-start.4) | collective-permute-done | bytes 131104 | tf_op jit(solution)/shard_map/ppermute | solution.py:34
  132.3 51.8 %all-gather.15.cloned.1.call-done = bf16[256,8192]{1,0:T(8,128)(2,1)} async-done(((bf16[256,512]{1,0:T(8,128)(2,1)}), bf16[256,8192]{1,0:T(8,128)(2,1)}) %all-gather.15.cloned.1.call-update) | async-done | bytes 4194320 | tf_op jit(solution)/shard_map/all_gather | solution.py:72
  184.1 2.9 fusion.10
  187.0 50.5 %all-gather.9.cloned.1.call-done = bf16[4096,512]{1,0:T(8,128)(2,1)} async-done(((bf16[512,512]{1,0:T(8,128)(2,1)}), bf16[4096,512]{1,0:T(8,128)(2,1)}) %all-gather.9.cloned.1.call-update) | async-done | bytes 4194320 | tf_op jit(solution)/shard_map/all_gather | solution.py:46
  237.5 2.9 fusion.30
  240.8 1.5 collective-permute-start.3
  242.3 2.9 fusion.12
  245.3 2.4 fusion.25
  247.8 4.8 %collective-permute-start.2 = (f32[2,64,2,128]{3,1,2,0:T(8,128)S(1)}, f32[2,64,2,128]{3,1,2,0:T(8,128)S(1)}, u32[]{:S(2)}, u32[]{:S(2)}) collective-permute-start(f32[2,64,2,128]{3,1,2,0:T(8,128)S(1)} %convolution_bitcast_fusion.1), channel_id=1, source_target_pairs={{0,1},{1,0},{2,3},{3,2},{4,5},{5,4},{6,7},{7,6},{8,9},{9,8},{10,11... | collective-permute-start | bytes 393224 | tf_op jit(solution)/shard_map/ppermute | solution.py:34
  253.0 4.3 %fusion.1 = f32[256,4096]{1,0:T(8,128)} fusion(bf16[4096,512]{1,0:T(8,128)(2,1)} %all-gather.9.cloned.1.call-done, bf16[32,8,2,128]{3,2,1,0:T(2,128)(2,1)S(1)} %bitcast.98), kind=kOutput, calls=%fused_computation.13 | convolution fusion | flops 536870912 | bytes 6422528 | tf_op jit(solution)/shard_map/dot_general | solution.py:14
  257.3 2.5 collective-permute-done.2
  260.8 2.5 fusion.50
  264.1 3.7 collective-permute-start.5
  270.1 6.1 %collective-permute-done.5 = f32[2,64,2,128]{3,1,2,0:T(8,128)S(1)} collective-permute-done((f32[2,64,2,128]{3,1,2,0:T(8,128)S(1)}, f32[2,64,2,128]{3,1,2,0:T(8,128)S(1)}, u32[]{:S(2)}, u32[]{:S(2)}) %collective-permute-start.5) | collective-permute-done | bytes 131104 | tf_op jit(solution)/shard_map/ppermute | solution.py:34
  278.0 3.7 pad_maximum_fusion
  281.7 90.3 %reduce-scatter.2.cloned.1.call-done = bf16[512,512]{1,0:T(8,128)(2,1)} async-done(((bf16[512,8192]{1,0:T(8,128)(2,1)}), bf16[512,512]{1,0:T(8,128)(2,1)}) %reduce-scatter.2.cloned.1.call-update) | async-done | bytes 524304 | tf_op jit(solution)/shard_map/reduce_scatter | solution.py:156
  373.0 2.1 collective-permute-start.6
  375.1 14.0 %collective-permute-done.6 = bf16[256,512]{1,0:T(8,128)(2,1)S(1)} collective-permute-done((bf16[256,512]{1,0:T(8,128)(2,1)S(1)}, bf16[256,512]{1,0:T(8,128)(2,1)S(1)}, u32[]{:S(2)}, u32[]{:S(2)}) %collective-permute-start.6) | collective-permute-done | bytes 262176 | tf_op jit(solution)/shard_map/ppermute | solution.py:158
  389.1 1.1 fusion.80
  (93 shorter events, 18.5 us)
Async XLA Ops:
  7.2 111.9 %copy-start = (bf16[256,4096]{1,0:T(8,128)(2,1)S(1)}, bf16[256,4096]{1,0:T(8,128)(2,1)}, u32[]{:S(2)}) copy-start(bf16[256,4096]{1,0:T(8,128)(2,1)} %param.16) | copy-start | bytes 6291460
  7.2 86.3 %all-gather.11.cloned.1.call-start = ((), (), s32[]{:S(2)}) async-start(), calls=%async_computation.3 | async-start | bytes 2228224 | tf_op jit(solution)/shard_map/all_gather | solution.py:40
  9.0 110.1 %all-gather.13.cloned.1.call-start = ((), (), s32[]{:S(2)}) async-start(), calls=%async_computation.4 | async-start | bytes 2228224 | tf_op jit(solution)/shard_map/all_gather | solution.py:41
  40.8 7.0 %copy-start.7 = (s32[2,1,128]{2,1,0:T(1,128)S(1)}, s32[2,1,128]{2,1,0:T(1,128)}, u32[]{:S(2)}) copy-start(s32[2,1,128]{2,1,0:T(1,128)} %param.10) | copy-start | bytes 3076
  40.8 30.3 %all-to-all-start = ((bf16[16,64,512]{2,1,0:T(8,128)(2,1)}), bf16[16,64,512]{2,1,0:T(8,128)(2,1)S(1)}, u32[]{:S(2)}, u32[]{:S(2)}) async-start(bf16[16,64,512]{2,1,0:T(8,128)(2,1)} %bitcast.97), calls=%async_computation | async-start | bytes 2097152 | tf_op jit(solution)/shard_map/all_to_all | solution.py:65
  47.8 136.2 %all-gather.15.cloned.1.call-start = ((), (), s32[]{:S(2)}) async-start(), calls=%async_computation.6 | async-start | bytes 4456448 | tf_op jit(solution)/shard_map/all_gather | solution.py:72
  73.0 164.5 %all-gather.9.cloned.1.call-start = ((), (), s32[]{:S(2)}) async-start(), calls=%async_computation.2 | async-start | bytes 4718592 | tf_op jit(solution)/shard_map/all_gather | solution.py:46
  73.0 20.4 %copy-start.8 = (s32[2]{0:T(128)S(1)}, s32[2]{0:T(128)}, u32[]{:S(2)}) copy-start(s32[2]{0:T(128)} %param.11) | copy-start | bytes 28
  74.1 18.4 %collective-permute-start = (bf16[512,512]{1,0:T(8,128)(2,1)S(1)}, bf16[512,512]{1,0:T(8,128)(2,1)S(1)}, u32[]{:S(2)}, u32[]{:S(2)}) collective-permute-start(bf16[512,512]{1,0:T(8,128)(2,1)S(1)} %fusion.46), channel_id=1, source_target_pairs={{0,1},{1,0},{2,3},{3,2},{4,5},{5,4},{6,7},{7,6},{8,9},{9,8},{10,11... | collective-permute-start | bytes 1572872 | tf_op jit(solution)/shard_map/ppermute | solution.py:47
  92.5 0.8 copy-start.6
  93.4 278.7 %reduce-scatter.2.cloned.1.call-start = ((), (), s32[]{:S(2)}) async-start(), calls=%async_computation.5 | async-start | bytes 8912896 | tf_op jit(solution)/shard_map/reduce_scatter | solution.py:156
  95.8 27.3 %collective-permute-start.1 = (f32[128,256]{1,0:T(8,128)S(1)}, f32[128,256]{1,0:T(8,128)S(1)}, u32[]{:S(2)}, u32[]{:S(2)}) collective-permute-start(f32[128,256]{1,0:T(8,128)S(1)} %fusion.43), channel_id=1, source_target_pairs={{0,1},{1,0},{2,3},{3,2},{4,5},{5,4},{6,7},{7,6},{8,9},{9,8},{10,11... | collective-permute-start | bytes 393224 | tf_op jit(solution)/shard_map/ppermute | solution.py:34
  121.1 11.2 %collective-permute-start.4 = (f32[128,256]{1,0:T(8,128)S(1)}, f32[128,256]{1,0:T(8,128)S(1)}, u32[]{:S(2)}, u32[]{:S(2)}) collective-permute-start(f32[128,256]{1,0:T(8,128)S(1)} %fusion.41), channel_id=1, source_target_pairs={{0,1},{1,0},{2,3},{3,2},{4,5},{5,4},{6,7},{7,6},{8,9},{9,8},{10,11... | collective-permute-start | bytes 393224 | tf_op jit(solution)/shard_map/ppermute | solution.py:34
  240.8 4.5 %copy-start.4 = (bf16[4096,512]{1,0:T(8,128)(2,1)S(1)}, bf16[4096,512]{1,0:T(8,128)(2,1)}, u32[]{:S(2)}) copy-start(bf16[4096,512]{1,0:T(8,128)(2,1)} %all-gather.9.cloned.1.call-done) | copy-start | bytes 12582916
  240.8 11.8 %collective-permute-start.3 = (f32[2,2,64]{2,1,0:T(2,128)S(1)}, f32[2,2,64]{2,1,0:T(2,128)S(1)}, u32[]{:S(2)}, u32[]{:S(2)}) collective-permute-start(f32[2,2,64]{2,1,0:T(2,128)S(1)} %get-tuple-element.23), channel_id=1, source_target_pairs={{0,1},{1,0},{2,3},{3,2},{4,5},{5,4},{6,7},{7,6},{8,9},{9,8},{10,11... | collective-permute-start | bytes 3080 | tf_op jit(solution)/shard_map/ppermute | solution.py:34
  247.8 12.0 %collective-permute-start.2 = (f32[2,64,2,128]{3,1,2,0:T(8,128)S(1)}, f32[2,64,2,128]{3,1,2,0:T(8,128)S(1)}, u32[]{:S(2)}, u32[]{:S(2)}) collective-permute-start(f32[2,64,2,128]{3,1,2,0:T(8,128)S(1)} %convolution_bitcast_fusion.1), channel_id=1, source_target_pairs={{0,1},{1,0},{2,3},{3,2},{4,5},{5,4},{6,7},{7,6},{8,9},{9,8},{10,11... | collective-permute-start | bytes 393224 | tf_op jit(solution)/shard_map/ppermute | solution.py:34
  260.8 2.5 copy-start.1
  263.3 4.5 %copy-start.2 = (f32[256,4096]{1,0:T(8,128)S(1)}, f32[256,4096]{1,0:T(8,128)}, u32[]{:S(2)}) copy-start(f32[256,4096]{1,0:T(8,128)} %fusion.1) | copy-start | bytes 12582916
  263.3 4.5 %copy-start.5 = (bf16[4096,512]{1,0:T(8,128)(2,1)S(1)}, bf16[4096,512]{1,0:T(8,128)(2,1)}, u32[]{:S(2)}) copy-start(bf16[4096,512]{1,0:T(8,128)(2,1)} %all-gather.9.cloned.1.call-done) | copy-start | bytes 12582916
  264.1 12.2 %collective-permute-start.5 = (f32[2,64,2,128]{3,1,2,0:T(8,128)S(1)}, f32[2,64,2,128]{3,1,2,0:T(8,128)S(1)}, u32[]{:S(2)}, u32[]{:S(2)}) collective-permute-start(f32[2,64,2,128]{3,1,2,0:T(8,128)S(1)} %convolution_bitcast_fusion), channel_id=1, source_target_pairs={{0,1},{1,0},{2,3},{3,2},{4,5},{5,4},{6,7},{7,6},{8,9},{9,8},{10,11... | collective-permute-start | bytes 393224 | tf_op jit(solution)/shard_map/ppermute | solution.py:34
  269.6 6.7 %copy-start.3 = (bf16[4096,256]{1,0:T(8,128)(2,1)S(1)}, bf16[4096,256]{1,0:T(8,128)(2,1)}, u32[]{:S(2)}) copy-start(bf16[4096,256]{1,0:T(8,128)(2,1)} %param.13) | copy-start | bytes 6291460
  373.0 16.1 %collective-permute-start.6 = (bf16[256,512]{1,0:T(8,128)(2,1)S(1)}, bf16[256,512]{1,0:T(8,128)(2,1)S(1)}, u32[]{:S(2)}, u32[]{:S(2)}) collective-permute-start(bf16[256,512]{1,0:T(8,128)(2,1)S(1)} %slice.60), channel_id=1, source_target_pairs={{0,1},{1,0},{2,3},{3,2},{4,5},{5,4},{6,7},{7,6},{8,9},{9,8},{10,11... | collective-permute-start | bytes 786440 | tf_op jit(solution)/shard_map/ppermute | solution.py:158
Sparse Core Ops, SparseCore 0:
  11.0 53.4 all-gather.10
  66.9 52.0 all-gather.12
  122.0 62.0 all-gather.14
  186.3 51.1 all-gather.8
  281.8 90.1 reduce-scatter.1

commit v4 on v3

--- a/solution.py
+++ b/solution.py
@@ -40,21 +40,37 @@
         lax.all_gather(query_rows, "mp", axis=1, tiled=True),
         lax.all_gather(grad_rows, "mp", axis=1, tiled=True),
     )
+    flat_ids = neighbour_ids.reshape(-1)
+    n_ids = flat_ids.shape[0]
+    block_rows = embed_table.shape[0]
+    owners = lax.axis_size("dp") * lax.axis_size("group")
+    cap = n_ids // 4
     piece_rows = half // lax.axis_size("dp")
     kv_local = jnp.concatenate([w_key, w_value], axis=1)
+    width_kv = kv_local.shape[1]
     kv_piece = lax.dynamic_slice_in_dim(kv_local, me_dp * piece_rows, piece_rows, 0)
-    kv_other = lax.all_gather(
-        lax.ppermute(kv_piece, "group", swap), "dp", axis=0, tiled=True
-    )
+
+    def id_row(ids):
+        row = jnp.concatenate([ids // 256, ids % 256]).astype(jnp.bfloat16)
+        return jnp.pad(row, (0, width_kv - row.shape[0]))[None, :]
+
+    tail_pad = jnp.zeros((7, width_kv), jnp.bfloat16)
+    mine_row = id_row(flat_ids)
+    got = lax.ppermute(jnp.concatenate([kv_piece, mine_row, tail_pad], 0), "group", swap)
+    partner_row = got[piece_rows : piece_rows + 1]
+    pair_rows = jnp.where(
+        me_group == 0,
+        jnp.concatenate([mine_row, partner_row], 0),
+        jnp.concatenate([partner_row, mine_row], 0),
+    )
+    shared = jnp.concatenate([got[:piece_rows], pair_rows, tail_pad[:6]], 0)
+    gathered = lax.all_gather(shared, "dp", axis=0)
+    kv_other = gathered[:, :piece_rows].reshape(-1, width_kv)
     cols_kv = w_key.shape[1]
     wk_other, wv_other = kv_other[:, :cols_kv], kv_other[:, cols_kv:]
-
-    flat_ids = neighbour_ids.reshape(-1)
-    block_rows = embed_table.shape[0]
-    owners = lax.axis_size("dp") * lax.axis_size("group")
-    cap = flat_ids.shape[0] // 4
-    ids_f = lax.all_gather(flat_ids.astype(jnp.float32), "group", axis=0)
-    every_id = lax.all_gather(ids_f, "dp", axis=0).astype(jnp.int32).reshape(owners, -1)
+    id_bytes = gathered[:, piece_rows : piece_rows + 2, : 2 * n_ids].astype(jnp.int32)
+    id_bytes = id_bytes.reshape(owners, 2, n_ids)
+    every_id = id_bytes[:, 0] * 256 + id_bytes[:, 1]
     owner = me_dp * lax.axis_size("group") + me_group
     local_ids = every_id - owner * block_rows
     inside = (local_ids >= 0) & (local_ids < block_rows)

time: 402 us -> 432 us (1.075)
  waiting for transfers between devices: 280 us -> 335 us
  blocking collectives: 20.3 us -> 0 us
    all_gather x1, waiting for transfers between devices: 0.02 us -> 51 us  [per_device(): lax.all_gather(query_rows, 'mp', axis=1, tiled=True)]
    all_gather x2 -> x0, blocking collectives: 20.3 us -> none  [the longest x1 12.1 us: per_device(): lax.all_gather(ids_f, 'dp', axis=0).astype(jnp.int32).reshape(owners, -1)]
    ppermute x1, waiting for transfers between devices: 13.9 us -> 28.4 us  [per_device(): lax.ppermute(jnp.concatenate([kv_piece, mine_row, tail_pad], 0), 'group',...]
    all_gather x1, waiting for transfers between devices: 19.9 us -> 14.4 us  [per_device(): lax.all_gather(grad_rows, 'mp', axis=1, tiled=True)]
    all_gather x1, waiting for transfers between devices: 51.8 us -> 46.7 us  [per_device(): neighbours = lax.all_gather(own_cols, 'mp', axis=1, tiled=True)]
    slice x1 -> x5, local copies, waits for them, and re-layouts: 0.18 us -> 4.8 us  [the longest x1 4.58 us: per_device(): kv_other = gathered[:, :piece_rows].reshape(-1, width_kv)]
  transfers between devices with their start and end apart: 13 -> 13, of which waited for: 10 -> 11; matrix products, arithmetic and copies ran while one was open for 9% -> 7% of each run, Pallas kernels for 0% -> 0%
where the time goes in v4:
time: 432 us; the launch traced here: 430 us
  waiting for transfers between devices  335 us (78%)
  starting transfers between devices  24.8 us (6%)
  matrix products  22.4 us (5%)
  local copies, waits for them, and re-layouts  20.2 us (5%)
  between operations  14.3 us (3%)
  other arithmetic  13.4 us (3%)
    reduce_scatter x1, waiting for transfers between devices, per_device(): reduced = lax.psum_scatter(stacked, 'mp', scatter_dimension=1, tiled=True)  88.8 us
    all_gather x1, waiting for transfers between devices, per_device(): gathered = lax.all_gather(shared, 'dp', axis=0)  51.4 us
    all_gather x1, waiting for transfers between devices, per_device(): lax.all_gather(query_rows, 'mp', axis=1, tiled=True)  51 us
    all_gather x1, waiting for transfers between devices, per_device(): neighbours = lax.all_gather(own_cols, 'mp', axis=1, tiled=True)  46.7 us
    ppermute x1, waiting for transfers between devices, per_device(): lax.ppermute(jnp.concatenate([kv_piece, mine_row, tail_pad], 0), 'group',...  28.4 us
    all_to_all x1, waiting for transfers between devices, per_device(): recv_buf = lax.all_to_all(send_buf, ('dp', 'group'), 0, 0, tiled=True)  22.2 us
    ppermute x5, waiting for transfers between devices, group_sum(): return x + lax.ppermute(x, 'group', swap)  17.7 us
    ppermute x5, starting transfers between devices, group_sum(): return x + lax.ppermute(x, 'group', swap)  14.4 us
  transfers between devices with their start and end apart: 13, of which 11 were waited for; matrix products, arithmetic and copies ran while one was open for 7% of the time, Pallas kernels for 0%

profile of v4, /device:TPU:192, one launch (start us, length us, event | category | flops | bytes accessed | tf_op | source)
XLA Modules:
  0.0 429.9 jit_solution(14530083088535112875)
XLA Ops:
  8.2 1.1 fusion.38
  10.2 28.4 %collective-permute-done = bf16[520,512]{1,0:T(8,128)(2,1)S(1)} collective-permute-done((bf16[520,512]{1,0:T(8,128)(2,1)S(1)}, bf16[520,512]{1,0:T(8,128)(2,1)S(1)}, u32[]{:S(2)}, u32[]{:S(2)}) %collective-permute-start) | collective-permute-done | bytes 532512 | tf_op jit(solution)/shard_map/ppermute | solution.py:59
  41.2 51.4 %all-gather.11.cloned.1.call-done = bf16[4160,512]{1,0:T(8,128)(2,1)} async-done(((bf16[520,512]{1,0:T(8,128)(2,1)}), bf16[4160,512]{1,0:T(8,128)(2,1)}) %all-gather.11.cloned.1.call-update) | async-done | bytes 4259856 | tf_op jit(solution)/shard_map/all_gather | solution.py:67
  95.0 7.8 %gather_fusion = bf16[1024,512]{1,0:T(8,128)(2,1)} fusion(bf16[4096,512]{1,0:T(8,128)(2,1)} %param.12, s32[1024]{0:T(1024)S(1)} %broadcast_clamp_fusion), kind=kCustom, calls=%fused_computation | custom fusion | bytes 2101248 | tf_op jit(solution)/shard_map/gather | solution.py:80
  102.8 7.5 %all-to-all-start = ((bf16[16,64,512]{2,1,0:T(8,128)(2,1)}), bf16[16,64,512]{2,1,0:T(8,128)(2,1)S(1)}, u32[]{:S(2)}, u32[]{:S(2)}) async-start(bf16[16,64,512]{2,1,0:T(8,128)(2,1)} %bitcast.99), calls=%async_computation | async-start | bytes 2097152 | tf_op jit(solution)/shard_map/all_to_all | solution.py:81
  111.3 22.2 %all-to-all-done = bf16[16,64,512]{2,1,0:T(8,128)(2,1)S(1)} async-done(((bf16[16,64,512]{2,1,0:T(8,128)(2,1)}), bf16[16,64,512]{2,1,0:T(8,128)(2,1)S(1)}, u32[]{:S(2)}, u32[]{:S(2)}) %all-to-all-start) | async-done | bytes 1048608 | tf_op jit(solution)/shard_map/all_to_all | solution.py:81
  133.5 1.9 gather_fusion.1
  135.5 14.4 %all-gather.9.cloned.1.call-done = bf16[128,8192]{1,0:T(8,128)(2,1)} async-done(((bf16[128,512]{1,0:T(8,128)(2,1)}), bf16[128,8192]{1,0:T(8,128)(2,1)}) %all-gather.9.cloned.1.call-update) | async-done | bytes 2097168 | tf_op jit(solution)/shard_map/all_gather | solution.py:41
  149.9 2.1 fusion.33
  151.9 2.1 collective-permute-start.4
  154.0 51.0 %all-gather.7.cloned.1.call-done = bf16[128,8192]{1,0:T(8,128)(2,1)} async-done(((bf16[128,512]{1,0:T(8,128)(2,1)}), bf16[128,8192]{1,0:T(8,128)(2,1)}) %all-gather.7.cloned.1.call-update) | async-done | bytes 2097168 | tf_op jit(solution)/shard_map/all_gather | solution.py:40
  205.0 2.4 fusion.35
  207.4 2.1 collective-permute-start.1
  209.5 9.0 %collective-permute-done.1 = f32[128,256]{1,0:T(8,128)S(1)} collective-permute-done((f32[128,256]{1,0:T(8,128)S(1)}, f32[128,256]{1,0:T(8,128)S(1)}, u32[]{:S(2)}, u32[]{:S(2)}) %collective-permute-start.1) | collective-permute-done | bytes 131104 | tf_op jit(solution)/shard_map/ppermute | solution.py:34
  218.6 4.6 %slice.91 = bf16[8,512,512]{2,1,0:T(8,128)(2,1)} slice(bf16[8,520,512]{2,1,0:T(8,128)(2,1)} %bitcast.101), slice={[0:8], [0:512], [0:512]} | slice | bytes 8388608 | tf_op jit(solution)/shard_map/slice | solution.py:68
  223.1 46.7 %all-gather.13.cloned.1.call-done = bf16[256,8192]{1,0:T(8,128)(2,1)} async-done(((bf16[256,512]{1,0:T(8,128)(2,1)}), bf16[256,8192]{1,0:T(8,128)(2,1)}) %all-gather.13.cloned.1.call-update) | async-done | bytes 4194320 | tf_op jit(solution)/shard_map/all_gather | solution.py:88
  269.9 3.1 fusion.6
  273.0 2.3 fusion.20
  275.7 2.1 collective-permute-start.3
  277.7 2.9 fusion.2
  280.7 2.3 fusion.23
  283.2 4.2 collective-permute-start.2
  287.8 6.5 %collective-permute-done.2 = f32[2,64,2,128]{3,1,2,0:T(8,128)S(1)} collective-permute-done((f32[2,64,2,128]{3,1,2,0:T(8,128)S(1)}, f32[2,64,2,128]{3,1,2,0:T(8,128)S(1)}, u32[]{:S(2)}, u32[]{:S(2)}) %collective-permute-start.2) | collective-permute-done | bytes 131104 | tf_op jit(solution)/shard_map/ppermute | solution.py:34
  295.3 2.5 fusion.4
  298.6 4.0 collective-permute-start.5
  305.0 1.0 fusion
  306.4 2.2 collective-permute-done.5
  310.4 3.5 pad_maximum_fusion
  314.0 88.8 %reduce-scatter.2.cloned.1.call-done = bf16[512,512]{1,0:T(8,128)(2,1)} async-done(((bf16[512,8192]{1,0:T(8,128)(2,1)}), bf16[512,512]{1,0:T(8,128)(2,1)}) %reduce-scatter.2.cloned.1.call-update) | async-done | bytes 524304 | tf_op jit(solution)/shard_map/reduce_scatter | solution.py:172
  403.7 2.1 collective-permute-start.6
  405.8 14.1 %collective-permute-done.6 = bf16[256,512]{1,0:T(8,128)(2,1)S(1)} collective-permute-done((bf16[256,512]{1,0:T(8,128)(2,1)S(1)}, bf16[256,512]{1,0:T(8,128)(2,1)S(1)}, u32[]{:S(2)}, u32[]{:S(2)}) %collective-permute-start.6) | collective-permute-done | bytes 262176 | tf_op jit(solution)/shard_map/ppermute | solution.py:174
  419.9 1.1 fusion.76
  (107 shorter events, 18.3 us)
Async XLA Ops:
  7.2 142.7 %copy-start = (bf16[256,4096]{1,0:T(8,128)(2,1)S(1)}, bf16[256,4096]{1,0:T(8,128)(2,1)}, u32[]{:S(2)}) copy-start(bf16[256,4096]{1,0:T(8,128)(2,1)} %param.16) | copy-start | bytes 6291460
  7.2 85.4 %all-gather.11.cloned.1.call-start = ((), (), s32[]{:S(2)}) async-start(), calls=%async_computation.5 | async-start | bytes 4792320 | tf_op jit(solution)/shard_map/all_gather | solution.py:67
  9.2 30.4 %copy-start.7 = (bf16[128,512]{1,0:T(8,128)(2,1)S(1)}, bf16[128,512]{1,0:T(8,128)(2,1)}, u32[]{:S(2)}) copy-start(bf16[128,512]{1,0:T(8,128)(2,1)} %param.17) | copy-start | bytes 393220
  9.3 31.2 %copy-start.8 = (bf16[128,512]{1,0:T(8,128)(2,1)S(1)}, bf16[128,512]{1,0:T(8,128)(2,1)}, u32[]{:S(2)}) copy-start(bf16[128,512]{1,0:T(8,128)(2,1)} %param.9) | copy-start | bytes 393220
  9.4 29.1 %collective-permute-start = (bf16[520,512]{1,0:T(8,128)(2,1)S(1)}, bf16[520,512]{1,0:T(8,128)(2,1)S(1)}, u32[]{:S(2)}, u32[]{:S(2)}) collective-permute-start(bf16[520,512]{1,0:T(8,128)(2,1)S(1)} %maximum_maximum_fusion), channel_id=1, source_target_pairs={{0,1},{1,0},{2,3},{3,2},{4,5},{5,4},{6,7},{7,6},{8,9},{9,8},{10,11... | collective-permute-start | bytes 1597448 | tf_op jit(solution)/shard_map/ppermute | solution.py:59
  39.6 110.2 %all-gather.9.cloned.1.call-start = ((), (), s32[]{:S(2)}) async-start(), calls=%async_computation.3 | async-start | bytes 2228224 | tf_op jit(solution)/shard_map/all_gather | solution.py:41
  40.4 164.6 %all-gather.7.cloned.1.call-start = ((), (), s32[]{:S(2)}) async-start(), calls=%async_computation.2 | async-start | bytes 2228224 | tf_op jit(solution)/shard_map/all_gather | solution.py:40
  102.8 7.5 %copy-start.9 = (s32[2,1,128]{2,1,0:T(1,128)S(1)}, s32[2,1,128]{2,1,0:T(1,128)}, u32[]{:S(2)}) copy-start(s32[2,1,128]{2,1,0:T(1,128)} %param.10) | copy-start | bytes 3076
  102.8 32.7 %copy-start.10 = (s32[2]{0:T(128)S(1)}, s32[2]{0:T(128)}, u32[]{:S(2)}) copy-start(s32[2]{0:T(128)} %param.11) | copy-start | bytes 28
  102.8 30.7 %all-to-all-start = ((bf16[16,64,512]{2,1,0:T(8,128)(2,1)}), bf16[16,64,512]{2,1,0:T(8,128)(2,1)S(1)}, u32[]{:S(2)}, u32[]{:S(2)}) async-start(bf16[16,64,512]{2,1,0:T(8,128)(2,1)} %bitcast.99), calls=%async_computation | async-start | bytes 2097152 | tf_op jit(solution)/shard_map/all_to_all | solution.py:81
  110.2 159.6 %all-gather.13.cloned.1.call-start = ((), (), s32[]{:S(2)}) async-start(), calls=%async_computation.6 | async-start | bytes 4456448 | tf_op jit(solution)/shard_map/all_gather | solution.py:88
  135.4 267.3 %reduce-scatter.2.cloned.1.call-start = ((), (), s32[]{:S(2)}) async-start(), calls=%async_computation.4 | async-start | bytes 8912896 | tf_op jit(solution)/shard_map/reduce_scatter | solution.py:172
  151.9 57.5 %collective-permute-start.4 = (f32[128,256]{1,0:T(8,128)S(1)}, f32[128,256]{1,0:T(8,128)S(1)}, u32[]{:S(2)}, u32[]{:S(2)}) collective-permute-start(f32[128,256]{1,0:T(8,128)S(1)} %fusion.33), channel_id=1, source_target_pairs={{0,1},{1,0},{2,3},{3,2},{4,5},{5,4},{6,7},{7,6},{8,9},{9,8},{10,11... | collective-permute-start | bytes 393224 | tf_op jit(solution)/shard_map/ppermute | solution.py:34
  207.4 11.2 %collective-permute-start.1 = (f32[128,256]{1,0:T(8,128)S(1)}, f32[128,256]{1,0:T(8,128)S(1)}, u32[]{:S(2)}, u32[]{:S(2)}) collective-permute-start(f32[128,256]{1,0:T(8,128)S(1)} %fusion.35), channel_id=1, source_target_pairs={{0,1},{1,0},{2,3},{3,2},{4,5},{5,4},{6,7},{7,6},{8,9},{9,8},{10,11... | collective-permute-start | bytes 393224 | tf_op jit(solution)/shard_map/ppermute | solution.py:34
  269.9 3.1 copy-start.1
  275.6 5.0 %copy-start.3 = (bf16[4096,256]{1,0:T(8,128)(2,1)S(1)}, bf16[4096,256]{1,0:T(8,128)(2,1)}, u32[]{:S(2)}) copy-start(bf16[4096,256]{1,0:T(8,128)(2,1)} %param.15) | copy-start | bytes 6291460
  275.7 11.7 %collective-permute-start.3 = (f32[2,2,64]{2,1,0:T(2,128)S(1)}, f32[2,2,64]{2,1,0:T(2,128)S(1)}, u32[]{:S(2)}, u32[]{:S(2)}) collective-permute-start(f32[2,2,64]{2,1,0:T(2,128)S(1)} %get-tuple-element.26), channel_id=1, source_target_pairs={{0,1},{1,0},{2,3},{3,2},{4,5},{5,4},{6,7},{7,6},{8,9},{9,8},{10,11... | collective-permute-start | bytes 3080 | tf_op jit(solution)/shard_map/ppermute | solution.py:34
  283.2 11.1 %collective-permute-start.2 = (f32[2,64,2,128]{3,1,2,0:T(8,128)S(1)}, f32[2,64,2,128]{3,1,2,0:T(8,128)S(1)}, u32[]{:S(2)}, u32[]{:S(2)}) collective-permute-start(f32[2,64,2,128]{3,1,2,0:T(8,128)S(1)} %convolution_bitcast_fusion.1), channel_id=1, source_target_pairs={{0,1},{1,0},{2,3},{3,2},{4,5},{5,4},{6,7},{7,6},{8,9},{9,8},{10,11... | collective-permute-start | bytes 393224 | tf_op jit(solution)/shard_map/ppermute | solution.py:34
  295.3 2.5 copy-start.2
  297.8 4.8 %copy-start.5 = (bf16[8,512,512]{2,1,0:T(8,128)(2,1)S(1)}, bf16[8,512,512]{2,1,0:T(8,128)(2,1)}, u32[]{:S(2)}) copy-start(bf16[8,512,512]{2,1,0:T(8,128)(2,1)} %slice.91) | copy-start | bytes 12582916
  298.6 10.0 %collective-permute-start.5 = (f32[2,64,2,128]{3,1,2,0:T(8,128)S(1)}, f32[2,64,2,128]{3,1,2,0:T(8,128)S(1)}, u32[]{:S(2)}, u32[]{:S(2)}) collective-permute-start(f32[2,64,2,128]{3,1,2,0:T(8,128)S(1)} %convolution_bitcast_fusion), channel_id=1, source_target_pairs={{0,1},{1,0},{2,3},{3,2},{4,5},{5,4},{6,7},{7,6},{8,9},{9,8},{10,11... | collective-permute-start | bytes 393224 | tf_op jit(solution)/shard_map/ppermute | solution.py:34
  302.6 1.6 copy-start.4
  306.0 2.8 copy-start.6
  403.7 16.2 %collective-permute-start.6 = (bf16[256,512]{1,0:T(8,128)(2,1)S(1)}, bf16[256,512]{1,0:T(8,128)(2,1)S(1)}, u32[]{:S(2)}, u32[]{:S(2)}) collective-permute-start(bf16[256,512]{1,0:T(8,128)(2,1)S(1)} %slice.94), channel_id=1, source_target_pairs={{0,1},{1,0},{2,3},{3,2},{4,5},{5,4},{6,7},{7,6},{8,9},{9,8},{10,11... | collective-permute-start | bytes 786440 | tf_op jit(solution)/shard_map/ppermute | solution.py:174
Sparse Core Ops, SparseCore 0:
  39.7 52.8 all-gather.10
  95.6 54.2 all-gather.8
  152.8 52.0 all-gather.6
  207.8 62.0 all-gather.12
  314.1 88.5 reduce-scatter.1

commit v5 on v3

--- a/solution.py
+++ b/solution.py
@@ -36,10 +36,7 @@
     pad_rows = jnp.zeros((tail_rows, hidden.shape[1]), jnp.bfloat16)
     query_rows = jnp.concatenate([hidden[tail_rows:], pad_rows], 0)
     grad_rows = jnp.concatenate([grad_out[tail_rows:], pad_rows], 0)
-    full_query, full_grad = (
-        lax.all_gather(query_rows, "mp", axis=1, tiled=True),
-        lax.all_gather(grad_rows, "mp", axis=1, tiled=True),
-    )
+    full_query = lax.all_gather(query_rows, "mp", axis=1, tiled=True)
     piece_rows = half // lax.axis_size("dp")
     kv_local = jnp.concatenate([w_key, w_value], axis=1)
     kv_piece = lax.dynamic_slice_in_dim(kv_local, me_dp * piece_rows, piece_rows, 0)
@@ -70,6 +67,8 @@
     ) - 1
     own_cols = recv_buf.reshape(owners * cap, -1)[own_owner * cap + own_rank]
     neighbours = lax.all_gather(own_cols, "mp", axis=1, tiled=True)
+    grad_rows, neighbours = lax.optimization_barrier((grad_rows, neighbours))
+    full_grad = lax.all_gather(grad_rows, "mp", axis=1, tiled=True)
 
     def this_half(x):
         return lax.dynamic_slice_in_dim(x, me_group * half, half, 1)

time: 402 us -> 453 us (1.13)
  waiting for transfers between devices: 280 us -> 339 us
    all_gather x2, waiting for transfers between devices: 20 us -> 96.7 us  [the longest x1 55 us: per_device(): full_query = lax.all_gather(query_rows, 'mp', axis=1, tiled=True)]
    all_gather x1, waiting for transfers between devices: 50.5 us -> 37.1 us  [per_device(): lax.all_gather(lax.ppermute(kv_piece, 'group', swap), 'dp', axis=0, tiled...]
    all_gather x1, waiting for transfers between devices: 51.8 us -> 43.5 us  [per_device(): neighbours = lax.all_gather(own_cols, 'mp', axis=1, tiled=True)]
  transfers between devices with their start and end apart: 13 -> 13, of which waited for: 10 -> 11; matrix products, arithmetic and copies ran while one was open for 9% -> 5% of each run, Pallas kernels for 0% -> 0%
where the time goes in v5:
time: 453 us; the launch traced here: 451 us
  waiting for transfers between devices  339 us (75%)
  starting transfers between devices  26.3 us (6%)
  matrix products  22.9 us (5%)
  blocking collectives  20.3 us (4%)
  local copies, waits for them, and re-layouts  16.7 us (4%)
  between operations  14.2 us (3%)
  other arithmetic  11.4 us (3%)
    reduce_scatter x1, waiting for transfers between devices, per_device(): reduced = lax.psum_scatter(stacked, 'mp', scatter_dimension=1, tiled=True)  91.5 us
    all_gather x1, waiting for transfers between devices, per_device(): full_query = lax.all_gather(query_rows, 'mp', axis=1, tiled=True)  55 us
    all_gather x1, waiting for transfers between devices, per_device(): neighbours = lax.all_gather(own_cols, 'mp', axis=1, tiled=True)  43.5 us
    all_gather x1, waiting for transfers between devices, per_device(): full_grad = lax.all_gather(grad_rows, 'mp', axis=1, tiled=True)  41.6 us
    all_gather x1, waiting for transfers between devices, per_device(): lax.all_gather(lax.ppermute(kv_piece, 'group', swap), 'dp', axis=0, tiled...  37.1 us
    all_to_all x1, waiting for transfers between devices, per_device(): recv_buf = lax.all_to_all(send_buf, ('dp', 'group'), 0, 0, tiled=True)  22.2 us
    ppermute x5, waiting for transfers between devices, group_sum(): return x + lax.ppermute(x, 'group', swap)  19.7 us
    ppermute x1, waiting for transfers between devices, per_device(): lax.ppermute(both_cols, 'group', swap)  14 us
  transfers between devices with their start and end apart: 13, of which 11 were waited for; matrix products, arithmetic and copies ran while one was open for 5% of the time, Pallas kernels for 0%

profile of v5, /device:TPU:192, one launch (start us, length us, event | category | flops | bytes accessed | tf_op | source)
XLA Modules:
  0.0 450.5 jit_solution(14588110167346637011)
XLA Ops:
  8.0 8.1 %all-gather.2 = f32[2,1,256]{2,1,0:T(1,128)S(1)} all-gather(f32[1,1,256]{2,1,0:T(1,128)S(1)} %convert_bitcast_fusion.1), channel_id=1, replica_groups=mesh['dp'=8,'mp'=16,'group'=2] {'group'}, dimensions={0}, use_global_device_ids=true | all-gather | bytes 3072 | tf_op jit(solution)/shard_map/all_gather | solution.py:53
  16.2 12.1 %all-gather.3 = f32[8,2,256]{2,1,0:T(2,128)S(1)} all-gather(f32[1,2,256]{2,1,0:T(2,128)S(1)} %copy.55), channel_id=2, replica_groups=mesh['dp'=8,'mp'=16,'group'=2] {'dp'}, dimensions={0}, use_global_device_ids=true | all-gather | bytes 18432 | tf_op jit(solution)/shard_map/all_gather | solution.py:54
  29.7 7.8 %gather_fusion = bf16[1024,512]{1,0:T(8,128)(2,1)} fusion(bf16[4096,512]{1,0:T(8,128)(2,1)} %param.12, s32[1024]{0:T(1024)S(1)} %broadcast_clamp_fusion), kind=kCustom, calls=%fused_computation | custom fusion | bytes 2101248 | tf_op jit(solution)/shard_map/gather | solution.py:61
  37.6 7.0 %all-to-all-start = ((bf16[16,64,512]{2,1,0:T(8,128)(2,1)}), bf16[16,64,512]{2,1,0:T(8,128)(2,1)S(1)}, u32[]{:S(2)}, u32[]{:S(2)}) async-start(bf16[16,64,512]{2,1,0:T(8,128)(2,1)} %bitcast.97), calls=%async_computation | async-start | bytes 2097152 | tf_op jit(solution)/shard_map/all_to_all | solution.py:62
  45.6 22.2 %all-to-all-done = bf16[16,64,512]{2,1,0:T(8,128)(2,1)S(1)} async-done(((bf16[16,64,512]{2,1,0:T(8,128)(2,1)}), bf16[16,64,512]{2,1,0:T(8,128)(2,1)S(1)}, u32[]{:S(2)}, u32[]{:S(2)}) %all-to-all-start) | async-done | bytes 1048608 | tf_op jit(solution)/shard_map/all_to_all | solution.py:62
  67.8 1.9 gather_fusion.1
  71.7 4.5 collective-permute-start
  76.1 14.0 %collective-permute-done = bf16[512,512]{1,0:T(8,128)(2,1)S(1)} collective-permute-done((bf16[512,512]{1,0:T(8,128)(2,1)S(1)}, bf16[512,512]{1,0:T(8,128)(2,1)S(1)}, u32[]{:S(2)}, u32[]{:S(2)}) %collective-permute-start) | collective-permute-done | bytes 524320 | tf_op jit(solution)/shard_map/ppermute | solution.py:44
  91.7 43.5 %all-gather.15.cloned.1.call-done = bf16[256,8192]{1,0:T(8,128)(2,1)} async-done(((bf16[256,512]{1,0:T(8,128)(2,1)}), bf16[256,8192]{1,0:T(8,128)(2,1)}) %all-gather.15.cloned.1.call-update) | async-done | bytes 4194320 | tf_op jit(solution)/shard_map/all_gather | solution.py:69
  135.2 55.0 %all-gather.11.cloned.1.call-done = bf16[128,8192]{1,0:T(8,128)(2,1)} async-done(((bf16[128,512]{1,0:T(8,128)(2,1)}), bf16[128,8192]{1,0:T(8,128)(2,1)}) %all-gather.11.cloned.1.call-update) | async-done | bytes 2097168 | tf_op jit(solution)/shard_map/all_gather | solution.py:39
  190.2 2.4 fusion.43
  192.6 2.1 collective-permute-start.1
  194.7 9.1 %collective-permute-done.1 = f32[128,256]{1,0:T(8,128)S(1)} collective-permute-done((f32[128,256]{1,0:T(8,128)S(1)}, f32[128,256]{1,0:T(8,128)S(1)}, u32[]{:S(2)}, u32[]{:S(2)}) %collective-permute-start.1) | collective-permute-done | bytes 131104 | tf_op jit(solution)/shard_map/ppermute | solution.py:34
  203.8 2.9 fusion.10
  206.7 37.1 %all-gather.9.cloned.1.call-done = bf16[4096,512]{1,0:T(8,128)(2,1)} async-done(((bf16[512,512]{1,0:T(8,128)(2,1)}), bf16[4096,512]{1,0:T(8,128)(2,1)}) %all-gather.9.cloned.1.call-update) | async-done | bytes 4194320 | tf_op jit(solution)/shard_map/all_gather | solution.py:43
  243.8 2.9 fusion.30
  247.1 1.6 collective-permute-start.3
  248.7 2.9 fusion.12
  251.6 2.4 fusion.25
  254.2 4.5 %collective-permute-start.2 = (f32[2,64,2,128]{3,1,2,0:T(8,128)S(1)}, f32[2,64,2,128]{3,1,2,0:T(8,128)S(1)}, u32[]{:S(2)}, u32[]{:S(2)}) collective-permute-start(f32[2,64,2,128]{3,1,2,0:T(8,128)S(1)} %convolution_bitcast_fusion.1), channel_id=1, source_target_pairs={{0,1},{1,0},{2,3},{3,2},{4,5},{5,4},{6,7},{7,6},{8,9},{9,8},{10,11... | collective-permute-start | bytes 393224 | tf_op jit(solution)/shard_map/ppermute | solution.py:34
  258.7 41.6 %all-gather.13.cloned.1.call-done = bf16[128,8192]{1,0:T(8,128)(2,1)} async-done(((bf16[128,512]{1,0:T(8,128)(2,1)}), bf16[128,8192]{1,0:T(8,128)(2,1)}) %all-gather.13.cloned.1.call-update) | async-done | bytes 2097168 | tf_op jit(solution)/shard_map/all_gather | solution.py:71
  300.3 2.1 fusion.41
  302.4 2.1 collective-permute-start.4
  304.5 9.1 %collective-permute-done.4 = f32[128,256]{1,0:T(8,128)S(1)} collective-permute-done((f32[128,256]{1,0:T(8,128)S(1)}, f32[128,256]{1,0:T(8,128)S(1)}, u32[]{:S(2)}, u32[]{:S(2)}) %collective-permute-start.4) | collective-permute-done | bytes 131104 | tf_op jit(solution)/shard_map/ppermute | solution.py:34
  315.0 2.5 fusion.50
  317.5 2.3 collective-permute-start.5
  320.6 1.4 copy-done.4
  325.1 1.5 collective-permute-done.5
  328.4 3.5 pad_maximum_fusion
  332.0 91.5 %reduce-scatter.2.cloned.1.call-done = bf16[512,512]{1,0:T(8,128)(2,1)} async-done(((bf16[512,8192]{1,0:T(8,128)(2,1)}), bf16[512,512]{1,0:T(8,128)(2,1)}) %reduce-scatter.2.cloned.1.call-update) | async-done | bytes 524304 | tf_op jit(solution)/shard_map/reduce_scatter | solution.py:155
  424.5 2.1 collective-permute-start.6
  426.5 14.0 %collective-permute-done.6 = bf16[256,512]{1,0:T(8,128)(2,1)S(1)} collective-permute-done((bf16[256,512]{1,0:T(8,128)(2,1)S(1)}, bf16[256,512]{1,0:T(8,128)(2,1)S(1)}, u32[]{:S(2)}, u32[]{:S(2)}) %collective-permute-start.6) | collective-permute-done | bytes 262176 | tf_op jit(solution)/shard_map/ppermute | solution.py:157
  (95 shorter events, 18.7 us)
Async XLA Ops:
  7.2 293.2 %copy-start = (bf16[256,4096]{1,0:T(8,128)(2,1)S(1)}, bf16[256,4096]{1,0:T(8,128)(2,1)}, u32[]{:S(2)}) copy-start(bf16[256,4096]{1,0:T(8,128)(2,1)} %param.16) | copy-start | bytes 6291460
  37.6 7.1 %copy-start.8 = (s32[2,1,128]{2,1,0:T(1,128)S(1)}, s32[2,1,128]{2,1,0:T(1,128)}, u32[]{:S(2)}) copy-start(s32[2,1,128]{2,1,0:T(1,128)} %param.10) | copy-start | bytes 3076
  37.6 32.2 %copy-start.6 = (bf16[128,512]{1,0:T(8,128)(2,1)S(1)}, bf16[128,512]{1,0:T(8,128)(2,1)}, u32[]{:S(2)}) copy-start(bf16[128,512]{1,0:T(8,128)(2,1)} %param.9) | copy-start | bytes 393220
  37.6 30.3 %all-to-all-start = ((bf16[16,64,512]{2,1,0:T(8,128)(2,1)}), bf16[16,64,512]{2,1,0:T(8,128)(2,1)S(1)}, u32[]{:S(2)}, u32[]{:S(2)}) async-start(bf16[16,64,512]{2,1,0:T(8,128)(2,1)} %bitcast.97), calls=%async_computation | async-start | bytes 2097152 | tf_op jit(solution)/shard_map/all_to_all | solution.py:62
  44.6 90.6 %all-gather.15.cloned.1.call-start = ((), (), s32[]{:S(2)}) async-start(), calls=%async_computation.6 | async-start | bytes 4456448 | tf_op jit(solution)/shard_map/all_gather | solution.py:69
  69.7 120.5 %all-gather.11.cloned.1.call-start = ((), (), s32[]{:S(2)}) async-start(), calls=%async_computation.3 | async-start | bytes 2228224 | tf_op jit(solution)/shard_map/all_gather | solution.py:39
  70.5 173.3 %all-gather.9.cloned.1.call-start = ((), (), s32[]{:S(2)}) async-start(), calls=%async_computation.2 | async-start | bytes 4718592 | tf_op jit(solution)/shard_map/all_gather | solution.py:43
  70.5 20.4 %copy-start.7 = (bf16[128,512]{1,0:T(8,128)(2,1)S(1)}, bf16[128,512]{1,0:T(8,128)(2,1)}, u32[]{:S(2)}) copy-start(bf16[128,512]{1,0:T(8,128)(2,1)} %param.17) | copy-start | bytes 393220
  71.7 18.4 %collective-permute-start = (bf16[512,512]{1,0:T(8,128)(2,1)S(1)}, bf16[512,512]{1,0:T(8,128)(2,1)S(1)}, u32[]{:S(2)}, u32[]{:S(2)}) collective-permute-start(bf16[512,512]{1,0:T(8,128)(2,1)S(1)} %fusion.46), channel_id=1, source_target_pairs={{0,1},{1,0},{2,3},{3,2},{4,5},{5,4},{6,7},{7,6},{8,9},{9,8},{10,11... | collective-permute-start | bytes 1572872 | tf_op jit(solution)/shard_map/ppermute | solution.py:44
  90.1 0.8 copy-start.5
  90.1 104.6 %copy-start.9 = (s32[2]{0:T(128)S(1)}, s32[2]{0:T(128)}, u32[]{:S(2)}) copy-start(s32[2]{0:T(128)} %param.11) | copy-start | bytes 28
  90.9 209.4 %all-gather.13.cloned.1.call-start = ((), (), s32[]{:S(2)}) async-start(), calls=%async_computation.4 | async-start | bytes 2228224 | tf_op jit(solution)/shard_map/all_gather | solution.py:71
  135.1 288.3 %reduce-scatter.2.cloned.1.call-start = ((), (), s32[]{:S(2)}) async-start(), calls=%async_computation.5 | async-start | bytes 8912896 | tf_op jit(solution)/shard_map/reduce_scatter | solution.py:155
  192.6 11.2 %collective-permute-start.1 = (f32[128,256]{1,0:T(8,128)S(1)}, f32[128,256]{1,0:T(8,128)S(1)}, u32[]{:S(2)}, u32[]{:S(2)}) collective-permute-start(f32[128,256]{1,0:T(8,128)S(1)} %fusion.43), channel_id=1, source_target_pairs={{0,1},{1,0},{2,3},{3,2},{4,5},{5,4},{6,7},{7,6},{8,9},{9,8},{10,11... | collective-permute-start | bytes 393224 | tf_op jit(solution)/shard_map/ppermute | solution.py:34
  247.1 4.5 %copy-start.3 = (bf16[4096,512]{1,0:T(8,128)(2,1)S(1)}, bf16[4096,512]{1,0:T(8,128)(2,1)}, u32[]{:S(2)}) copy-start(bf16[4096,512]{1,0:T(8,128)(2,1)} %all-gather.9.cloned.1.call-done) | copy-start | bytes 12582916
  247.1 57.4 %collective-permute-start.3 = (f32[2,2,64]{2,1,0:T(2,128)S(1)}, f32[2,2,64]{2,1,0:T(2,128)S(1)}, u32[]{:S(2)}, u32[]{:S(2)}) collective-permute-start(f32[2,2,64]{2,1,0:T(2,128)S(1)} %get-tuple-element.27), channel_id=1, source_target_pairs={{0,1},{1,0},{2,3},{3,2},{4,5},{5,4},{6,7},{7,6},{8,9},{9,8},{10,11... | collective-permute-start | bytes 3080 | tf_op jit(solution)/shard_map/ppermute | solution.py:34
  254.2 59.7 %collective-permute-start.2 = (f32[2,64,2,128]{3,1,2,0:T(8,128)S(1)}, f32[2,64,2,128]{3,1,2,0:T(8,128)S(1)}, u32[]{:S(2)}, u32[]{:S(2)}) collective-permute-start(f32[2,64,2,128]{3,1,2,0:T(8,128)S(1)} %convolution_bitcast_fusion.1), channel_id=1, source_target_pairs={{0,1},{1,0},{2,3},{3,2},{4,5},{5,4},{6,7},{7,6},{8,9},{9,8},{10,11... | collective-permute-start | bytes 393224 | tf_op jit(solution)/shard_map/ppermute | solution.py:34
  302.4 11.2 %collective-permute-start.4 = (f32[128,256]{1,0:T(8,128)S(1)}, f32[128,256]{1,0:T(8,128)S(1)}, u32[]{:S(2)}, u32[]{:S(2)}) collective-permute-start(f32[128,256]{1,0:T(8,128)S(1)} %fusion.41), channel_id=1, source_target_pairs={{0,1},{1,0},{2,3},{3,2},{4,5},{5,4},{6,7},{7,6},{8,9},{9,8},{10,11... | collective-permute-start | bytes 393224 | tf_op jit(solution)/shard_map/ppermute | solution.py:34
  315.0 4.9 %copy-start.1 = (bf16[4096,256]{1,0:T(8,128)(2,1)S(1)}, bf16[4096,256]{1,0:T(8,128)(2,1)}, u32[]{:S(2)}) copy-start(bf16[4096,256]{1,0:T(8,128)(2,1)} %param.15) | copy-start | bytes 6291460
  317.5 9.1 %collective-permute-start.5 = (f32[2,64,2,128]{3,1,2,0:T(8,128)S(1)}, f32[2,64,2,128]{3,1,2,0:T(8,128)S(1)}, u32[]{:S(2)}, u32[]{:S(2)}) collective-permute-start(f32[2,64,2,128]{3,1,2,0:T(8,128)S(1)} %convolution_bitcast_fusion), channel_id=1, source_target_pairs={{0,1},{1,0},{2,3},{3,2},{4,5},{5,4},{6,7},{7,6},{8,9},{9,8},{10,11... | collective-permute-start | bytes 393224 | tf_op jit(solution)/shard_map/ppermute | solution.py:34
  319.9 2.2 copy-start.4
  324.7 2.1 copy-start.2
  424.5 16.1 %collective-permute-start.6 = (bf16[256,512]{1,0:T(8,128)(2,1)S(1)}, bf16[256,512]{1,0:T(8,128)(2,1)S(1)}, u32[]{:S(2)}, u32[]{:S(2)}) collective-permute-start(bf16[256,512]{1,0:T(8,128)(2,1)S(1)} %slice.60), channel_id=1, source_target_pairs={{0,1},{1,0},{2,3},{3,2},{4,5},{5,4},{6,7},{7,6},{8,9},{9,8},{10,11... | collective-permute-start | bytes 786440 | tf_op jit(solution)/shard_map/ppermute | solution.py:157
Sparse Core Ops, SparseCore 0:
  69.8 65.2 all-gather.14
  138.1 52.0 all-gather.10
  192.6 51.1 all-gather.8
  246.1 54.2 all-gather.12
  332.1 91.3 reduce-scatter.1

commit v6 on v5

--- a/solution.py
+++ b/solution.py
@@ -1,8 +1,11 @@
+import functools
 import math
 
 import jax
 import jax.numpy as jnp
 from jax import lax
+from jax.experimental import pallas as pl
+from jax.experimental.pallas import tpu as pltpu
 from jax.sharding import PartitionSpec as P
 
 HD = 128
@@ -16,8 +19,85 @@
     )
 
 
+MESH = pl.DeviceIdType.MESH
+
+
+def _half_rows_kernel(n_mp, rows_ref, out_ref, held, send_sem, recv_sem):
+    me_dp = lax.axis_index("dp")
+    me_mp = lax.axis_index("mp")
+    me_group = lax.axis_index("group")
+    half_blocks = n_mp // 2
+    barrier = pltpu.get_barrier_semaphore()
+    for off in range(1, n_mp):
+        peer = lax.rem(me_mp + off, n_mp)
+        pl.semaphore_signal(
+            barrier, inc=1, device_id=(me_dp, peer, me_group), device_id_type=MESH
+        )
+    pl.semaphore_wait(barrier, n_mp - 1)
+    slot = lax.rem(me_mp, half_blocks)
+    sender = lax.div(me_mp, half_blocks) == me_group
+
+    def copy_to(off):
+        return pltpu.make_async_remote_copy(
+            src_ref=rows_ref,
+            dst_ref=held.at[slot],
+            send_sem=send_sem.at[off - 1],
+            recv_sem=recv_sem.at[slot],
+            device_id=(me_dp, lax.rem(me_mp + off, n_mp), me_group),
+            device_id_type=MESH,
+        )
+
+    @pl.when(sender)
+    def _():
+        for off in range(1, n_mp):
+            copy_to(off).start()
+        held[slot] = rows_ref[...]
+
+    for s in range(half_blocks):
+        source = half_blocks * me_group + s
+
+        @pl.when(source != me_mp)
+        def _():
+            pltpu.make_async_remote_copy(
+                src_ref=rows_ref,
+                dst_ref=held.at[s],
+                send_sem=send_sem.at[0],
+                recv_sem=recv_sem.at[s],
+                device_id=(me_dp, source, me_group),
+                device_id_type=MESH,
+            ).wait_recv()
+
+    @pl.when(sender)
+    def _():
+        for off in range(1, n_mp):
+            copy_to(off).wait_send()
+
+    out_ref[...] = held[...]
+
+
+def half_rows_exchange(rows, n_mp):
+    half_blocks = n_mp // 2
+    shape = (half_blocks,) + rows.shape
+    moved = rows.size * rows.dtype.itemsize * (n_mp - 1)
+    return pl.pallas_call(
+        functools.partial(_half_rows_kernel, n_mp),
+        out_shape=jax.ShapeDtypeStruct(shape, rows.dtype),
+        in_specs=[pl.BlockSpec(memory_space=pltpu.VMEM)],
+        out_specs=pl.BlockSpec(memory_space=pltpu.VMEM),
+        scratch_shapes=[
+            pltpu.VMEM(shape, rows.dtype),
+            pltpu.SemaphoreType.DMA((n_mp - 1,)),
+            pltpu.SemaphoreType.DMA((half_blocks,)),
+        ],
+        compiler_params=pltpu.CompilerParams(collective_id=0, has_side_effects=True),
+        cost_estimate=pl.CostEstimate(
+            flops=0, transcendentals=0, bytes_accessed=moved
+        ),
+    )(rows)
+
+
 def per_device(
-    hidden, neighbour_ids, counts, embed_table, w_query, w_key, w_value, w_out, grad_out
+    hidden, neighbour_ids, counts, embed_table, w_query, w_key, w_value, w_out, grad_out, n_mp
 ):
     tail_rows = BLOCK - 1
     rows_here = hidden.shape[0]
@@ -36,7 +116,9 @@
     pad_rows = jnp.zeros((tail_rows, hidden.shape[1]), jnp.bfloat16)
     query_rows = jnp.concatenate([hidden[tail_rows:], pad_rows], 0)
     grad_rows = jnp.concatenate([grad_out[tail_rows:], pad_rows], 0)
-    full_query = lax.all_gather(query_rows, "mp", axis=1, tiled=True)
+    halves = half_rows_exchange(jnp.stack([query_rows, grad_rows]), n_mp)
+    halves = jnp.transpose(halves, (1, 2, 0, 3)).reshape(2, rows_here, half)
+    query_half, grad_half = halves[0], halves[1]
     piece_rows = half // lax.axis_size("dp")
     kv_local = jnp.concatenate([w_key, w_value], axis=1)
     kv_piece = lax.dynamic_slice_in_dim(kv_local, me_dp * piece_rows, piece_rows, 0)
@@ -67,8 +149,6 @@
     ) - 1
     own_cols = recv_buf.reshape(owners * cap, -1)[own_owner * cap + own_rank]
     neighbours = lax.all_gather(own_cols, "mp", axis=1, tiled=True)
-    grad_rows, neighbours = lax.optimization_barrier((grad_rows, neighbours))
-    full_grad = lax.all_gather(grad_rows, "mp", axis=1, tiled=True)
 
     def this_half(x):
         return lax.dynamic_slice_in_dim(x, me_group * half, half, 1)
@@ -76,7 +156,7 @@
     def other_half(x):
         return lax.dynamic_slice_in_dim(x, (1 - me_group) * half, half, 1)
 
-    query_part = jnp.dot(this_half(full_query), w_query, preferred_element_type=jnp.float32)
+    query_part = jnp.dot(query_half, w_query, preferred_element_type=jnp.float32)
     query = group_sum(query_part).astype(jnp.bfloat16)
     n_here, n_there = this_half(neighbours), other_half(neighbours)
     keys = (
@@ -115,7 +195,7 @@
         )
 
     out_term = jnp.dot(attn_bf, w_out, preferred_element_type=jnp.float32)
-    d_attn_part = contract(this_half(full_grad), w_out)
+    d_attn_part = contract(grad_half, w_out)
     d_attn = group_sum(d_attn_part).astype(jnp.bfloat16)
     d_block = d_attn.reshape(blocks_here, BLOCK, heads_here, HD)
     prob = weights / total[..., None]
@@ -166,7 +246,7 @@
 
 def solution(mesh):
     return jax.shard_map(
-        per_device,
+        functools.partial(per_device, n_mp=mesh.shape["mp"]),
         mesh=mesh,
         in_specs=(
             P("dp", "mp"),

time: 453 us -> 406 us (0.90)
  waiting for transfers between devices: 339 us -> 220 us
  Pallas kernels: 0 us -> 50.1 us
  starting transfers between devices: 26.3 us -> 37.2 us
  local copies, waits for them, and re-layouts: 16.7 us -> 23.8 us
    all_gather x2 -> x0, waiting for transfers between devices: 96.7 us -> none  [the longest x1 55 us: per_device(): full_query = lax.all_gather(query_rows, 'mp', axis=1, tiled=True)]
    pallas_call x0 -> x1, Pallas kernels: none -> 50.1 us  [half_rows_exchange(): pl.pallas_call(functools.partial(_half_rows_kernel, n_mp), out_shape=jax....]
    all_gather x1, waiting for transfers between devices: 43.5 us -> 0.02 us  [per_device(): neighbours = lax.all_gather(own_cols, 'mp', axis=1, tiled=True)]
    all_gather x1, waiting for transfers between devices: 37.1 us -> 54.9 us  [per_device(): lax.all_gather(lax.ppermute(kv_piece, 'group', swap), 'dp', axis=0, tiled...]
    ppermute x5, starting transfers between devices: 12.5 us -> 23.5 us  [group_sum(): return x + lax.ppermute(x, 'group', swap)]
    reduce_scatter x1, waiting for transfers between devices: 91.5 us -> 99.8 us  [per_device(): reduced = lax.psum_scatter(stacked, 'mp', scatter_dimension=1, tiled=True)]
    slice x1 -> x4, local copies, waits for them, and re-layouts: 0.18 us -> 6.45 us  [the longest x3 6.27 us: per_device(): query_half, grad_half = (halves[0], halves[1])]
    ppermute x5, waiting for transfers between devices: 19.7 us -> 14.8 us  [group_sum(): return x + lax.ppermute(x, 'group', swap)]
  transfers between devices with their start and end apart: 13 -> 11, of which waited for: 11 -> 9; matrix products, arithmetic and copies ran while one was open for 5% -> 6% of each run, Pallas kernels for 0% -> 12%
where the time goes in v6:
time: 406 us; the launch traced here: 403 us
  waiting for transfers between devices  220 us (54%)
  Pallas kernels  50.1 us (12%)
  starting transfers between devices  37.2 us (9%)
  matrix products  25.2 us (6%)
  local copies, waits for them, and re-layouts  23.8 us (6%)
  blocking collectives  20.3 us (5%)
  between operations  14.2 us (3%)
  other arithmetic  12.3 us (3%)
    reduce_scatter x1, waiting for transfers between devices, per_device(): reduced = lax.psum_scatter(stacked, 'mp', scatter_dimension=1, tiled=True)  99.8 us
    all_gather x1, waiting for transfers between devices, per_device(): lax.all_gather(lax.ppermute(kv_piece, 'group', swap), 'dp', axis=0, tiled...  54.9 us
    pallas_call x1, Pallas kernels, half_rows_exchange(): pl.pallas_call(functools.partial(_half_rows_kernel, n_mp), out_shape=jax....  50.1 us
    ppermute x5, starting transfers between devices, group_sum(): return x + lax.ppermute(x, 'group', swap)  23.5 us
    all_to_all x1, waiting for transfers between devices, per_device(): recv_buf = lax.all_to_all(send_buf, ('dp', 'group'), 0, 0, tiled=True)  22.2 us
    ppermute x5, waiting for transfers between devices, group_sum(): return x + lax.ppermute(x, 'group', swap)  14.8 us
    ppermute x1, waiting for transfers between devices, per_device(): lax.ppermute(both_cols, 'group', swap)  14 us
    ppermute x1, waiting for transfers between devices, per_device(): lax.ppermute(kv_piece, 'group', swap)  14 us
  transfers between devices with their start and end apart: 11, of which 9 were waited for; matrix products, arithmetic and copies ran while one was open for 6% of the time, Pallas kernels for 12%

profile of v6, /device:TPU:192, one launch (start us, length us, event | category | flops | bytes accessed | tf_op | source)
XLA Modules:
  0.0 403.1 jit_solution(17252670038885433781)
XLA Ops:
  8.0 8.1 %all-gather.2 = f32[2,1,256]{2,1,0:T(1,128)S(1)} all-gather(f32[1,1,256]{2,1,0:T(1,128)S(1)} %convert_bitcast_fusion.1), channel_id=1, replica_groups=mesh['dp'=8,'mp'=16,'group'=2] {'group'}, dimensions={0}, use_global_device_ids=true | all-gather | bytes 3072 | tf_op jit(solution)/shard_map/all_gather | solution.py:135
  16.2 12.1 %all-gather.3 = f32[8,2,256]{2,1,0:T(2,128)S(1)} all-gather(f32[1,2,256]{2,1,0:T(2,128)S(1)} %copy.59), channel_id=2, replica_groups=mesh['dp'=8,'mp'=16,'group'=2] {'dp'}, dimensions={0}, use_global_device_ids=true | all-gather | bytes 18432 | tf_op jit(solution)/shard_map/all_gather | solution.py:136
  29.7 7.8 %gather_fusion = bf16[1024,512]{1,0:T(8,128)(2,1)} fusion(bf16[4096,512]{1,0:T(8,128)(2,1)} %param.12, s32[1024]{0:T(1024)S(1)} %broadcast_clamp_fusion), kind=kCustom, calls=%fused_computation | custom fusion | bytes 2101248 | tf_op jit(solution)/shard_map/gather | solution.py:143
  37.5 7.0 %all-to-all-start = ((bf16[16,64,512]{2,1,0:T(8,128)(2,1)}), bf16[16,64,512]{2,1,0:T(8,128)(2,1)S(1)}, u32[]{:S(2)}, u32[]{:S(2)}) async-start(bf16[16,64,512]{2,1,0:T(8,128)(2,1)} %bitcast.107), calls=%async_computation | async-start | bytes 2097152 | tf_op jit(solution)/shard_map/all_to_all | solution.py:144
  45.6 22.2 %all-to-all-done = bf16[16,64,512]{2,1,0:T(8,128)(2,1)S(1)} async-done(((bf16[16,64,512]{2,1,0:T(8,128)(2,1)}), bf16[16,64,512]{2,1,0:T(8,128)(2,1)S(1)}, u32[]{:S(2)}, u32[]{:S(2)}) %all-to-all-start) | async-done | bytes 1048608 | tf_op jit(solution)/shard_map/all_to_all | solution.py:144
  67.8 1.9 gather_fusion.1
  70.9 4.5 %collective-permute-start = (bf16[512,512]{1,0:T(8,128)(2,1)S(1)}, bf16[512,512]{1,0:T(8,128)(2,1)S(1)}, u32[]{:S(2)}, u32[]{:S(2)}) collective-permute-start(bf16[512,512]{1,0:T(8,128)(2,1)S(1)} %fusion.42), channel_id=1, source_target_pairs={{0,1},{1,0},{2,3},{3,2},{4,5},{5,4},{6,7},{7,6},{8,9},{9,8},{10,11... | collective-permute-start | bytes 1572872 | tf_op jit(solution)/shard_map/ppermute | solution.py:126
  75.4 14.0 %collective-permute-done = bf16[512,512]{1,0:T(8,128)(2,1)S(1)} collective-permute-done((bf16[512,512]{1,0:T(8,128)(2,1)S(1)}, bf16[512,512]{1,0:T(8,128)(2,1)S(1)}, u32[]{:S(2)}, u32[]{:S(2)}) %collective-permute-start) | collective-permute-done | bytes 524320 | tf_op jit(solution)/shard_map/ppermute | solution.py:126
  91.0 50.1 %shard_map.112 = bf16[8,2,128,512]{3,2,1,0:T(8,128)(2,1)} custom-call(bf16[2,128,512]{2,1,0:T(8,128)(2,1)} %pad_maximum_fusion.1.rows_ref), custom_call_target="tpu_custom_call" | custom-call | bytes 3932160 | tf_op jit(solution)/shard_map/pallas_call | solution.py:82
  141.2 3.0 fusion.74
  144.2 1.6 copy.63
  145.8 2.2 fusion.78
  148.0 15.9 %collective-permute-start.1 = (f32[128,256]{1,0:T(8,128)S(1)}, f32[128,256]{1,0:T(8,128)S(1)}, u32[]{:S(2)}, u32[]{:S(2)}) collective-permute-start(f32[128,256]{1,0:T(8,128)S(1)} %fusion.78), channel_id=1, source_target_pairs={{0,1},{1,0},{2,3},{3,2},{4,5},{5,4},{6,7},{7,6},{8,9},{9,8},{10,11... | collective-permute-start | bytes 393224 | tf_op jit(solution)/shard_map/ppermute | solution.py:114
  164.0 1.6 copy.68
  167.2 8.2 %collective-permute-done.4 = f32[128,256]{1,0:T(8,128)S(1)} collective-permute-done((f32[128,256]{1,0:T(8,128)S(1)}, f32[128,256]{1,0:T(8,128)S(1)}, u32[]{:S(2)}, u32[]{:S(2)}) %collective-permute-start.4) | collective-permute-done | bytes 131104 | tf_op jit(solution)/shard_map/ppermute | solution.py:114
  175.5 2.9 fusion.10
  178.4 54.9 %all-gather.7.cloned.1.call-done = bf16[4096,512]{1,0:T(8,128)(2,1)} async-done(((bf16[512,512]{1,0:T(8,128)(2,1)}), bf16[4096,512]{1,0:T(8,128)(2,1)}) %all-gather.7.cloned.1.call-update) | async-done | bytes 4194320 | tf_op jit(solution)/shard_map/all_gather | solution.py:125
  233.4 2.9 fusion.30
  236.3 3.1 fusion.12
  239.8 2.4 fusion.25
  242.5 5.0 %collective-permute-start.3 = (f32[2,2,64]{2,1,0:T(2,128)S(1)}, f32[2,2,64]{2,1,0:T(2,128)S(1)}, u32[]{:S(2)}, u32[]{:S(2)}) collective-permute-start(f32[2,2,64]{2,1,0:T(2,128)S(1)} %get-tuple-element.25), channel_id=1, source_target_pairs={{0,1},{1,0},{2,3},{3,2},{4,5},{5,4},{6,7},{7,6},{8,9},{9,8},{10,11... | collective-permute-start | bytes 3080 | tf_op jit(solution)/shard_map/ppermute | solution.py:114
  247.7 1.2 collective-permute-start.2
  248.9 1.1 collective-permute-done.3
  250.5 4.3 %fusion.1 = f32[256,4096]{1,0:T(8,128)} fusion(bf16[4096,512]{1,0:T(8,128)(2,1)} %all-gather.7.cloned.1.call-done, bf16[32,8,2,128]{3,2,1,0:T(2,128)(2,1)S(1)} %bitcast.110), kind=kOutput, calls=%fused_computation.13 | convolution fusion | flops 536870912 | bytes 6422528 | tf_op jit(solution)/shard_map/dot_general | solution.py:17
  254.8 4.9 %collective-permute-done.2 = f32[2,64,2,128]{3,1,2,0:T(8,128)S(1)} collective-permute-done((f32[2,64,2,128]{3,1,2,0:T(8,128)S(1)}, f32[2,64,2,128]{3,1,2,0:T(8,128)S(1)}, u32[]{:S(2)}, u32[]{:S(2)}) %collective-permute-start.2) | collective-permute-done | bytes 131104 | tf_op jit(solution)/shard_map/ppermute | solution.py:114
  260.5 1.2 collective-permute-start.5
  261.8 2.5 fusion.46
  266.5 1.3 copy-done.5
  272.4 3.8 pad_maximum_fusion
  276.2 99.8 %reduce-scatter.2.cloned.1.call-done = bf16[512,512]{1,0:T(8,128)(2,1)} async-done(((bf16[512,8192]{1,0:T(8,128)(2,1)}), bf16[512,512]{1,0:T(8,128)(2,1)}) %reduce-scatter.2.cloned.1.call-update) | async-done | bytes 524304 | tf_op jit(solution)/shard_map/reduce_scatter | solution.py:235
  377.0 2.1 collective-permute-start.6
  379.1 14.0 %collective-permute-done.6 = bf16[256,512]{1,0:T(8,128)(2,1)S(1)} collective-permute-done((bf16[256,512]{1,0:T(8,128)(2,1)S(1)}, bf16[256,512]{1,0:T(8,128)(2,1)S(1)}, u32[]{:S(2)}, u32[]{:S(2)}) %collective-permute-start.6) | collective-permute-done | bytes 262176 | tf_op jit(solution)/shard_map/ppermute | solution.py:237
  (96 shorter events, 21.0 us)
Async XLA Ops:
  7.2 158.4 %copy-start = (bf16[256,4096]{1,0:T(8,128)(2,1)S(1)}, bf16[256,4096]{1,0:T(8,128)(2,1)}, u32[]{:S(2)}) copy-start(bf16[256,4096]{1,0:T(8,128)(2,1)} %param.16) | copy-start | bytes 6291460
  37.5 7.0 %copy-start.9 = (s32[2,1,128]{2,1,0:T(1,128)S(1)}, s32[2,1,128]{2,1,0:T(1,128)}, u32[]{:S(2)}) copy-start(s32[2,1,128]{2,1,0:T(1,128)} %param.10) | copy-start | bytes 3076
  37.5 30.3 %all-to-all-start = ((bf16[16,64,512]{2,1,0:T(8,128)(2,1)}), bf16[16,64,512]{2,1,0:T(8,128)(2,1)S(1)}, u32[]{:S(2)}, u32[]{:S(2)}) async-start(bf16[16,64,512]{2,1,0:T(8,128)(2,1)} %bitcast.107), calls=%async_computation | async-start | bytes 2097152 | tf_op jit(solution)/shard_map/all_to_all | solution.py:144
  44.5 130.9 %all-gather.9.cloned.1.call-start = ((), (), s32[]{:S(2)}) async-start(), calls=%async_computation.4 | async-start | bytes 4456448 | tf_op jit(solution)/shard_map/all_gather | solution.py:151
  69.7 163.7 %all-gather.7.cloned.1.call-start = ((), (), s32[]{:S(2)}) async-start(), calls=%async_computation.2 | async-start | bytes 4718592 | tf_op jit(solution)/shard_map/all_gather | solution.py:125
  69.7 20.5 %copy-start.7 = (bf16[128,512]{1,0:T(8,128)(2,1)S(1)}, bf16[128,512]{1,0:T(8,128)(2,1)}, u32[]{:S(2)}) copy-start(bf16[128,512]{1,0:T(8,128)(2,1)} %param.9) | copy-start | bytes 393220
  69.8 20.5 %copy-start.8 = (bf16[128,512]{1,0:T(8,128)(2,1)S(1)}, bf16[128,512]{1,0:T(8,128)(2,1)}, u32[]{:S(2)}) copy-start(bf16[128,512]{1,0:T(8,128)(2,1)} %param.17) | copy-start | bytes 393220
  70.9 18.4 %collective-permute-start = (bf16[512,512]{1,0:T(8,128)(2,1)S(1)}, bf16[512,512]{1,0:T(8,128)(2,1)S(1)}, u32[]{:S(2)}, u32[]{:S(2)}) collective-permute-start(bf16[512,512]{1,0:T(8,128)(2,1)S(1)} %fusion.42), channel_id=1, source_target_pairs={{0,1},{1,0},{2,3},{3,2},{4,5},{5,4},{6,7},{7,6},{8,9},{9,8},{10,11... | collective-permute-start | bytes 1572872 | tf_op jit(solution)/shard_map/ppermute | solution.py:126
  89.3 0.8 copy-start.6
  90.2 285.9 %reduce-scatter.2.cloned.1.call-start = ((), (), s32[]{:S(2)}) async-start(), calls=%async_computation.3 | async-start | bytes 8912896 | tf_op jit(solution)/shard_map/reduce_scatter | solution.py:235
  148.0 19.2 %collective-permute-start.1 = (f32[128,256]{1,0:T(8,128)S(1)}, f32[128,256]{1,0:T(8,128)S(1)}, u32[]{:S(2)}, u32[]{:S(2)}) collective-permute-start(f32[128,256]{1,0:T(8,128)S(1)} %fusion.78), channel_id=1, source_target_pairs={{0,1},{1,0},{2,3},{3,2},{4,5},{5,4},{6,7},{7,6},{8,9},{9,8},{10,11... | collective-permute-start | bytes 393224 | tf_op jit(solution)/shard_map/ppermute | solution.py:114
  165.6 1.0 copy-start.10
  166.4 9.0 %collective-permute-start.4 = (f32[128,256]{1,0:T(8,128)S(1)}, f32[128,256]{1,0:T(8,128)S(1)}, u32[]{:S(2)}, u32[]{:S(2)}) collective-permute-start(f32[128,256]{1,0:T(8,128)S(1)} %fusion.79), channel_id=1, source_target_pairs={{0,1},{1,0},{2,3},{3,2},{4,5},{5,4},{6,7},{7,6},{8,9},{9,8},{10,11... | collective-permute-start | bytes 393224 | tf_op jit(solution)/shard_map/ppermute | solution.py:114
  236.3 3.5 copy-start.4
  242.5 7.6 %collective-permute-start.3 = (f32[2,2,64]{2,1,0:T(2,128)S(1)}, f32[2,2,64]{2,1,0:T(2,128)S(1)}, u32[]{:S(2)}, u32[]{:S(2)}) collective-permute-start(f32[2,2,64]{2,1,0:T(2,128)S(1)} %get-tuple-element.25), channel_id=1, source_target_pairs={{0,1},{1,0},{2,3},{3,2},{4,5},{5,4},{6,7},{7,6},{8,9},{9,8},{10,11... | collective-permute-start | bytes 3080 | tf_op jit(solution)/shard_map/ppermute | solution.py:114
  247.7 12.0 %collective-permute-start.2 = (f32[2,64,2,128]{3,1,2,0:T(8,128)S(1)}, f32[2,64,2,128]{3,1,2,0:T(8,128)S(1)}, u32[]{:S(2)}, u32[]{:S(2)}) collective-permute-start(f32[2,64,2,128]{3,1,2,0:T(8,128)S(1)} %convolution_bitcast_fusion.1), channel_id=1, source_target_pairs={{0,1},{1,0},{2,3},{3,2},{4,5},{5,4},{6,7},{7,6},{8,9},{9,8},{10,11... | collective-permute-start | bytes 393224 | tf_op jit(solution)/shard_map/ppermute | solution.py:114
  260.5 9.5 %collective-permute-start.5 = (f32[2,64,2,128]{3,1,2,0:T(8,128)S(1)}, f32[2,64,2,128]{3,1,2,0:T(8,128)S(1)}, u32[]{:S(2)}, u32[]{:S(2)}) collective-permute-start(f32[2,64,2,128]{3,1,2,0:T(8,128)S(1)} %convolution_bitcast_fusion), channel_id=1, source_target_pairs={{0,1},{1,0},{2,3},{3,2},{4,5},{5,4},{6,7},{7,6},{8,9},{9,8},{10,11... | collective-permute-start | bytes 393224 | tf_op jit(solution)/shard_map/ppermute | solution.py:114
  261.8 2.5 copy-start.1
  264.3 2.2 copy-start.2
  264.3 3.5 copy-start.5
  269.6 1.6 copy-start.3
  377.0 16.1 %collective-permute-start.6 = (bf16[256,512]{1,0:T(8,128)(2,1)S(1)}, bf16[256,512]{1,0:T(8,128)(2,1)S(1)}, u32[]{:S(2)}, u32[]{:S(2)}) collective-permute-start(bf16[256,512]{1,0:T(8,128)(2,1)S(1)} %slice.72), channel_id=1, source_target_pairs={{0,1},{1,0},{2,3},{3,2},{4,5},{5,4},{6,7},{7,6},{8,9},{9,8},{10,11... | collective-permute-start | bytes 786440 | tf_op jit(solution)/shard_map/ppermute | solution.py:237
Sparse Core Ops, SparseCore 0:
  69.8 101.3 all-gather.8
  173.6 59.6 all-gather.6
  276.3 99.6 reduce-scatter.1

commit v7 on v3

--- a/solution.py
+++ b/solution.py
@@ -1,8 +1,11 @@
+import functools
 import math
 
 import jax
 import jax.numpy as jnp
 from jax import lax
+from jax.experimental import pallas as pl
+from jax.experimental.pallas import tpu as pltpu
 from jax.sharding import PartitionSpec as P
 
 HD = 128
@@ -16,8 +19,120 @@
     )
 
 
+MESH = pl.DeviceIdType.MESH
+
+
+def _other_half_kernel(n_dp, own_ref, out_ref, send_sem, recv_sem):
+    me_dp = lax.axis_index("dp")
+    me_mp = lax.axis_index("mp")
+    me_group = lax.axis_index("group")
+    chips = n_dp // 2
+    ring = 2 * chips
+    z_lo = lax.div(me_dp, 2)
+    core = lax.rem(me_dp, 2)
+    z = me_group * chips + z_lo
+    z_next = lax.rem(z + 1, ring)
+    z_prev = lax.rem(z + ring - 1, ring)
+
+    def at_z(zz, cc):
+        return (lax.rem(zz, chips) * 2 + cc, me_mp, lax.div(zz, chips))
+
+    next_dev, prev_dev = at_z(z_next, core), at_z(z_prev, core)
+    sibling = (z_lo * 2 + 1 - core, me_mp, me_group)
+
+    barrier = pltpu.get_barrier_semaphore()
+    for dev in (next_dev, prev_dev, sibling):
+        pl.semaphore_signal(barrier, inc=1, device_id=dev, device_id_type=MESH)
+    pl.semaphore_wait(barrier, 3)
+
+    n_pieces = out_ref.shape[0]
+    rows = out_ref.shape[1]
+    quarter = n_pieces // 4
+
+    def plus_piece(k):
+        return 2 * quarter + 2 * k + core
+
+    def minus_piece(k):
+        return 2 * k + core
+
+    def chain(src, p, dev):
+        return pltpu.make_async_remote_copy(
+            src_ref=src,
+            dst_ref=out_ref.at[p],
+            send_sem=send_sem.at[p],
+            recv_sem=recv_sem.at[p],
+            device_id=dev,
+            device_id_type=MESH,
+        )
+
+    def to_sibling(p):
+        return pltpu.make_async_remote_copy(
+            src_ref=out_ref.at[p],
+            dst_ref=out_ref.at[p],
+            send_sem=send_sem.at[n_pieces + p],
+            recv_sem=recv_sem.at[p],
+            device_id=sibling,
+            device_id_type=MESH,
+        )
+
+    def own(p):
+        return own_ref.at[pl.ds(pl.multiple_of(p * rows, rows), rows)]
+
+    @pl.when(z_lo == chips - 1)
+    def _():
+        for k in range(quarter):
+            p = plus_piece(k)
+            chain(own(p), p, next_dev).start()
+
+    @pl.when(z_lo == 0)
+    def _():
+        for k in range(quarter):
+            p = minus_piece(k)
+            chain(own(p), p, prev_dev).start()
+
+    for k in range(quarter):
+        for p, fwd, dev in (
+            (plus_piece(k), z_lo < chips - 1, next_dev),
+            (minus_piece(k), z_lo > 0, prev_dev),
+        ):
+            chain(out_ref.at[p], p, dev).wait_recv()
+
+            @pl.when(fwd)
+            def _():
+                chain(out_ref.at[p], p, dev).start()
+
+            to_sibling(p).start()
+
+    for k in range(quarter):
+        for p in (plus_piece(k) + 1 - 2 * core, minus_piece(k) + 1 - 2 * core):
+            to_sibling(p).wait_recv()
+    for k in range(quarter):
+        for p in (plus_piece(k), minus_piece(k)):
+            chain(out_ref.at[p], p, next_dev).wait_send()
+            to_sibling(p).wait_send()
+
+
+def other_half_exchange(own, n_dp):
+    n_pieces = n_dp
+    rows = own.shape[0] // n_pieces
+    shape = (n_pieces, rows, own.shape[1])
+    moved = own.size * own.dtype.itemsize
+    return pl.pallas_call(
+        functools.partial(_other_half_kernel, n_dp),
+        out_shape=jax.ShapeDtypeStruct(shape, own.dtype),
+        in_specs=[pl.BlockSpec(memory_space=pltpu.VMEM)],
+        out_specs=pl.BlockSpec(memory_space=pltpu.VMEM),
+        scratch_shapes=[
+            pltpu.SemaphoreType.DMA((2 * n_pieces,)),
+            pltpu.SemaphoreType.DMA((n_pieces,)),
+        ],
+        compiler_params=pltpu.CompilerParams(collective_id=0, has_side_effects=True),
+        cost_estimate=pl.CostEstimate(flops=0, transcendentals=0, bytes_accessed=moved),
+    )(own).reshape(own.shape)
+
+
 def per_device(
-    hidden, neighbour_ids, counts, embed_table, w_query, w_key, w_value, w_out, grad_out
+    hidden, neighbour_ids, counts, embed_table, w_query, w_key, w_value, w_out, grad_out, n_dp
 ):
     tail_rows = BLOCK - 1
     rows_here = hidden.shape[0]
@@ -40,14 +155,6 @@
         lax.all_gather(query_rows, "mp", axis=1, tiled=True),
         lax.all_gather(grad_rows, "mp", axis=1, tiled=True),
     )
-    piece_rows = half // lax.axis_size("dp")
-    kv_local = jnp.concatenate([w_key, w_value], axis=1)
-    kv_piece = lax.dynamic_slice_in_dim(kv_local, me_dp * piece_rows, piece_rows, 0)
-    kv_other = lax.all_gather(
-        lax.ppermute(kv_piece, "group", swap), "dp", axis=0, tiled=True
-    )
-    cols_kv = w_key.shape[1]
-    wk_other, wv_other = kv_other[:, :cols_kv], kv_other[:, cols_kv:]
 
     flat_ids = neighbour_ids.reshape(-1)
     block_rows = embed_table.shape[0]
@@ -70,6 +177,11 @@
     ) - 1
     own_cols = recv_buf.reshape(owners * cap, -1)[own_owner * cap + own_rank]
     neighbours = lax.all_gather(own_cols, "mp", axis=1, tiled=True)
+    kv_local = jnp.concatenate([w_key, w_value], axis=1)
+    kv_local, own_cols = lax.optimization_barrier((kv_local, own_cols))
+    kv_other = other_half_exchange(kv_local, n_dp)
+    cols_kv = w_key.shape[1]
+    wk_other, wv_other = kv_other[:, :cols_kv], kv_other[:, cols_kv:]
 
     def this_half(x):
         return lax.dynamic_slice_in_dim(x, me_group * half, half, 1)
@@ -167,7 +279,7 @@
 
 def solution(mesh):
     return jax.shard_map(
-        per_device,
+        functools.partial(per_device, n_dp=mesh.shape["dp"]),
         mesh=mesh,
         in_specs=(
             P("dp", "mp"),

time: 402 us -> 398 us (0.990)
  Pallas kernels: 0 us -> 126 us
  waiting for transfers between devices: 280 us -> 157 us
  starting transfers between devices: 29.1 us -> 22 us
    pallas_call x0 -> x1, Pallas kernels: none -> 126 us  [other_half_exchange(): pl.pallas_call(functools.partial(_other_half_kernel, n_dp), out_shape=jax...]
    all_gather x1, waiting for transfers between devices: 51.8 us -> 0.02 us  [per_device(): neighbours = lax.all_gather(own_cols, 'mp', axis=1, tiled=True)]
    all_gather x1 -> x0, waiting for transfers between devices: 50.5 us -> none  [per_device(): lax.all_gather(lax.ppermute(kv_piece, 'group', swap), 'dp', axis=0, tiled...]
    all_gather x1, waiting for transfers between devices: 19.9 us -> 0.02 us  [per_device(): lax.all_gather(grad_rows, 'mp', axis=1, tiled=True)]
    ppermute x1 -> x0, waiting for transfers between devices: 13.9 us -> none  [per_device(): lax.ppermute(kv_piece, 'group', swap)]
    reduce_scatter x1, waiting for transfers between devices: 90.3 us -> 103 us  [per_device(): reduced = lax.psum_scatter(stacked, 'mp', scatter_dimension=1, tiled=True)]
    ppermute x1 -> x0, starting transfers between devices: 4.49 us -> none  [per_device(): lax.ppermute(kv_piece, 'group', swap)]
  transfers between devices with their start and end apart: 13 -> 11, of which waited for: 10 -> 7; matrix products, arithmetic and copies ran while one was open for 9% -> 8% of each run, Pallas kernels for 0% -> 32%
where the time goes in v7:
time: 398 us; the launch traced here: 395 us
  waiting for transfers between devices  157 us (39%)
  Pallas kernels  126 us (32%)
  matrix products  22.4 us (6%)
  starting transfers between devices  22 us (6%)
  blocking collectives  20.3 us (5%)
  local copies, waits for them, and re-layouts  18.4 us (5%)
  other arithmetic  14.8 us (4%)
  between operations  14.2 us (4%)
    pallas_call x1, Pallas kernels, other_half_exchange(): pl.pallas_call(functools.partial(_other_half_kernel, n_dp), out_shape=jax...  126 us
    reduce_scatter x1, waiting for transfers between devices, per_device(): reduced = lax.psum_scatter(stacked, 'mp', scatter_dimension=1, tiled=True)  103 us
    all_to_all x1, waiting for transfers between devices, per_device(): recv_buf = lax.all_to_all(send_buf, ('dp', 'group'), 0, 0, tiled=True)  22.2 us
    ppermute x5, waiting for transfers between devices, group_sum(): return x + lax.ppermute(x, 'group', swap)  17.8 us
    ppermute x1, waiting for transfers between devices, per_device(): lax.ppermute(both_cols, 'group', swap)  14.2 us
    ppermute x5, starting transfers between devices, group_sum(): return x + lax.ppermute(x, 'group', swap)  12.7 us
    all_gather x1, blocking collectives, per_device(): lax.all_gather(ids_f, 'dp', axis=0).astype(jnp.int32).reshape(owners, -1)  12.1 us
    all_gather x1, blocking collectives, per_device(): ids_f = lax.all_gather(flat_ids.astype(jnp.float32), 'group', axis=0)  8.14 us
  transfers between devices with their start and end apart: 11, of which 7 were waited for; matrix products, arithmetic and copies ran while one was open for 8% of the time, Pallas kernels for 32%

profile of v7, /device:TPU:192, one launch (start us, length us, event | category | flops | bytes accessed | tf_op | source)
XLA Modules:
  0.0 395.0 jit_solution(15706037354717797721)
XLA Ops:
  7.2 1.0 slice.47
  9.0 0.9 slice.45
  11.3 8.1 %all-gather.2 = f32[2,1,256]{2,1,0:T(1,128)S(1)} all-gather(f32[1,1,256]{2,1,0:T(1,128)S(1)} %convert_bitcast_fusion.1), channel_id=1, replica_groups=mesh['dp'=8,'mp'=16,'group'=2] {'group'}, dimensions={0}, use_global_device_ids=true | all-gather | bytes 3072 | tf_op jit(solution)/shard_map/all_gather | solution.py:163
  19.4 12.1 %all-gather.3 = f32[8,2,256]{2,1,0:T(2,128)S(1)} all-gather(f32[1,2,256]{2,1,0:T(2,128)S(1)} %copy.55), channel_id=2, replica_groups=mesh['dp'=8,'mp'=16,'group'=2] {'dp'}, dimensions={0}, use_global_device_ids=true | all-gather | bytes 18432 | tf_op jit(solution)/shard_map/all_gather | solution.py:164
  33.0 7.9 %gather_fusion = bf16[1024,512]{1,0:T(8,128)(2,1)} fusion(bf16[4096,512]{1,0:T(8,128)(2,1)} %param.12, s32[1024]{0:T(1024)S(1)} %broadcast_clamp_fusion), kind=kCustom, calls=%fused_computation | custom fusion | bytes 2101248 | tf_op jit(solution)/shard_map/gather | solution.py:171
  40.9 7.0 %all-to-all-start = ((bf16[16,64,512]{2,1,0:T(8,128)(2,1)}), bf16[16,64,512]{2,1,0:T(8,128)(2,1)S(1)}, u32[]{:S(2)}, u32[]{:S(2)}) async-start(bf16[16,64,512]{2,1,0:T(8,128)(2,1)} %bitcast.102), calls=%async_computation | async-start | bytes 2097152 | tf_op jit(solution)/shard_map/all_to_all | solution.py:172
  48.9 22.2 %all-to-all-done = bf16[16,64,512]{2,1,0:T(8,128)(2,1)S(1)} async-done(((bf16[16,64,512]{2,1,0:T(8,128)(2,1)}), bf16[16,64,512]{2,1,0:T(8,128)(2,1)S(1)}, u32[]{:S(2)}, u32[]{:S(2)}) %all-to-all-start) | async-done | bytes 1048608 | tf_op jit(solution)/shard_map/all_to_all | solution.py:172
  71.1 1.9 gather_fusion.1
  73.1 4.5 %pad_maximum_fusion.1.own_ref = bf16[4096,512]{1,0:T(8,128)(2,1)} fusion(bf16[4096,256]{1,0:T(8,128)(2,1)} %param.15, bf16[4096,256]{1,0:T(8,128)(2,1)} %param.14), kind=kLoop, calls=%fused_computation.9 | loop fusion | flops 8388608 | bytes 8388608 | tf_op jit(solution)/shard_map/concatenate | solution.py:180
  77.6 126.0 %shard_map.112 = bf16[8,512,512]{2,1,0:T(8,128)(2,1)} custom-call(bf16[4096,512]{1,0:T(8,128)(2,1)} %pad_maximum_fusion.1.own_ref), custom_call_target="tpu_custom_call" | custom-call | bytes 4194304 | tf_op jit(solution)/shard_map/pallas_call | solution.py:120
  203.6 2.1 fusion.33
  205.8 2.4 fusion.35
  208.2 6.0 %collective-permute-start = (f32[128,256]{1,0:T(8,128)S(1)}, f32[128,256]{1,0:T(8,128)S(1)}, u32[]{:S(2)}, u32[]{:S(2)}) collective-permute-start(f32[128,256]{1,0:T(8,128)S(1)} %fusion.35), channel_id=1, source_target_pairs={{0,1},{1,0},{2,3},{3,2},{4,5},{5,4},{6,7},{7,6},{8,9},{9,8},{10,11... | collective-permute-start | bytes 393224 | tf_op jit(solution)/shard_map/ppermute | solution.py:149
  214.7 2.5 collective-permute-done
  217.3 3.1 fusion.6
  220.4 2.3 fusion.20
  223.0 6.0 %collective-permute-start.2 = (f32[2,2,64]{2,1,0:T(2,128)S(1)}, f32[2,2,64]{2,1,0:T(2,128)S(1)}, u32[]{:S(2)}, u32[]{:S(2)}) collective-permute-start(f32[2,2,64]{2,1,0:T(2,128)S(1)} %get-tuple-element.25), channel_id=1, source_target_pairs={{0,1},{1,0},{2,3},{3,2},{4,5},{5,4},{6,7},{7,6},{8,9},{9,8},{10,11... | collective-permute-start | bytes 3080 | tf_op jit(solution)/shard_map/ppermute | solution.py:149
  229.0 2.9 fusion.2
  231.9 2.3 fusion.23
  235.3 8.3 %collective-permute-done.1 = f32[2,64,2,128]{3,1,2,0:T(8,128)S(1)} collective-permute-done((f32[2,64,2,128]{3,1,2,0:T(8,128)S(1)}, f32[2,64,2,128]{3,1,2,0:T(8,128)S(1)}, u32[]{:S(2)}, u32[]{:S(2)}) %collective-permute-start.1) | collective-permute-done | bytes 131104 | tf_op jit(solution)/shard_map/ppermute | solution.py:149
  244.6 2.5 fusion.4
  248.2 1.1 copy-done.5
  250.0 0.8 copy-done.4
  251.6 1.0 fusion
  253.1 6.6 %collective-permute-done.4 = f32[2,64,2,128]{3,1,2,0:T(8,128)S(1)} collective-permute-done((f32[2,64,2,128]{3,1,2,0:T(8,128)S(1)}, f32[2,64,2,128]{3,1,2,0:T(8,128)S(1)}, u32[]{:S(2)}, u32[]{:S(2)}) %collective-permute-start.4) | collective-permute-done | bytes 131104 | tf_op jit(solution)/shard_map/ppermute | solution.py:149
  261.4 3.7 pad_maximum_fusion
  265.2 102.6 %reduce-scatter.2.cloned.1.call-done = bf16[512,512]{1,0:T(8,128)(2,1)} async-done(((bf16[512,8192]{1,0:T(8,128)(2,1)}), bf16[512,512]{1,0:T(8,128)(2,1)}) %reduce-scatter.2.cloned.1.call-update) | async-done | bytes 524304 | tf_op jit(solution)/shard_map/reduce_scatter | solution.py:268
  367.7 1.0 slice.60
  368.7 2.1 collective-permute-start.5
  370.8 14.2 %collective-permute-done.5 = bf16[256,512]{1,0:T(8,128)(2,1)S(1)} collective-permute-done((bf16[256,512]{1,0:T(8,128)(2,1)S(1)}, bf16[256,512]{1,0:T(8,128)(2,1)S(1)}, u32[]{:S(2)}, u32[]{:S(2)}) %collective-permute-start.5) | collective-permute-done | bytes 262176 | tf_op jit(solution)/shard_map/ppermute | solution.py:270
  385.0 1.1 fusion.71
  386.1 0.9 convert.3
  (89 shorter events, 13.8 us)
Async XLA Ops:
  7.2 196.5 %copy-start = (bf16[256,4096]{1,0:T(8,128)(2,1)S(1)}, bf16[256,4096]{1,0:T(8,128)(2,1)}, u32[]{:S(2)}) copy-start(bf16[256,4096]{1,0:T(8,128)(2,1)} %param.16) | copy-start | bytes 6291460
  7.2 196.4 %all-gather.10.cloned.1.call-start = ((), (), s32[]{:S(2)}) async-start(), calls=%async_computation.3 | async-start | bytes 2228224 | tf_op jit(solution)/shard_map/all_gather | solution.py:156
  9.0 196.9 %all-gather.8.cloned.1.call-start = ((), (), s32[]{:S(2)}) async-start(), calls=%async_computation.2 | async-start | bytes 2228224 | tf_op jit(solution)/shard_map/all_gather | solution.py:155
  40.9 7.0 %copy-start.7 = (s32[2,1,128]{2,1,0:T(1,128)S(1)}, s32[2,1,128]{2,1,0:T(1,128)}, u32[]{:S(2)}) copy-start(s32[2,1,128]{2,1,0:T(1,128)} %param.10) | copy-start | bytes 3076
  40.9 32.2 %copy-start.8 = (s32[2]{0:T(128)S(1)}, s32[2]{0:T(128)}, u32[]{:S(2)}) copy-start(s32[2]{0:T(128)} %param.11) | copy-start | bytes 28
  40.9 30.3 %all-to-all-start = ((bf16[16,64,512]{2,1,0:T(8,128)(2,1)}), bf16[16,64,512]{2,1,0:T(8,128)(2,1)S(1)}, u32[]{:S(2)}, u32[]{:S(2)}) async-start(bf16[16,64,512]{2,1,0:T(8,128)(2,1)} %bitcast.102), calls=%async_computation | async-start | bytes 2097152 | tf_op jit(solution)/shard_map/all_to_all | solution.py:172
  47.9 169.4 %all-gather.12.cloned.1.call-start = ((), (), s32[]{:S(2)}) async-start(), calls=%async_computation.5 | async-start | bytes 4456448 | tf_op jit(solution)/shard_map/all_gather | solution.py:179
  73.0 294.7 %reduce-scatter.2.cloned.1.call-start = ((), (), s32[]{:S(2)}) async-start(), calls=%async_computation.4 | async-start | bytes 8912896 | tf_op jit(solution)/shard_map/reduce_scatter | solution.py:268
  205.7 9.0 %collective-permute-start.3 = (f32[128,256]{1,0:T(8,128)S(1)}, f32[128,256]{1,0:T(8,128)S(1)}, u32[]{:S(2)}, u32[]{:S(2)}) collective-permute-start(f32[128,256]{1,0:T(8,128)S(1)} %fusion.33), channel_id=1, source_target_pairs={{0,1},{1,0},{2,3},{3,2},{4,5},{5,4},{6,7},{7,6},{8,9},{9,8},{10,11... | collective-permute-start | bytes 393224 | tf_op jit(solution)/shard_map/ppermute | solution.py:149
  208.2 9.0 %collective-permute-start = (f32[128,256]{1,0:T(8,128)S(1)}, f32[128,256]{1,0:T(8,128)S(1)}, u32[]{:S(2)}, u32[]{:S(2)}) collective-permute-start(f32[128,256]{1,0:T(8,128)S(1)} %fusion.35), channel_id=1, source_target_pairs={{0,1},{1,0},{2,3},{3,2},{4,5},{5,4},{6,7},{7,6},{8,9},{9,8},{10,11... | collective-permute-start | bytes 393224 | tf_op jit(solution)/shard_map/ppermute | solution.py:149
  217.2 3.1 copy-start.1
  223.0 8.9 %copy-start.3 = (bf16[4096,256]{1,0:T(8,128)(2,1)S(1)}, bf16[4096,256]{1,0:T(8,128)(2,1)}, u32[]{:S(2)}) copy-start(bf16[4096,256]{1,0:T(8,128)(2,1)} %param.15) | copy-start | bytes 6291460
  223.0 11.9 %collective-permute-start.2 = (f32[2,2,64]{2,1,0:T(2,128)S(1)}, f32[2,2,64]{2,1,0:T(2,128)S(1)}, u32[]{:S(2)}, u32[]{:S(2)}) collective-permute-start(f32[2,2,64]{2,1,0:T(2,128)S(1)} %get-tuple-element.25), channel_id=1, source_target_pairs={{0,1},{1,0},{2,3},{3,2},{4,5},{5,4},{6,7},{7,6},{8,9},{9,8},{10,11... | collective-permute-start | bytes 3080 | tf_op jit(solution)/shard_map/ppermute | solution.py:149
  234.5 9.1 %collective-permute-start.1 = (f32[2,64,2,128]{3,1,2,0:T(8,128)S(1)}, f32[2,64,2,128]{3,1,2,0:T(8,128)S(1)}, u32[]{:S(2)}, u32[]{:S(2)}) collective-permute-start(f32[2,64,2,128]{3,1,2,0:T(8,128)S(1)} %convolution_bitcast_fusion.1), channel_id=1, source_target_pairs={{0,1},{1,0},{2,3},{3,2},{4,5},{5,4},{6,7},{7,6},{8,9},{9,8},{10,11... | collective-permute-start | bytes 393224 | tf_op jit(solution)/shard_map/ppermute | solution.py:149
  244.6 2.5 copy-start.2
  247.1 2.2 copy-start.5
  247.9 11.8 %collective-permute-start.4 = (f32[2,64,2,128]{3,1,2,0:T(8,128)S(1)}, f32[2,64,2,128]{3,1,2,0:T(8,128)S(1)}, u32[]{:S(2)}, u32[]{:S(2)}) collective-permute-start(f32[2,64,2,128]{3,1,2,0:T(8,128)S(1)} %convolution_bitcast_fusion), channel_id=1, source_target_pairs={{0,1},{1,0},{2,3},{3,2},{4,5},{5,4},{6,7},{7,6},{8,9},{9,8},{10,11... | collective-permute-start | bytes 393224 | tf_op jit(solution)/shard_map/ppermute | solution.py:149
  249.3 1.6 copy-start.4
  252.6 7.2 %copy-start.6 = (bf16[4096,256]{1,0:T(8,128)(2,1)S(1)}, bf16[4096,256]{1,0:T(8,128)(2,1)}, u32[]{:S(2)}) copy-start(bf16[4096,256]{1,0:T(8,128)(2,1)} %param.13) | copy-start | bytes 6291460
  368.7 16.4 %collective-permute-start.5 = (bf16[256,512]{1,0:T(8,128)(2,1)S(1)}, bf16[256,512]{1,0:T(8,128)(2,1)S(1)}, u32[]{:S(2)}, u32[]{:S(2)}) collective-permute-start(bf16[256,512]{1,0:T(8,128)(2,1)S(1)} %slice.60), channel_id=1, source_target_pairs={{0,1},{1,0},{2,3},{3,2},{4,5},{5,4},{6,7},{7,6},{8,9},{9,8},{10,11... | collective-permute-start | bytes 786440 | tf_op jit(solution)/shard_map/ppermute | solution.py:270
Sparse Core Ops, SparseCore 0:
  11.0 53.4 all-gather.9
  67.5 52.0 all-gather.7
  122.6 62.0 all-gather.11
  265.3 102.3 reduce-scatter.1

commit v8 on v7

--- a/solution.py
+++ b/solution.py
@@ -113,7 +113,7 @@
 
 
 def other_half_exchange(own, n_dp):
-    n_pieces = n_dp
+    n_pieces = 2 * n_dp
     rows = own.shape[0] // n_pieces
     shape = (n_pieces, rows, own.shape[1])
     moved = own.size * own.dtype.itemsize

time: 398 us -> 409 us (1.028)
  Pallas kernels: 126 us -> 140 us
  waiting for transfers between devices: 157 us -> 152 us
    pallas_call x1, Pallas kernels: 126 us -> 140 us  [other_half_exchange(): pl.pallas_call(functools.partial(_other_half_kernel, n_dp), out_shape=jax...]
  transfers between devices with their start and end apart: 11 -> 11, of which waited for: 7 -> 7; matrix products, arithmetic and copies ran while one was open for 8% -> 8% of each run, Pallas kernels for 32% -> 34%
where the time goes in v8:
time: 409 us; the launch traced here: 407 us
  waiting for transfers between devices  152 us (37%)
  Pallas kernels  140 us (34%)
  starting transfers between devices  25.8 us (6%)
  matrix products  22.4 us (5%)
  blocking collectives  20.3 us (5%)
  local copies, waits for them, and re-layouts  17.3 us (4%)
  other arithmetic  14.8 us (4%)
  between operations  14.2 us (3%)
    pallas_call x1, Pallas kernels, other_half_exchange(): pl.pallas_call(functools.partial(_other_half_kernel, n_dp), out_shape=jax...  140 us
    reduce_scatter x1, waiting for transfers between devices, per_device(): reduced = lax.psum_scatter(stacked, 'mp', scatter_dimension=1, tiled=True)  102 us
    all_to_all x1, waiting for transfers between devices, per_device(): recv_buf = lax.all_to_all(send_buf, ('dp', 'group'), 0, 0, tiled=True)  22.2 us
    ppermute x5, starting transfers between devices, group_sum(): return x + lax.ppermute(x, 'group', swap)  16.5 us
    ppermute x1, waiting for transfers between devices, per_device(): lax.ppermute(both_cols, 'group', swap)  14.1 us
    ppermute x5, waiting for transfers between devices, group_sum(): return x + lax.ppermute(x, 'group', swap)  13.8 us
    all_gather x1, blocking collectives, per_device(): lax.all_gather(ids_f, 'dp', axis=0).astype(jnp.int32).reshape(owners, -1)  12.1 us
  transfers between devices with their start and end apart: 11, of which 7 were waited for; matrix products, arithmetic and copies ran while one was open for 8% of the time, Pallas kernels for 34%

profile of v8, /device:TPU:192, one launch (start us, length us, event | category | flops | bytes accessed | tf_op | source)
XLA Modules:
  0.0 406.6 jit_solution(15444402446526655446)
XLA Ops:
  7.2 1.0 slice.47
  9.0 0.9 slice.45
  11.3 8.1 %all-gather.2 = f32[2,1,256]{2,1,0:T(1,128)S(1)} all-gather(f32[1,1,256]{2,1,0:T(1,128)S(1)} %convert_bitcast_fusion.1), channel_id=1, replica_groups=mesh['dp'=8,'mp'=16,'group'=2] {'group'}, dimensions={0}, use_global_device_ids=true | all-gather | bytes 3072 | tf_op jit(solution)/shard_map/all_gather | solution.py:163
  19.4 12.1 %all-gather.3 = f32[8,2,256]{2,1,0:T(2,128)S(1)} all-gather(f32[1,2,256]{2,1,0:T(2,128)S(1)} %copy.55), channel_id=2, replica_groups=mesh['dp'=8,'mp'=16,'group'=2] {'dp'}, dimensions={0}, use_global_device_ids=true | all-gather | bytes 18432 | tf_op jit(solution)/shard_map/all_gather | solution.py:164
  33.0 7.9 %gather_fusion = bf16[1024,512]{1,0:T(8,128)(2,1)} fusion(bf16[4096,512]{1,0:T(8,128)(2,1)} %param.12, s32[1024]{0:T(1024)S(1)} %broadcast_clamp_fusion), kind=kCustom, calls=%fused_computation | custom fusion | bytes 2101248 | tf_op jit(solution)/shard_map/gather | solution.py:171
  40.9 7.0 %all-to-all-start = ((bf16[16,64,512]{2,1,0:T(8,128)(2,1)}), bf16[16,64,512]{2,1,0:T(8,128)(2,1)S(1)}, u32[]{:S(2)}, u32[]{:S(2)}) async-start(bf16[16,64,512]{2,1,0:T(8,128)(2,1)} %bitcast.102), calls=%async_computation | async-start | bytes 2097152 | tf_op jit(solution)/shard_map/all_to_all | solution.py:172
  48.9 22.2 %all-to-all-done = bf16[16,64,512]{2,1,0:T(8,128)(2,1)S(1)} async-done(((bf16[16,64,512]{2,1,0:T(8,128)(2,1)}), bf16[16,64,512]{2,1,0:T(8,128)(2,1)S(1)}, u32[]{:S(2)}, u32[]{:S(2)}) %all-to-all-start) | async-done | bytes 1048608 | tf_op jit(solution)/shard_map/all_to_all | solution.py:172
  71.1 1.9 gather_fusion.1
  73.1 4.5 %pad_maximum_fusion.1.own_ref = bf16[4096,512]{1,0:T(8,128)(2,1)} fusion(bf16[4096,256]{1,0:T(8,128)(2,1)} %param.15, bf16[4096,256]{1,0:T(8,128)(2,1)} %param.14), kind=kLoop, calls=%fused_computation.9 | loop fusion | flops 8388608 | bytes 8388608 | tf_op jit(solution)/shard_map/concatenate | solution.py:180
  77.6 139.6 %shard_map.112 = bf16[16,256,512]{2,1,0:T(8,128)(2,1)} custom-call(bf16[4096,512]{1,0:T(8,128)(2,1)} %pad_maximum_fusion.1.own_ref), custom_call_target="tpu_custom_call" | custom-call | bytes 4194304 | tf_op jit(solution)/shard_map/pallas_call | solution.py:120
  217.2 2.1 fusion.33
  219.3 4.1 %collective-permute-start.3 = (f32[128,256]{1,0:T(8,128)S(1)}, f32[128,256]{1,0:T(8,128)S(1)}, u32[]{:S(2)}, u32[]{:S(2)}) collective-permute-start(f32[128,256]{1,0:T(8,128)S(1)} %fusion.33), channel_id=1, source_target_pairs={{0,1},{1,0},{2,3},{3,2},{4,5},{5,4},{6,7},{7,6},{8,9},{9,8},{10,11... | collective-permute-start | bytes 393224 | tf_op jit(solution)/shard_map/ppermute | solution.py:149
  223.4 2.4 fusion.35
  225.8 2.0 collective-permute-start
  228.3 6.5 %collective-permute-done = f32[128,256]{1,0:T(8,128)S(1)} collective-permute-done((f32[128,256]{1,0:T(8,128)S(1)}, f32[128,256]{1,0:T(8,128)S(1)}, u32[]{:S(2)}, u32[]{:S(2)}) %collective-permute-start) | collective-permute-done | bytes 131104 | tf_op jit(solution)/shard_map/ppermute | solution.py:149
  234.8 3.1 fusion.6
  237.9 2.3 fusion.20
  240.6 2.0 collective-permute-start.2
  242.6 2.9 fusion.2
  245.5 2.3 fusion.23
  248.0 4.3 %collective-permute-start.1 = (f32[2,64,2,128]{3,1,2,0:T(8,128)S(1)}, f32[2,64,2,128]{3,1,2,0:T(8,128)S(1)}, u32[]{:S(2)}, u32[]{:S(2)}) collective-permute-start(f32[2,64,2,128]{3,1,2,0:T(8,128)S(1)} %convolution_bitcast_fusion.1), channel_id=1, source_target_pairs={{0,1},{1,0},{2,3},{3,2},{4,5},{5,4},{6,7},{7,6},{8,9},{9,8},{10,11... | collective-permute-start | bytes 393224 | tf_op jit(solution)/shard_map/ppermute | solution.py:149
  252.8 4.4 %collective-permute-done.1 = f32[2,64,2,128]{3,1,2,0:T(8,128)S(1)} collective-permute-done((f32[2,64,2,128]{3,1,2,0:T(8,128)S(1)}, f32[2,64,2,128]{3,1,2,0:T(8,128)S(1)}, u32[]{:S(2)}, u32[]{:S(2)}) %collective-permute-start.1) | collective-permute-done | bytes 131104 | tf_op jit(solution)/shard_map/ppermute | solution.py:149
  258.1 2.5 fusion.4
  261.5 4.1 %collective-permute-start.4 = (f32[2,64,2,128]{3,1,2,0:T(8,128)S(1)}, f32[2,64,2,128]{3,1,2,0:T(8,128)S(1)}, u32[]{:S(2)}, u32[]{:S(2)}) collective-permute-start(f32[2,64,2,128]{3,1,2,0:T(8,128)S(1)} %convolution_bitcast_fusion), channel_id=1, source_target_pairs={{0,1},{1,0},{2,3},{3,2},{4,5},{5,4},{6,7},{7,6},{8,9},{9,8},{10,11... | collective-permute-start | bytes 393224 | tf_op jit(solution)/shard_map/ppermute | solution.py:149
  268.0 1.0 fusion
  269.4 2.5 collective-permute-done.4
  273.7 3.7 pad_maximum_fusion
  277.4 102.0 %reduce-scatter.2.cloned.1.call-done = bf16[512,512]{1,0:T(8,128)(2,1)} async-done(((bf16[512,8192]{1,0:T(8,128)(2,1)}), bf16[512,512]{1,0:T(8,128)(2,1)}) %reduce-scatter.2.cloned.1.call-update) | async-done | bytes 524304 | tf_op jit(solution)/shard_map/reduce_scatter | solution.py:268
  379.4 1.0 slice.60
  380.4 2.1 collective-permute-start.5
  382.5 14.1 %collective-permute-done.5 = bf16[256,512]{1,0:T(8,128)(2,1)S(1)} collective-permute-done((bf16[256,512]{1,0:T(8,128)(2,1)S(1)}, bf16[256,512]{1,0:T(8,128)(2,1)S(1)}, u32[]{:S(2)}, u32[]{:S(2)}) %collective-permute-start.5) | collective-permute-done | bytes 262176 | tf_op jit(solution)/shard_map/ppermute | solution.py:270
  396.6 1.1 fusion.71
  (89 shorter events, 14.7 us)
Async XLA Ops:
  7.2 210.0 %copy-start = (bf16[256,4096]{1,0:T(8,128)(2,1)S(1)}, bf16[256,4096]{1,0:T(8,128)(2,1)}, u32[]{:S(2)}) copy-start(bf16[256,4096]{1,0:T(8,128)(2,1)} %param.16) | copy-start | bytes 6291460
  7.2 210.0 %all-gather.10.cloned.1.call-start = ((), (), s32[]{:S(2)}) async-start(), calls=%async_computation.3 | async-start | bytes 2228224 | tf_op jit(solution)/shard_map/all_gather | solution.py:156
  9.0 214.4 %all-gather.8.cloned.1.call-start = ((), (), s32[]{:S(2)}) async-start(), calls=%async_computation.2 | async-start | bytes 2228224 | tf_op jit(solution)/shard_map/all_gather | solution.py:155
  40.9 7.0 %copy-start.7 = (s32[2,1,128]{2,1,0:T(1,128)S(1)}, s32[2,1,128]{2,1,0:T(1,128)}, u32[]{:S(2)}) copy-start(s32[2,1,128]{2,1,0:T(1,128)} %param.10) | copy-start | bytes 3076
  40.9 32.2 %copy-start.8 = (s32[2]{0:T(128)S(1)}, s32[2]{0:T(128)}, u32[]{:S(2)}) copy-start(s32[2]{0:T(128)} %param.11) | copy-start | bytes 28
  40.9 30.3 %all-to-all-start = ((bf16[16,64,512]{2,1,0:T(8,128)(2,1)}), bf16[16,64,512]{2,1,0:T(8,128)(2,1)S(1)}, u32[]{:S(2)}, u32[]{:S(2)}) async-start(bf16[16,64,512]{2,1,0:T(8,128)(2,1)} %bitcast.102), calls=%async_computation | async-start | bytes 2097152 | tf_op jit(solution)/shard_map/all_to_all | solution.py:172
  47.9 186.9 %all-gather.12.cloned.1.call-start = ((), (), s32[]{:S(2)}) async-start(), calls=%async_computation.5 | async-start | bytes 4456448 | tf_op jit(solution)/shard_map/all_gather | solution.py:179
  73.0 306.4 %reduce-scatter.2.cloned.1.call-start = ((), (), s32[]{:S(2)}) async-start(), calls=%async_computation.4 | async-start | bytes 8912896 | tf_op jit(solution)/shard_map/reduce_scatter | solution.py:268
  219.3 9.0 %collective-permute-start.3 = (f32[128,256]{1,0:T(8,128)S(1)}, f32[128,256]{1,0:T(8,128)S(1)}, u32[]{:S(2)}, u32[]{:S(2)}) collective-permute-start(f32[128,256]{1,0:T(8,128)S(1)} %fusion.33), channel_id=1, source_target_pairs={{0,1},{1,0},{2,3},{3,2},{4,5},{5,4},{6,7},{7,6},{8,9},{9,8},{10,11... | collective-permute-start | bytes 393224 | tf_op jit(solution)/shard_map/ppermute | solution.py:149
  225.8 9.0 %collective-permute-start = (f32[128,256]{1,0:T(8,128)S(1)}, f32[128,256]{1,0:T(8,128)S(1)}, u32[]{:S(2)}, u32[]{:S(2)}) collective-permute-start(f32[128,256]{1,0:T(8,128)S(1)} %fusion.35), channel_id=1, source_target_pairs={{0,1},{1,0},{2,3},{3,2},{4,5},{5,4},{6,7},{7,6},{8,9},{9,8},{10,11... | collective-permute-start | bytes 393224 | tf_op jit(solution)/shard_map/ppermute | solution.py:149
  234.8 3.1 copy-start.1
  240.6 4.9 %copy-start.3 = (bf16[4096,256]{1,0:T(8,128)(2,1)S(1)}, bf16[4096,256]{1,0:T(8,128)(2,1)}, u32[]{:S(2)}) copy-start(bf16[4096,256]{1,0:T(8,128)(2,1)} %param.15) | copy-start | bytes 6291460
  240.6 11.7 %collective-permute-start.2 = (f32[2,2,64]{2,1,0:T(2,128)S(1)}, f32[2,2,64]{2,1,0:T(2,128)S(1)}, u32[]{:S(2)}, u32[]{:S(2)}) collective-permute-start(f32[2,2,64]{2,1,0:T(2,128)S(1)} %get-tuple-element.25), channel_id=1, source_target_pairs={{0,1},{1,0},{2,3},{3,2},{4,5},{5,4},{6,7},{7,6},{8,9},{9,8},{10,11... | collective-permute-start | bytes 3080 | tf_op jit(solution)/shard_map/ppermute | solution.py:149
  248.0 9.2 %collective-permute-start.1 = (f32[2,64,2,128]{3,1,2,0:T(8,128)S(1)}, f32[2,64,2,128]{3,1,2,0:T(8,128)S(1)}, u32[]{:S(2)}, u32[]{:S(2)}) collective-permute-start(f32[2,64,2,128]{3,1,2,0:T(8,128)S(1)} %convolution_bitcast_fusion.1), channel_id=1, source_target_pairs={{0,1},{1,0},{2,3},{3,2},{4,5},{5,4},{6,7},{7,6},{8,9},{9,8},{10,11... | collective-permute-start | bytes 393224 | tf_op jit(solution)/shard_map/ppermute | solution.py:149
  258.1 2.5 copy-start.2
  260.6 5.0 %copy-start.5 = (bf16[16,256,512]{2,1,0:T(8,128)(2,1)S(1)}, bf16[16,256,512]{2,1,0:T(8,128)(2,1)}, u32[]{:S(2)}) copy-start(bf16[16,256,512]{2,1,0:T(8,128)(2,1)} %shard_map.112) | copy-start | bytes 12582916
  261.5 10.4 %collective-permute-start.4 = (f32[2,64,2,128]{3,1,2,0:T(8,128)S(1)}, f32[2,64,2,128]{3,1,2,0:T(8,128)S(1)}, u32[]{:S(2)}, u32[]{:S(2)}) collective-permute-start(f32[2,64,2,128]{3,1,2,0:T(8,128)S(1)} %convolution_bitcast_fusion), channel_id=1, source_target_pairs={{0,1},{1,0},{2,3},{3,2},{4,5},{5,4},{6,7},{7,6},{8,9},{9,8},{10,11... | collective-permute-start | bytes 393224 | tf_op jit(solution)/shard_map/ppermute | solution.py:149
  265.6 1.6 copy-start.4
  269.0 3.0 copy-start.6
  380.4 16.2 %collective-permute-start.5 = (bf16[256,512]{1,0:T(8,128)(2,1)S(1)}, bf16[256,512]{1,0:T(8,128)(2,1)S(1)}, u32[]{:S(2)}, u32[]{:S(2)}) collective-permute-start(bf16[256,512]{1,0:T(8,128)(2,1)S(1)} %slice.60), channel_id=1, source_target_pairs={{0,1},{1,0},{2,3},{3,2},{4,5},{5,4},{6,7},{7,6},{8,9},{9,8},{10,11... | collective-permute-start | bytes 786440 | tf_op jit(solution)/shard_map/ppermute | solution.py:270
Sparse Core Ops, SparseCore 0:
  11.0 53.4 all-gather.9
  67.5 52.0 all-gather.7
  122.6 62.0 all-gather.11
  277.5 101.8 reduce-scatter.1

commit v9 on v7

--- a/solution.py
+++ b/solution.py
@@ -160,8 +160,8 @@
     block_rows = embed_table.shape[0]
     owners = lax.axis_size("dp") * lax.axis_size("group")
     cap = flat_ids.shape[0] // 4
-    ids_f = lax.all_gather(flat_ids.astype(jnp.float32), "group", axis=0)
-    every_id = lax.all_gather(ids_f, "dp", axis=0).astype(jnp.int32).reshape(owners, -1)
+    ids_out = jnp.broadcast_to(flat_ids.astype(jnp.float32)[None], (owners, flat_ids.shape[0]))
+    every_id = lax.all_to_all(ids_out, ("dp", "group"), 0, 0, tiled=True).astype(jnp.int32)
     owner = me_dp * lax.axis_size("group") + me_group
     local_ids = every_id - owner * block_rows
     inside = (local_ids >= 0) & (local_ids < block_rows)
@@ -190,7 +190,9 @@
         return lax.dynamic_slice_in_dim(x, (1 - me_group) * half, half, 1)
 
     query_part = jnp.dot(this_half(full_query), w_query, preferred_element_type=jnp.float32)
-    query = group_sum(query_part).astype(jnp.bfloat16)
+    d_attn_part = contract(this_half(full_grad), w_out)
+    query_sum, d_attn_sum = group_sum(jnp.stack([query_part, d_attn_part]))
+    query = query_sum.astype(jnp.bfloat16)
     n_here, n_there = this_half(neighbours), other_half(neighbours)
     keys = (
         jnp.dot(n_here, w_key, preferred_element_type=jnp.float32)
@@ -216,7 +218,10 @@
         preferred_element_type=jnp.float32,
     )
     partial_total = jnp.sum(weights, -1)
-    numer, partial_total = group_sum(numer), group_sum(partial_total)
+    numer_size = numer.size
+    joined = group_sum(jnp.concatenate([numer.reshape(-1), partial_total.reshape(-1)]))
+    numer = joined[:numer_size].reshape(numer.shape)
+    partial_total = joined[numer_size:].reshape(partial_total.shape)
     total = partial_total + 1.0
     attn = numer / jnp.transpose(total, (0, 2, 1))[..., None]
     attn_bf = attn.reshape(rows_here, heads_here * HD).astype(jnp.bfloat16)
@@ -228,8 +233,7 @@
         )
 
     out_term = jnp.dot(attn_bf, w_out, preferred_element_type=jnp.float32)
-    d_attn_part = contract(this_half(full_grad), w_out)
-    d_attn = group_sum(d_attn_part).astype(jnp.bfloat16)
+    d_attn = d_attn_sum.astype(jnp.bfloat16)
     d_block = d_attn.reshape(blocks_here, BLOCK, heads_here, HD)
     prob = weights / total[..., None]
     d_prob = jnp.einsum("cqhd,ckhd->chqk", d_block, value_block, preferred_element_type=jnp.float32)

time: 398 us -> 441 us (1.11)
  waiting for transfers between devices: 157 us -> 203 us
  blocking collectives: 20.3 us -> 0 us
  Pallas kernels: 126 us -> 135 us
  matrix products: 22.4 us -> 29.5 us
    all_gather x1, waiting for transfers between devices: 0.02 us -> 52.8 us  [per_device(): lax.all_gather(grad_rows, 'mp', axis=1, tiled=True)]
    all_gather x2 -> x0, blocking collectives: 20.3 us -> none  [the longest x1 12.1 us: per_device(): lax.all_gather(ids_f, 'dp', axis=0).astype(jnp.int32).reshape(owners, -1)]
    ppermute x5 -> x3, waiting for transfers between devices: 17.8 us -> 6.65 us  [group_sum(): return x + lax.ppermute(x, 'group', swap)]
    pallas_call x1, Pallas kernels: 126 us -> 135 us  [other_half_exchange(): pl.pallas_call(functools.partial(_other_half_kernel, n_dp), out_shape=jax...]
    dot_general x6, matrix products: 7.59 us -> 14.6 us  [contract(): lax.dot_general(left, right, (((1,), (1,)), ((), ())), preferred_element_...]
    all_to_all x0 -> x1, starting transfers between devices: none -> 6.32 us  [per_device(): lax.all_to_all(ids_out, ('dp', 'group'), 0, 0, tiled=True).astype(jnp.int32)]
    ppermute x5 -> x3, starting transfers between devices: 12.7 us -> 6.93 us  [group_sum(): return x + lax.ppermute(x, 'group', swap)]
  transfers between devices with their start and end apart: 11 -> 10, of which waited for: 7 -> 7; matrix products, arithmetic and copies ran while one was open for 8% -> 7% of each run, Pallas kernels for 32% -> 31%
where the time goes in v9:
time: 441 us; the launch traced here: 439 us
  waiting for transfers between devices  203 us (46%)
  Pallas kernels  135 us (31%)
  matrix products  29.5 us (7%)
  starting transfers between devices  22.7 us (5%)
  local copies, waits for them, and re-layouts  19.5 us (4%)
  other arithmetic  14.3 us (3%)
  between operations  14.2 us (3%)
    pallas_call x1, Pallas kernels, other_half_exchange(): pl.pallas_call(functools.partial(_other_half_kernel, n_dp), out_shape=jax...  135 us
    reduce_scatter x1, waiting for transfers between devices, per_device(): reduced = lax.psum_scatter(stacked, 'mp', scatter_dimension=1, tiled=True)  103 us
    all_gather x1, waiting for transfers between devices, per_device(): lax.all_gather(grad_rows, 'mp', axis=1, tiled=True)  52.8 us
    all_to_all x1, waiting for transfers between devices, per_device(): recv_buf = lax.all_to_all(send_buf, ('dp', 'group'), 0, 0, tiled=True)  22.2 us
    dot_general x6, matrix products, contract(): lax.dot_general(left, right, (((1,), (1,)), ((), ())), preferred_element_...  14.6 us
    ppermute x1, waiting for transfers between devices, per_device(): lax.ppermute(both_cols, 'group', swap)  14.2 us
  transfers between devices with their start and end apart: 10, of which 7 were waited for; matrix products, arithmetic and copies ran while one was open for 7% of the time, Pallas kernels for 31%

profile of v9, /device:TPU:192, one launch (start us, length us, event | category | flops | bytes accessed | tf_op | source)
XLA Modules:
  0.0 438.9 jit_solution(10286073461706278863)
XLA Ops:
  7.2 1.0 slice.69
  9.0 0.9 slice.70
  11.9 6.3 %all-to-all-start = ((f32[16,1,256]{2,1,0:T(1,128)}), f32[16,1,256]{2,1,0:T(1,128)S(1)}, u32[]{:S(2)}, u32[]{:S(2)}) async-start(f32[16,1,256]{2,1,0:T(1,128)} %broadcast_in_dim.13), calls=%async_computation | async-start | bytes 32768 | tf_op jit(solution)/shard_map/all_to_all | solution.py:164
  18.2 4.2 all-to-all-done
  23.9 7.9 %gather_fusion = bf16[1024,512]{1,0:T(8,128)(2,1)} fusion(bf16[4096,512]{1,0:T(8,128)(2,1)} %param.12, s32[1024]{0:T(1024)S(1)} %broadcast_clamp_fusion), kind=kCustom, calls=%fused_computation | custom fusion | bytes 2101248 | tf_op jit(solution)/shard_map/gather | solution.py:171
  31.8 7.2 %all-to-all-start.1 = ((bf16[16,64,512]{2,1,0:T(8,128)(2,1)}), bf16[16,64,512]{2,1,0:T(8,128)(2,1)S(1)}, u32[]{:S(2)}, u32[]{:S(2)}) async-start(bf16[16,64,512]{2,1,0:T(8,128)(2,1)} %bitcast.106), calls=%async_computation.1 | async-start | bytes 2097152 | tf_op jit(solution)/shard_map/all_to_all | solution.py:172
  40.0 22.2 %all-to-all-done.1 = bf16[16,64,512]{2,1,0:T(8,128)(2,1)S(1)} async-done(((bf16[16,64,512]{2,1,0:T(8,128)(2,1)}), bf16[16,64,512]{2,1,0:T(8,128)(2,1)S(1)}, u32[]{:S(2)}, u32[]{:S(2)}) %all-to-all-start.1) | async-done | bytes 1048608 | tf_op jit(solution)/shard_map/all_to_all | solution.py:172
  62.2 1.9 gather_fusion.1
  64.5 2.4 convolution_bitcast_fusion.3
  66.9 52.8 %all-gather.7.cloned.1.call-done = bf16[128,8192]{1,0:T(8,128)(2,1)} async-done(((bf16[128,512]{1,0:T(8,128)(2,1)}), bf16[128,8192]{1,0:T(8,128)(2,1)}) %all-gather.7.cloned.1.call-update) | async-done | bytes 2097168 | tf_op jit(solution)/shard_map/all_gather | solution.py:156
  119.6 2.2 convolution_bitcast_fusion.2
  121.9 2.1 collective-permute-start
  123.9 3.8 pad_maximum_fusion.1.own_ref
  127.8 135.3 %shard_map.112 = bf16[8,512,512]{2,1,0:T(8,128)(2,1)} custom-call(bf16[4096,512]{1,0:T(8,128)(2,1)} %pad_maximum_fusion.1.own_ref), custom_call_target="tpu_custom_call" | custom-call | bytes 4194304 | tf_op jit(solution)/shard_map/pallas_call | solution.py:120
  263.2 3.1 fusion.6
  266.3 2.3 fusion.20
  269.1 3.1 fusion.2
  272.2 2.3 fusion.23
  274.9 2.3 collective-permute-start.1
  277.2 6.6 %collective-permute-done.1 = f32[33024]{0:T(1024)S(1)} collective-permute-done((f32[33024]{0:T(1024)S(1)}, f32[33024]{0:T(1024)S(1)}, u32[]{:S(2)}, u32[]{:S(2)}) %collective-permute-start.1) | collective-permute-done | bytes 132128 | tf_op jit(solution)/shard_map/ppermute | solution.py:149
  285.7 4.4 %fusion.4 = f32[256,4096]{1,0:T(8,128)} fusion(bf16[4096,512]{1,0:T(8,128)(2,1)} %bitcast.103, bf16[32,8,2,128]{3,2,1,0:T(2,128)(2,1)S(1)} %bitcast.109), kind=kOutput, calls=%fused_computation.15 | convolution fusion | flops 536870912 | bytes 6422528 | tf_op jit(solution)/shard_map/dot_general | solution.py:17
  290.1 2.7 fusion.39
  292.9 2.5 collective-permute-start.2
  295.4 3.7 convolution_add_fusion
  299.2 0.9 copy-done.6
  300.9 1.0 fusion
  305.1 3.6 pad_maximum_fusion
  308.7 103.0 %reduce-scatter.2.cloned.1.call-done = bf16[512,512]{1,0:T(8,128)(2,1)} async-done(((bf16[512,8192]{1,0:T(8,128)(2,1)}), bf16[512,512]{1,0:T(8,128)(2,1)}) %reduce-scatter.2.cloned.1.call-update) | async-done | bytes 524304 | tf_op jit(solution)/shard_map/reduce_scatter | solution.py:272
  411.7 1.0 slice.89
  412.7 2.1 collective-permute-start.3
  414.8 14.2 %collective-permute-done.3 = bf16[256,512]{1,0:T(8,128)(2,1)S(1)} collective-permute-done((bf16[256,512]{1,0:T(8,128)(2,1)S(1)}, bf16[256,512]{1,0:T(8,128)(2,1)S(1)}, u32[]{:S(2)}, u32[]{:S(2)}) %collective-permute-start.3) | collective-permute-done | bytes 262176 | tf_op jit(solution)/shard_map/ppermute | solution.py:274
  429.0 1.1 fusion.70
  (97 shorter events, 14.6 us)
Async XLA Ops:
  7.2 112.4 %copy-start = (bf16[256,4096]{1,0:T(8,128)(2,1)S(1)}, bf16[256,4096]{1,0:T(8,128)(2,1)}, u32[]{:S(2)}) copy-start(bf16[256,4096]{1,0:T(8,128)(2,1)} %param.16) | copy-start | bytes 6291460
  7.2 57.3 %all-gather.5.cloned.1.call-start = ((), (), s32[]{:S(2)}) async-start(), calls=%async_computation.3 | async-start | bytes 2228224 | tf_op jit(solution)/shard_map/all_gather | solution.py:155
  9.0 110.6 %all-gather.7.cloned.1.call-start = ((), (), s32[]{:S(2)}) async-start(), calls=%async_computation.4 | async-start | bytes 2228224 | tf_op jit(solution)/shard_map/all_gather | solution.py:156
  11.9 10.6 %all-to-all-start = ((f32[16,1,256]{2,1,0:T(1,128)}), f32[16,1,256]{2,1,0:T(1,128)S(1)}, u32[]{:S(2)}, u32[]{:S(2)}) async-start(f32[16,1,256]{2,1,0:T(1,128)} %broadcast_in_dim.13), calls=%async_computation | async-start | bytes 32768 | tf_op jit(solution)/shard_map/all_to_all | solution.py:164
  31.8 7.2 %copy-start.8 = (s32[2,1,128]{2,1,0:T(1,128)S(1)}, s32[2,1,128]{2,1,0:T(1,128)}, u32[]{:S(2)}) copy-start(s32[2,1,128]{2,1,0:T(1,128)} %param.10) | copy-start | bytes 3076
  31.8 30.4 %all-to-all-start.1 = ((bf16[16,64,512]{2,1,0:T(8,128)(2,1)}), bf16[16,64,512]{2,1,0:T(8,128)(2,1)S(1)}, u32[]{:S(2)}, u32[]{:S(2)}) async-start(bf16[16,64,512]{2,1,0:T(8,128)(2,1)} %bitcast.106), calls=%async_computation.1 | async-start | bytes 2097152 | tf_op jit(solution)/shard_map/all_to_all | solution.py:172
  38.9 224.3 %all-gather.9.cloned.1.call-start = ((), (), s32[]{:S(2)}) async-start(), calls=%async_computation.6 | async-start | bytes 4456448 | tf_op jit(solution)/shard_map/all_gather | solution.py:179
  64.1 347.6 %reduce-scatter.2.cloned.1.call-start = ((), (), s32[]{:S(2)}) async-start(), calls=%async_computation.5 | async-start | bytes 8912896 | tf_op jit(solution)/shard_map/reduce_scatter | solution.py:272
  119.6 4.3 copy-start.1
  121.9 5.9 %copy-start.9 = (s32[2]{0:T(128)S(1)}, s32[2]{0:T(128)}, u32[]{:S(2)}) copy-start(s32[2]{0:T(128)} %param.11) | copy-start | bytes 28
  121.9 141.2 %collective-permute-start = (f32[2,128,256]{2,1,0:T(8,128)S(1)}, f32[2,128,256]{2,1,0:T(8,128)S(1)}, u32[]{:S(2)}, u32[]{:S(2)}) collective-permute-start(f32[2,128,256]{2,1,0:T(8,128)S(1)} %pad_maximum_fusion.2), channel_id=1, source_target_pairs={{0,1},{1,0},{2,3},{3,2},{4,5},{5,4},{6,7},{7,6},{8,9},{9,8},{10,11... | collective-permute-start | bytes 786440 | tf_op jit(solution)/shard_map/ppermute | solution.py:149
  263.2 3.1 copy-start.2
  269.1 3.1 copy-start.4
  274.9 9.0 %collective-permute-start.1 = (f32[33024]{0:T(1024)S(1)}, f32[33024]{0:T(1024)S(1)}, u32[]{:S(2)}, u32[]{:S(2)}) collective-permute-start(f32[33024]{0:T(1024)S(1)} %pad_maximum_fusion.3), channel_id=1, source_target_pairs={{0,1},{1,0},{2,3},{3,2},{4,5},{5,4},{6,7},{7,6},{8,9},{9,8},{10,11... | collective-permute-start | bytes 396296 | tf_op jit(solution)/shard_map/ppermute | solution.py:149
  285.7 4.4 %copy-start.3 = (bf16[4096,256]{1,0:T(8,128)(2,1)S(1)}, bf16[4096,256]{1,0:T(8,128)(2,1)}, u32[]{:S(2)}) copy-start(bf16[4096,256]{1,0:T(8,128)(2,1)} %param.14) | copy-start | bytes 6291460
  292.9 9.6 %collective-permute-start.2 = (f32[2,64,2,128]{3,1,2,0:T(8,128)S(1)}, f32[2,64,2,128]{3,1,2,0:T(8,128)S(1)}, u32[]{:S(2)}, u32[]{:S(2)}) collective-permute-start(f32[2,64,2,128]{3,1,2,0:T(8,128)S(1)} %convolution_bitcast_fusion), channel_id=1, source_target_pairs={{0,1},{1,0},{2,3},{3,2},{4,5},{5,4},{6,7},{7,6},{8,9},{9,8},{10,11... | collective-permute-start | bytes 393224 | tf_op jit(solution)/shard_map/ppermute | solution.py:149
  295.4 3.7 copy-start.5
  295.4 4.7 %copy-start.6 = (f32[256,4096]{1,0:T(8,128)S(1)}, f32[256,4096]{1,0:T(8,128)}, u32[]{:S(2)}) copy-start(f32[256,4096]{1,0:T(8,128)} %fusion.39) | copy-start | bytes 12582916
  301.9 1.6 copy-start.7
  412.7 16.3 %collective-permute-start.3 = (bf16[256,512]{1,0:T(8,128)(2,1)S(1)}, bf16[256,512]{1,0:T(8,128)(2,1)S(1)}, u32[]{:S(2)}, u32[]{:S(2)}) collective-permute-start(bf16[256,512]{1,0:T(8,128)(2,1)S(1)} %slice.89), channel_id=1, source_target_pairs={{0,1},{1,0},{2,3},{3,2},{4,5},{5,4},{6,7},{7,6},{8,9},{9,8},{10,11... | collective-permute-start | bytes 786440 | tf_op jit(solution)/shard_map/ppermute | solution.py:274
Sparse Core Ops, SparseCore 0:
  11.0 53.4 all-gather.4
  67.5 52.0 all-gather.6
  122.6 62.0 all-gather.8
  308.8 102.8 reduce-scatter.1

commit v10 on v3

--- a/solution.py
+++ b/solution.py
@@ -43,9 +43,21 @@
     piece_rows = half // lax.axis_size("dp")
     kv_local = jnp.concatenate([w_key, w_value], axis=1)
     kv_piece = lax.dynamic_slice_in_dim(kv_local, me_dp * piece_rows, piece_rows, 0)
-    kv_other = lax.all_gather(
-        lax.ppermute(kv_piece, "group", swap), "dp", axis=0, tiled=True
-    )
+    held = lax.ppermute(kv_piece, "group", swap)[None]
+    n_dp = lax.axis_size("dp")
+    bit = n_dp // 2
+    while bit >= 1:
+        pairs = [(i, i ^ bit) for i in range(n_dp)]
+        other = lax.ppermute(held, "dp", pairs)
+        low = (me_dp // bit) % 2 == 0
+        held = jnp.where(
+            low, jnp.concatenate([held, other], 0), jnp.concatenate([other, held], 0)
+        )
+        bit //= 2
+    n_bits = n_dp.bit_length() - 1
+    held = held.reshape((2,) * n_bits + held.shape[1:])
+    held = jnp.transpose(held, tuple(reversed(range(n_bits))) + (n_bits, n_bits + 1))
+    kv_other = held.reshape(-1, held.shape[-1])
     cols_kv = w_key.shape[1]
     wk_other, wv_other = kv_other[:, :cols_kv], kv_other[:, cols_kv:]
 
@@ -53,8 +65,8 @@
     block_rows = embed_table.shape[0]
     owners = lax.axis_size("dp") * lax.axis_size("group")
     cap = flat_ids.shape[0] // 4
-    ids_f = lax.all_gather(flat_ids.astype(jnp.float32), "group", axis=0)
-    every_id = lax.all_gather(ids_f, "dp", axis=0).astype(jnp.int32).reshape(owners, -1)
+    ids_out = jnp.broadcast_to(flat_ids.astype(jnp.float32)[None], (owners, flat_ids.shape[0]))
+    every_id = lax.all_to_all(ids_out, ("dp", "group"), 0, 0, tiled=True).astype(jnp.int32)
     owner = me_dp * lax.axis_size("group") + me_group
     local_ids = every_id - owner * block_rows
     inside = (local_ids >= 0) & (local_ids < block_rows)

time: 402 us -> 348 us (0.87)
  waiting for transfers between devices: 280 us -> 216 us
  starting transfers between devices: 29.1 us -> 51.3 us
  blocking collectives: 20.3 us -> 0 us
  other arithmetic: 11.4 us -> 20.1 us
    all_gather x1 -> x0, waiting for transfers between devices: 50.5 us -> none  [per_device(): lax.all_gather(lax.ppermute(kv_piece, 'group', swap), 'dp', axis=0, tiled...]
    ppermute x1 -> x4, waiting for transfers between devices: 13.9 us -> 60.3 us  [the longest x3 45.6 us: per_device(): other = lax.ppermute(held, 'dp', pairs)]
    all_gather x1, waiting for transfers between devices: 51.8 us -> 5.56 us  [per_device(): neighbours = lax.all_gather(own_cols, 'mp', axis=1, tiled=True)]
    all_gather x2 -> x0, blocking collectives: 20.3 us -> none  [the longest x1 12.1 us: per_device(): lax.all_gather(ids_f, 'dp', axis=0).astype(jnp.int32).reshape(owners, -1)]
    all_gather x1, waiting for transfers between devices: 19.9 us -> 0.02 us  [per_device(): lax.all_gather(grad_rows, 'mp', axis=1, tiled=True)]
    ppermute x1 -> x4, starting transfers between devices: 4.49 us -> 19.2 us  [the longest x3 14.6 us: per_device(): other = lax.ppermute(held, 'dp', pairs)]
    select_n x0 -> x3, other arithmetic: none -> 8.82 us  [per_device(): jnp.where(low, jnp.concatenate([held, other], 0), jnp.concatenate([other,...]
    all_to_all x0 -> x1, starting transfers between devices: none -> 6.32 us  [per_device(): lax.all_to_all(ids_out, ('dp', 'group'), 0, 0, tiled=True).astype(jnp.int32)]
  transfers between devices with their start and end apart: 13 -> 16, of which waited for: 10 -> 13; matrix products, arithmetic and copies ran while one was open for 9% -> 10% of each run, Pallas kernels for 0% -> 0%
where the time goes in v10:
time: 348 us; the launch traced here: 345 us
  waiting for transfers between devices  216 us (62%)
  starting transfers between devices  51.3 us (15%)
  matrix products  22.6 us (6%)
  local copies, waits for them, and re-layouts  21 us (6%)
  other arithmetic  20.1 us (6%)
  between operations  14.2 us (4%)
    reduce_scatter x1, waiting for transfers between devices, per_device(): reduced = lax.psum_scatter(stacked, 'mp', scatter_dimension=1, tiled=True)  88.8 us
    ppermute x3, waiting for transfers between devices, per_device(): other = lax.ppermute(held, 'dp', pairs)  45.6 us
    all_to_all x1, waiting for transfers between devices, per_device(): recv_buf = lax.all_to_all(send_buf, ('dp', 'group'), 0, 0, tiled=True)  22.2 us
    ppermute x5, waiting for transfers between devices, group_sum(): return x + lax.ppermute(x, 'group', swap)  20.8 us
    ppermute x5, starting transfers between devices, group_sum(): return x + lax.ppermute(x, 'group', swap)  16.3 us
    ppermute x1, waiting for transfers between devices, per_device(): held = lax.ppermute(kv_piece, 'group', swap)[None]  14.7 us
    ppermute x3, starting transfers between devices, per_device(): other = lax.ppermute(held, 'dp', pairs)  14.6 us
    ppermute x1, waiting for transfers between devices, per_device(): lax.ppermute(both_cols, 'group', swap)  13.9 us
  transfers between devices with their start and end apart: 16, of which 13 were waited for; matrix products, arithmetic and copies ran while one was open for 10% of the time, Pallas kernels for 0%

profile of v10, /device:TPU:192, one launch (start us, length us, event | category | flops | bytes accessed | tf_op | source)
XLA Modules:
  0.0 345.0 jit_solution(3667915172866085355)
XLA Ops:
  11.9 6.3 %all-to-all-start = ((f32[16,1,256]{2,1,0:T(1,128)}), f32[16,1,256]{2,1,0:T(1,128)S(1)}, u32[]{:S(2)}, u32[]{:S(2)}) async-start(f32[16,1,256]{2,1,0:T(1,128)} %broadcast_in_dim.19), calls=%async_computation | async-start | bytes 32768 | tf_op jit(solution)/shard_map/all_to_all | solution.py:69
  18.2 4.2 %all-to-all-done = f32[16,1,256]{2,1,0:T(1,128)S(1)} async-done(((f32[16,1,256]{2,1,0:T(1,128)}), f32[16,1,256]{2,1,0:T(1,128)S(1)}, u32[]{:S(2)}, u32[]{:S(2)}) %all-to-all-start) | async-done | bytes 16416 | tf_op jit(solution)/shard_map/all_to_all | solution.py:69
  23.9 7.9 %gather_fusion = bf16[1024,512]{1,0:T(8,128)(2,1)} fusion(bf16[4096,512]{1,0:T(8,128)(2,1)} %param.12, s32[1024]{0:T(1024)S(1)} %broadcast_clamp_fusion), kind=kCustom, calls=%fused_computation | custom fusion | bytes 2101248 | tf_op jit(solution)/shard_map/gather | solution.py:76
  31.8 7.2 %all-to-all-start.1 = ((bf16[16,64,512]{2,1,0:T(8,128)(2,1)}), bf16[16,64,512]{2,1,0:T(8,128)(2,1)S(1)}, u32[]{:S(2)}, u32[]{:S(2)}) async-start(bf16[16,64,512]{2,1,0:T(8,128)(2,1)} %bitcast.103), calls=%async_computation.1 | async-start | bytes 2097152 | tf_op jit(solution)/shard_map/all_to_all | solution.py:77
  40.0 22.2 %all-to-all-done.1 = bf16[16,64,512]{2,1,0:T(8,128)(2,1)S(1)} async-done(((bf16[16,64,512]{2,1,0:T(8,128)(2,1)}), bf16[16,64,512]{2,1,0:T(8,128)(2,1)S(1)}, u32[]{:S(2)}, u32[]{:S(2)}) %all-to-all-start.1) | async-done | bytes 1048608 | tf_op jit(solution)/shard_map/all_to_all | solution.py:77
  65.2 4.6 %collective-permute-start = (bf16[512,512]{1,0:T(8,128)(2,1)S(1)}, bf16[512,512]{1,0:T(8,128)(2,1)S(1)}, u32[]{:S(2)}, u32[]{:S(2)}) collective-permute-start(bf16[512,512]{1,0:T(8,128)(2,1)S(1)} %fusion.46), channel_id=1, source_target_pairs={{0,1},{1,0},{2,3},{3,2},{4,5},{5,4},{6,7},{7,6},{8,9},{9,8},{10,11... | collective-permute-start | bytes 1572872 | tf_op jit(solution)/shard_map/ppermute | solution.py:46
  69.8 14.7 %collective-permute-done = bf16[512,512]{1,0:T(8,128)(2,1)S(1)} collective-permute-done((bf16[512,512]{1,0:T(8,128)(2,1)S(1)}, bf16[512,512]{1,0:T(8,128)(2,1)S(1)}, u32[]{:S(2)}, u32[]{:S(2)}) %collective-permute-start) | collective-permute-done | bytes 524320 | tf_op jit(solution)/shard_map/ppermute | solution.py:46
  84.5 12.2 %collective-permute-start.1 = (bf16[1,512,512]{2,1,0:T(8,128)(2,1)S(1)}, bf16[1,512,512]{2,1,0:T(8,128)(2,1)}, u32[]{:S(2)}, u32[]{:S(2)}) collective-permute-start(bf16[1,512,512]{2,1,0:T(8,128)(2,1)S(1)} %bitcast.109), channel_id=1, source_target_pairs={{0,128},{32,160},{64,192},{96,224},{128,0},{160,32},{192,64},{224,... | collective-permute-start | bytes 1572872 | tf_op jit(solution)/shard_map/ppermute | solution.py:51
  96.7 22.1 %collective-permute-done.1 = bf16[1,512,512]{2,1,0:T(8,128)(2,1)} collective-permute-done((bf16[1,512,512]{2,1,0:T(8,128)(2,1)S(1)}, bf16[1,512,512]{2,1,0:T(8,128)(2,1)}, u32[]{:S(2)}, u32[]{:S(2)}) %collective-permute-start.1) | collective-permute-done | bytes 524320 | tf_op jit(solution)/shard_map/ppermute | solution.py:51
  120.6 2.4 collective-permute-start.2
  123.0 23.5 %collective-permute-done.2 = bf16[2,512,512]{2,1,0:T(8,128)(2,1)} collective-permute-done((bf16[2,512,512]{2,1,0:T(8,128)(2,1)S(1)}, bf16[2,512,512]{2,1,0:T(8,128)(2,1)}, u32[]{:S(2)}, u32[]{:S(2)}) %collective-permute-start.2) | collective-permute-done | bytes 1048608 | tf_op jit(solution)/shard_map/ppermute | solution.py:51
  146.5 3.2 maximum_select_fusion.2
  151.8 4.3 %collective-permute-start.7 = (f32[128,256]{1,0:T(8,128)S(1)}, f32[128,256]{1,0:T(8,128)S(1)}, u32[]{:S(2)}, u32[]{:S(2)}) collective-permute-start(f32[128,256]{1,0:T(8,128)S(1)} %fusion.41), channel_id=1, source_target_pairs={{0,1},{1,0},{2,3},{3,2},{4,5},{5,4},{6,7},{7,6},{8,9},{9,8},{10,11... | collective-permute-start | bytes 393224 | tf_op jit(solution)/shard_map/ppermute | solution.py:34
  156.1 2.4 fusion.43
  160.3 2.9 collective-permute-done.7
  163.3 8.9 %collective-permute-done.4 = f32[128,256]{1,0:T(8,128)S(1)} collective-permute-done((f32[128,256]{1,0:T(8,128)S(1)}, f32[128,256]{1,0:T(8,128)S(1)}, u32[]{:S(2)}, u32[]{:S(2)}) %collective-permute-start.4) | collective-permute-done | bytes 131104 | tf_op jit(solution)/shard_map/ppermute | solution.py:34
  172.3 3.8 %maximum_select_fusion.1 = bf16[8,512,512]{2,1,0:T(8,128)(2,1)S(1)} fusion(bf16[4,512,512]{2,1,0:T(8,128)(2,1)} %collective-permute-done.3, bf16[4,512,512]{2,1,0:T(8,128)(2,1)} %maximum_select_fusion.2, pred[]{:T(512)S(6)} %eq.62), kind=kLoop, calls=%fused_computation.11 | loop fusion | flops 6291456 | bytes 8388609 | tf_op jit(solution)/shard_map/jit(_where)/select_n | solution.py:53
  176.1 2.4 copy.75
  178.5 5.6 %all-gather.9.cloned.1.call-done = bf16[256,8192]{1,0:T(8,128)(2,1)} async-done(((bf16[256,512]{1,0:T(8,128)(2,1)}), bf16[256,8192]{1,0:T(8,128)(2,1)}) %all-gather.9.cloned.1.call-update) | async-done | bytes 4194320 | tf_op jit(solution)/shard_map/all_gather | solution.py:84
  184.1 3.1 fusion.12
  187.6 2.4 fusion.25
  190.0 3.1 fusion.10
  193.4 2.3 fusion.30
  196.1 2.2 collective-permute-start.6
  198.5 4.0 %collective-permute-start.5 = (f32[2,64,2,128]{3,1,2,0:T(8,128)S(1)}, f32[2,64,2,128]{3,1,2,0:T(8,128)S(1)}, u32[]{:S(2)}, u32[]{:S(2)}) collective-permute-start(f32[2,64,2,128]{3,1,2,0:T(8,128)S(1)} %convolution_bitcast_fusion.1), channel_id=1, source_target_pairs={{0,1},{1,0},{2,3},{3,2},{4,5},{5,4},{6,7},{7,6},{8,9},{9,8},{10,11... | collective-permute-start | bytes 393224 | tf_op jit(solution)/shard_map/ppermute | solution.py:34
  204.6 4.7 %collective-permute-done.5 = f32[2,64,2,128]{3,1,2,0:T(8,128)S(1)} collective-permute-done((f32[2,64,2,128]{3,1,2,0:T(8,128)S(1)}, f32[2,64,2,128]{3,1,2,0:T(8,128)S(1)}, u32[]{:S(2)}, u32[]{:S(2)}) %collective-permute-start.5) | collective-permute-done | bytes 131104 | tf_op jit(solution)/shard_map/ppermute | solution.py:34
  210.3 2.5 fusion.4
  213.6 4.0 %collective-permute-start.8 = (f32[2,64,2,128]{3,1,2,0:T(8,128)S(1)}, f32[2,64,2,128]{3,1,2,0:T(8,128)S(1)}, u32[]{:S(2)}, u32[]{:S(2)}) collective-permute-start(f32[2,64,2,128]{3,1,2,0:T(8,128)S(1)} %convolution_bitcast_fusion), channel_id=1, source_target_pairs={{0,1},{1,0},{2,3},{3,2},{4,5},{5,4},{6,7},{7,6},{8,9},{9,8},{10,11... | collective-permute-start | bytes 393224 | tf_op jit(solution)/shard_map/ppermute | solution.py:34
  221.4 2.5 collective-permute-done.8
  225.7 3.5 %pad_maximum_fusion = bf16[512,8192]{1,0:T(8,128)(2,1)} fusion(bf16[256,8192]{1,0:T(8,128)(2,1)S(1)} %fusion, bf16[128,8192]{1,0:T(8,128)(2,1)S(1)} %get-tuple-element.28, bf16[128,8192]{1,0:T(8,128)(2,1)S(1)} %get-tuple-element.29), kind=kLoop, calls=%fused_computation.4 | loop fusion | flops 25165824 | bytes 16777216 | tf_op jit(solution)/shard_map/concatenate | solution.py:160
  229.3 88.8 %reduce-scatter.2.cloned.1.call-done = bf16[512,512]{1,0:T(8,128)(2,1)} async-done(((bf16[512,8192]{1,0:T(8,128)(2,1)}), bf16[512,512]{1,0:T(8,128)(2,1)}) %reduce-scatter.2.cloned.1.call-update) | async-done | bytes 524304 | tf_op jit(solution)/shard_map/reduce_scatter | solution.py:168
  321.1 13.9 %collective-permute-done.9 = bf16[256,512]{1,0:T(8,128)(2,1)S(1)} collective-permute-done((bf16[256,512]{1,0:T(8,128)(2,1)S(1)}, bf16[256,512]{1,0:T(8,128)(2,1)S(1)}, u32[]{:S(2)}, u32[]{:S(2)}) %collective-permute-start.9) | collective-permute-done | bytes 262176 | tf_op jit(solution)/shard_map/ppermute | solution.py:170
  (102 shorter events, 33.0 us)
Async XLA Ops:
  7.2 142.6 %copy-start = (bf16[256,4096]{1,0:T(8,128)(2,1)S(1)}, bf16[256,4096]{1,0:T(8,128)(2,1)}, u32[]{:S(2)}) copy-start(bf16[256,4096]{1,0:T(8,128)(2,1)} %param.16) | copy-start | bytes 6291460
  7.2 142.5 %all-gather.7.cloned.1.call-start = ((), (), s32[]{:S(2)}) async-start(), calls=%async_computation.4 | async-start | bytes 2228224 | tf_op jit(solution)/shard_map/all_gather | solution.py:41
  9.0 147.1 %all-gather.5.cloned.1.call-start = ((), (), s32[]{:S(2)}) async-start(), calls=%async_computation.3 | async-start | bytes 2228224 | tf_op jit(solution)/shard_map/all_gather | solution.py:40
  11.9 10.6 %all-to-all-start = ((f32[16,1,256]{2,1,0:T(1,128)}), f32[16,1,256]{2,1,0:T(1,128)S(1)}, u32[]{:S(2)}, u32[]{:S(2)}) async-start(f32[16,1,256]{2,1,0:T(1,128)} %broadcast_in_dim.19), calls=%async_computation | async-start | bytes 32768 | tf_op jit(solution)/shard_map/all_to_all | solution.py:69
  31.8 7.2 %copy-start.8 = (s32[2,1,128]{2,1,0:T(1,128)S(1)}, s32[2,1,128]{2,1,0:T(1,128)}, u32[]{:S(2)}) copy-start(s32[2,1,128]{2,1,0:T(1,128)} %param.10) | copy-start | bytes 3076
  31.8 30.4 %all-to-all-start.1 = ((bf16[16,64,512]{2,1,0:T(8,128)(2,1)}), bf16[16,64,512]{2,1,0:T(8,128)(2,1)S(1)}, u32[]{:S(2)}, u32[]{:S(2)}) async-start(bf16[16,64,512]{2,1,0:T(8,128)(2,1)} %bitcast.103), calls=%async_computation.1 | async-start | bytes 2097152 | tf_op jit(solution)/shard_map/all_to_all | solution.py:77
  38.9 145.2 %all-gather.9.cloned.1.call-start = ((), (), s32[]{:S(2)}) async-start(), calls=%async_computation.6 | async-start | bytes 4456448 | tf_op jit(solution)/shard_map/all_gather | solution.py:84
  64.1 254.0 %reduce-scatter.2.cloned.1.call-start = ((), (), s32[]{:S(2)}) async-start(), calls=%async_computation.5 | async-start | bytes 8912896 | tf_op jit(solution)/shard_map/reduce_scatter | solution.py:168
  65.2 19.3 %collective-permute-start = (bf16[512,512]{1,0:T(8,128)(2,1)S(1)}, bf16[512,512]{1,0:T(8,128)(2,1)S(1)}, u32[]{:S(2)}, u32[]{:S(2)}) collective-permute-start(bf16[512,512]{1,0:T(8,128)(2,1)S(1)} %fusion.46), channel_id=1, source_target_pairs={{0,1},{1,0},{2,3},{3,2},{4,5},{5,4},{6,7},{7,6},{8,9},{9,8},{10,11... | collective-permute-start | bytes 1572872 | tf_op jit(solution)/shard_map/ppermute | solution.py:46
  84.5 12.2 %copy-start.7 = (bf16[512,512]{1,0:T(8,128)(2,1)}, bf16[512,512]{1,0:T(8,128)(2,1)S(1)}, u32[]{:S(2)}) copy-start(bf16[512,512]{1,0:T(8,128)(2,1)S(1)} %collective-permute-done) | copy-start | bytes 1572868
  84.5 34.3 %collective-permute-start.1 = (bf16[1,512,512]{2,1,0:T(8,128)(2,1)S(1)}, bf16[1,512,512]{2,1,0:T(8,128)(2,1)}, u32[]{:S(2)}, u32[]{:S(2)}) collective-permute-start(bf16[1,512,512]{2,1,0:T(8,128)(2,1)S(1)} %bitcast.109), channel_id=1, source_target_pairs={{0,128},{32,160},{64,192},{96,224},{128,0},{160,32},{192,64},{224,... | collective-permute-start | bytes 1572872 | tf_op jit(solution)/shard_map/ppermute | solution.py:51
  120.6 25.9 %collective-permute-start.2 = (bf16[2,512,512]{2,1,0:T(8,128)(2,1)S(1)}, bf16[2,512,512]{2,1,0:T(8,128)(2,1)}, u32[]{:S(2)}, u32[]{:S(2)}) collective-permute-start(bf16[2,512,512]{2,1,0:T(8,128)(2,1)S(1)} %maximum_select_fusion.3), channel_id=1, source_target_pairs={{0,64},{32,96},{64,0},{96,32},{128,192},{160,224},{192,128},{224,1... | collective-permute-start | bytes 3145736 | tf_op jit(solution)/shard_map/ppermute | solution.py:51
  123.0 26.7 %copy-start.9 = (s32[2]{0:T(128)S(1)}, s32[2]{0:T(128)}, u32[]{:S(2)}) copy-start(s32[2]{0:T(128)} %param.11) | copy-start | bytes 28
  149.7 22.6 %collective-permute-start.3 = (bf16[4,512,512]{2,1,0:T(8,128)(2,1)}, bf16[4,512,512]{2,1,0:T(8,128)(2,1)}, u32[]{:S(2)}, u32[]{:S(2)}) collective-permute-start(bf16[4,512,512]{2,1,0:T(8,128)(2,1)} %maximum_select_fusion.2), channel_id=1, source_target_pairs={{0,32},{32,0},{64,96},{96,64},{128,160},{160,128},{192,224},{224,1... | collective-permute-start | bytes 6291464 | tf_op jit(solution)/shard_map/ppermute | solution.py:51
  151.8 11.4 %collective-permute-start.7 = (f32[128,256]{1,0:T(8,128)S(1)}, f32[128,256]{1,0:T(8,128)S(1)}, u32[]{:S(2)}, u32[]{:S(2)}) collective-permute-start(f32[128,256]{1,0:T(8,128)S(1)} %fusion.41), channel_id=1, source_target_pairs={{0,1},{1,0},{2,3},{3,2},{4,5},{5,4},{6,7},{7,6},{8,9},{9,8},{10,11... | collective-permute-start | bytes 393224 | tf_op jit(solution)/shard_map/ppermute | solution.py:34
  158.4 13.8 %collective-permute-start.4 = (f32[128,256]{1,0:T(8,128)S(1)}, f32[128,256]{1,0:T(8,128)S(1)}, u32[]{:S(2)}, u32[]{:S(2)}) collective-permute-start(f32[128,256]{1,0:T(8,128)S(1)} %fusion.43), channel_id=1, source_target_pairs={{0,1},{1,0},{2,3},{3,2},{4,5},{5,4},{6,7},{7,6},{8,9},{9,8},{10,11... | collective-permute-start | bytes 393224 | tf_op jit(solution)/shard_map/ppermute | solution.py:34
  184.1 3.4 copy-start.3
  190.0 3.5 copy-start.4
  196.1 8.1 %collective-permute-start.6 = (f32[2,2,64]{2,1,0:T(2,128)S(1)}, f32[2,2,64]{2,1,0:T(2,128)S(1)}, u32[]{:S(2)}, u32[]{:S(2)}) collective-permute-start(f32[2,2,64]{2,1,0:T(2,128)S(1)} %get-tuple-element.26), channel_id=1, source_target_pairs={{0,1},{1,0},{2,3},{3,2},{4,5},{5,4},{6,7},{7,6},{8,9},{9,8},{10,11... | collective-permute-start | bytes 3080 | tf_op jit(solution)/shard_map/ppermute | solution.py:34
  198.5 10.9 %collective-permute-start.5 = (f32[2,64,2,128]{3,1,2,0:T(8,128)S(1)}, f32[2,64,2,128]{3,1,2,0:T(8,128)S(1)}, u32[]{:S(2)}, u32[]{:S(2)}) collective-permute-start(f32[2,64,2,128]{3,1,2,0:T(8,128)S(1)} %convolution_bitcast_fusion.1), channel_id=1, source_target_pairs={{0,1},{1,0},{2,3},{3,2},{4,5},{5,4},{6,7},{7,6},{8,9},{9,8},{10,11... | collective-permute-start | bytes 393224 | tf_op jit(solution)/shard_map/ppermute | solution.py:34
  210.3 2.5 copy-start.1
  212.8 4.8 %copy-start.5 = (bf16[2,2,2,512,512]{4,3,2,1,0:T(8,128)(2,1)S(1)}, bf16[2,2,2,512,512]{4,3,2,1,0:T(8,128)(2,1)}, u32[]{:S(2)}) copy-start(bf16[2,2,2,512,512]{4,3,2,1,0:T(8,128)(2,1)} %copy.75) | copy-start | bytes 12582916
  213.6 10.3 %collective-permute-start.8 = (f32[2,64,2,128]{3,1,2,0:T(8,128)S(1)}, f32[2,64,2,128]{3,1,2,0:T(8,128)S(1)}, u32[]{:S(2)}, u32[]{:S(2)}) collective-permute-start(f32[2,64,2,128]{3,1,2,0:T(8,128)S(1)} %convolution_bitcast_fusion), channel_id=1, source_target_pairs={{0,1},{1,0},{2,3},{3,2},{4,5},{5,4},{6,7},{7,6},{8,9},{9,8},{10,11... | collective-permute-start | bytes 393224 | tf_op jit(solution)/shard_map/ppermute | solution.py:34
  217.6 1.6 copy-start.2
  221.0 3.1 copy-start.6
  319.0 16.0 %collective-permute-start.9 = (bf16[256,512]{1,0:T(8,128)(2,1)S(1)}, bf16[256,512]{1,0:T(8,128)(2,1)S(1)}, u32[]{:S(2)}, u32[]{:S(2)}) collective-permute-start(bf16[256,512]{1,0:T(8,128)(2,1)S(1)} %slice.60), channel_id=1, source_target_pairs={{0,1},{1,0},{2,3},{3,2},{4,5},{5,4},{6,7},{7,6},{8,9},{9,8},{10,11... | collective-permute-start | bytes 786440 | tf_op jit(solution)/shard_map/ppermute | solution.py:170
Sparse Core Ops, SparseCore 0:
  10.4 53.4 all-gather.6
  66.9 52.0 all-gather.4
  122.0 62.0 all-gather.8
  229.4 88.6 reduce-scatter.1

commit v11 on v10

--- a/solution.py
+++ b/solution.py
@@ -36,10 +36,31 @@
     pad_rows = jnp.zeros((tail_rows, hidden.shape[1]), jnp.bfloat16)
     query_rows = jnp.concatenate([hidden[tail_rows:], pad_rows], 0)
     grad_rows = jnp.concatenate([grad_out[tail_rows:], pad_rows], 0)
-    full_query, full_grad = (
-        lax.all_gather(query_rows, "mp", axis=1, tiled=True),
-        lax.all_gather(grad_rows, "mp", axis=1, tiled=True),
-    )
+    n_mp = lax.axis_size("mp")
+    me_mp = lax.axis_index("mp")
+    rows2 = jnp.stack([query_rows, grad_rows])
+    across = lax.ppermute(rows2, "mp", [(i, i ^ (n_mp // 2)) for i in range(n_mp)])
+    held_rows = jnp.where(me_mp // (n_mp // 2) == me_group, rows2, across)[None]
+    bit = n_mp // 4
+    while bit >= 1:
+        pairs = [(i, i ^ bit) for i in range(n_mp)]
+        other = lax.ppermute(held_rows, "mp", pairs)
+        low = (me_mp // bit) % 2 == 0
+        held_rows = jnp.where(
+            low,
+            jnp.concatenate([held_rows, other], 0),
+            jnp.concatenate([other, held_rows], 0),
+        )
+        bit //= 2
+    m_bits = (n_mp // 2).bit_length() - 1
+    held_rows = held_rows.reshape((2,) * m_bits + held_rows.shape[1:])
+    held_rows = jnp.transpose(
+        held_rows, (m_bits,) + tuple(reversed(range(m_bits))) + (m_bits + 1, m_bits + 2)
+    )
+    halves = jnp.transpose(
+        held_rows.reshape((2, n_mp // 2) + held_rows.shape[-2:]), (0, 2, 1, 3)
+    ).reshape(2, rows_here, half)
+    query_half, grad_half = halves[0], halves[1]
     piece_rows = half // lax.axis_size("dp")
     kv_local = jnp.concatenate([w_key, w_value], axis=1)
     kv_piece = lax.dynamic_slice_in_dim(kv_local, me_dp * piece_rows, piece_rows, 0)
@@ -89,7 +110,7 @@
     def other_half(x):
         return lax.dynamic_slice_in_dim(x, (1 - me_group) * half, half, 1)
 
-    query_part = jnp.dot(this_half(full_query), w_query, preferred_element_type=jnp.float32)
+    query_part = jnp.dot(query_half, w_query, preferred_element_type=jnp.float32)
     query = group_sum(query_part).astype(jnp.bfloat16)
     n_here, n_there = this_half(neighbours), other_half(neighbours)
     keys = (
@@ -128,7 +149,7 @@
         )
 
     out_term = jnp.dot(attn_bf, w_out, preferred_element_type=jnp.float32)
-    d_attn_part = contract(this_half(full_grad), w_out)
+    d_attn_part = contract(grad_half, w_out)
     d_attn = group_sum(d_attn_part).astype(jnp.bfloat16)
     d_block = d_attn.reshape(blocks_here, BLOCK, heads_here, HD)
     prob = weights / total[..., None]

time: 348 us -> 362 us (1.040)
  other arithmetic: 20.1 us -> 29 us
  starting transfers between devices: 51.3 us -> 59.8 us
  waiting for transfers between devices: 216 us -> 212 us
    ppermute x0 -> x4, waiting for transfers between devices: none -> 29.8 us  [the longest x3 29.8 us: per_device(): other = lax.ppermute(held_rows, 'mp', pairs)]
    ppermute x3, waiting for transfers between devices: 45.6 us -> 21.3 us  [per_device(): other = lax.ppermute(held, 'dp', pairs)]
    ppermute x0 -> x4, starting transfers between devices: none -> 9.51 us  [the longest x3 6.4 us: per_device(): other = lax.ppermute(held_rows, 'mp', pairs)]
    select_n x0 -> x3, other arithmetic: none -> 7.28 us  [per_device(): jnp.where(low, jnp.concatenate([held_rows, other], 0), jnp.concatenate([o...]
    all_gather x1, waiting for transfers between devices: 5.56 us -> 0.01 us  [per_device(): neighbours = lax.all_gather(own_cols, 'mp', axis=1, tiled=True)]
    slice x1 -> x4, local copies, waits for them, and re-layouts: 0.18 us -> 4.97 us  [the longest x3 4.79 us: per_device(): query_half, grad_half = (halves[0], halves[1])]
  transfers between devices with their start and end apart: 16 -> 18, of which waited for: 13 -> 14; matrix products, arithmetic and copies ran while one was open for 10% -> 9% of each run, Pallas kernels for 0% -> 0%
where the time goes in v11:
time: 362 us; the launch traced here: 359 us
  waiting for transfers between devices  212 us (59%)
  starting transfers between devices  59.8 us (17%)
  other arithmetic  29 us (8%)
  local copies, waits for them, and re-layouts  22.7 us (6%)
  matrix products  21.1 us (6%)
  between operations  14.5 us (4%)
    reduce_scatter x1, waiting for transfers between devices, per_device(): reduced = lax.psum_scatter(stacked, 'mp', scatter_dimension=1, tiled=True)  90.5 us
    ppermute x3, waiting for transfers between devices, per_device(): other = lax.ppermute(held_rows, 'mp', pairs)  29.8 us
    all_to_all x1, waiting for transfers between devices, per_device(): recv_buf = lax.all_to_all(send_buf, ('dp', 'group'), 0, 0, tiled=True)  22.2 us
    ppermute x3, waiting for transfers between devices, per_device(): other = lax.ppermute(held, 'dp', pairs)  21.3 us
    ppermute x5, waiting for transfers between devices, group_sum(): return x + lax.ppermute(x, 'group', swap)  18 us
    ppermute x5, starting transfers between devices, group_sum(): return x + lax.ppermute(x, 'group', swap)  15.4 us
    ppermute x3, starting transfers between devices, per_device(): other = lax.ppermute(held, 'dp', pairs)  14.6 us
    ppermute x1, waiting for transfers between devices, per_device(): lax.ppermute(both_cols, 'group', swap)  14.2 us
  transfers between devices with their start and end apart: 18, of which 14 were waited for; matrix products, arithmetic and copies ran while one was open for 9% of the time, Pallas kernels for 0%

profile of v11, /device:TPU:192, one launch (start us, length us, event | category | flops | bytes accessed | tf_op | source)
XLA Modules:
  0.0 358.9 jit_solution(13112696260809005215)
XLA Ops:
  8.6 6.3 %all-to-all-start = ((f32[16,1,256]{2,1,0:T(1,128)}), f32[16,1,256]{2,1,0:T(1,128)S(1)}, u32[]{:S(2)}, u32[]{:S(2)}) async-start(f32[16,1,256]{2,1,0:T(1,128)} %broadcast_in_dim.21), calls=%async_computation | async-start | bytes 32768 | tf_op jit(solution)/shard_map/all_to_all | solution.py:90
  14.9 4.2 %all-to-all-done = f32[16,1,256]{2,1,0:T(1,128)S(1)} async-done(((f32[16,1,256]{2,1,0:T(1,128)}), f32[16,1,256]{2,1,0:T(1,128)S(1)}, u32[]{:S(2)}, u32[]{:S(2)}) %all-to-all-start) | async-done | bytes 16416 | tf_op jit(solution)/shard_map/all_to_all | solution.py:90
  20.6 7.8 %gather_fusion = bf16[1024,512]{1,0:T(8,128)(2,1)} fusion(bf16[4096,512]{1,0:T(8,128)(2,1)} %param.12, s32[1024]{0:T(1024)S(1)} %broadcast_clamp_fusion), kind=kCustom, calls=%fused_computation | custom fusion | bytes 2101248 | tf_op jit(solution)/shard_map/gather | solution.py:97
  28.5 7.2 %all-to-all-start.1 = ((bf16[16,64,512]{2,1,0:T(8,128)(2,1)}), bf16[16,64,512]{2,1,0:T(8,128)(2,1)S(1)}, u32[]{:S(2)}, u32[]{:S(2)}) async-start(bf16[16,64,512]{2,1,0:T(8,128)(2,1)} %bitcast.121), calls=%async_computation.1 | async-start | bytes 2097152 | tf_op jit(solution)/shard_map/all_to_all | solution.py:98
  36.7 22.2 %all-to-all-done.1 = bf16[16,64,512]{2,1,0:T(8,128)(2,1)S(1)} async-done(((bf16[16,64,512]{2,1,0:T(8,128)(2,1)}), bf16[16,64,512]{2,1,0:T(8,128)(2,1)S(1)}, u32[]{:S(2)}, u32[]{:S(2)}) %all-to-all-start.1) | async-done | bytes 1048608 | tf_op jit(solution)/shard_map/all_to_all | solution.py:98
  62.0 4.6 %collective-permute-start = (bf16[512,512]{1,0:T(8,128)(2,1)S(1)}, bf16[512,512]{1,0:T(8,128)(2,1)S(1)}, u32[]{:S(2)}, u32[]{:S(2)}) collective-permute-start(bf16[512,512]{1,0:T(8,128)(2,1)S(1)} %fusion.42), channel_id=1, source_target_pairs={{0,1},{1,0},{2,3},{3,2},{4,5},{5,4},{6,7},{7,6},{8,9},{9,8},{10,11... | collective-permute-start | bytes 1572872 | tf_op jit(solution)/shard_map/ppermute | solution.py:67
  66.7 3.1 collective-permute-start.4
  69.8 11.5 %collective-permute-done = bf16[512,512]{1,0:T(8,128)(2,1)S(1)} collective-permute-done((bf16[512,512]{1,0:T(8,128)(2,1)S(1)}, bf16[512,512]{1,0:T(8,128)(2,1)S(1)}, u32[]{:S(2)}, u32[]{:S(2)}) %collective-permute-start) | collective-permute-done | bytes 524320 | tf_op jit(solution)/shard_map/ppermute | solution.py:67
  81.3 12.2 %collective-permute-start.1 = (bf16[1,512,512]{2,1,0:T(8,128)(2,1)S(1)}, bf16[1,512,512]{2,1,0:T(8,128)(2,1)}, u32[]{:S(2)}, u32[]{:S(2)}) collective-permute-start(bf16[1,512,512]{2,1,0:T(8,128)(2,1)S(1)} %bitcast.129), channel_id=1, source_target_pairs={{0,128},{32,160},{64,192},{96,224},{128,0},{160,32},{192,64},{224,... | collective-permute-start | bytes 1572872 | tf_op jit(solution)/shard_map/ppermute | solution.py:72
  96.1 19.5 %collective-permute-done.1 = bf16[1,512,512]{2,1,0:T(8,128)(2,1)} collective-permute-done((bf16[1,512,512]{2,1,0:T(8,128)(2,1)S(1)}, bf16[1,512,512]{2,1,0:T(8,128)(2,1)}, u32[]{:S(2)}, u32[]{:S(2)}) %collective-permute-start.1) | collective-permute-done | bytes 524320 | tf_op jit(solution)/shard_map/ppermute | solution.py:72
  121.7 3.2 collective-permute-start.6
  124.9 12.2 %collective-permute-done.6 = bf16[2,2,128,512]{3,2,1,0:T(8,128)(2,1)} collective-permute-done((bf16[2,2,128,512]{3,2,1,0:T(8,128)(2,1)}, bf16[2,2,128,512]{3,2,1,0:T(8,128)(2,1)}, u32[]{:S(2)}, u32[]{:S(2)}) %collective-permute-start.6) | collective-permute-done | bytes 524320 | tf_op jit(solution)/shard_map/ppermute | solution.py:47
  137.1 2.7 maximum_select_fusion.4
  143.2 3.2 maximum_select_fusion.3
  146.5 17.6 %collective-permute-done.7 = bf16[4,2,128,512]{3,2,1,0:T(8,128)(2,1)} collective-permute-done((bf16[4,2,128,512]{3,2,1,0:T(8,128)(2,1)}, bf16[4,2,128,512]{3,2,1,0:T(8,128)(2,1)}, u32[]{:S(2)}, u32[]{:S(2)}) %collective-permute-start.7) | collective-permute-done | bytes 1048608 | tf_op jit(solution)/shard_map/ppermute | solution.py:47
  164.1 2.6 maximum_select_fusion.2
  172.1 4.3 %collective-permute-start.8 = (f32[128,256]{1,0:T(8,128)S(1)}, f32[128,256]{1,0:T(8,128)S(1)}, u32[]{:S(2)}, u32[]{:S(2)}) collective-permute-start(f32[128,256]{1,0:T(8,128)S(1)} %fusion.78), channel_id=1, source_target_pairs={{0,1},{1,0},{2,3},{3,2},{4,5},{5,4},{6,7},{7,6},{8,9},{9,8},{10,11... | collective-permute-start | bytes 393224 | tf_op jit(solution)/shard_map/ppermute | solution.py:34
  180.9 2.9 collective-permute-done.8
  183.8 5.9 %collective-permute-done.11 = f32[128,256]{1,0:T(8,128)S(1)} collective-permute-done((f32[128,256]{1,0:T(8,128)S(1)}, f32[128,256]{1,0:T(8,128)S(1)}, u32[]{:S(2)}, u32[]{:S(2)}) %collective-permute-start.11) | collective-permute-done | bytes 131104 | tf_op jit(solution)/shard_map/ppermute | solution.py:34
  189.8 4.0 %maximum_select_fusion.1 = bf16[8,512,512]{2,1,0:T(8,128)(2,1)S(1)} fusion(bf16[4,512,512]{2,1,0:T(8,128)(2,1)} %collective-permute-done.3, bf16[4,512,512]{2,1,0:T(8,128)(2,1)} %maximum_select_fusion.3, pred[]{:T(512)S(6)} %eq.77), kind=kLoop, calls=%fused_computation.11 | loop fusion | flops 6291456 | bytes 8388609 | tf_op jit(solution)/shard_map/jit(_where)/select_n | solution.py:74
  193.7 2.4 copy.83
  196.2 3.1 fusion.12
  202.0 3.1 fusion.10
  208.1 3.7 %collective-permute-start.10 = (f32[2,2,64]{2,1,0:T(2,128)S(1)}, f32[2,2,64]{2,1,0:T(2,128)S(1)}, u32[]{:S(2)}, u32[]{:S(2)}) collective-permute-start(f32[2,2,64]{2,1,0:T(2,128)S(1)} %get-tuple-element.28), channel_id=1, source_target_pairs={{0,1},{1,0},{2,3},{3,2},{4,5},{5,4},{6,7},{7,6},{8,9},{9,8},{10,11... | collective-permute-start | bytes 3080 | tf_op jit(solution)/shard_map/ppermute | solution.py:34
  212.0 2.4 collective-permute-start.9
  216.3 5.3 %collective-permute-done.9 = f32[2,64,2,128]{3,1,2,0:T(8,128)S(1)} collective-permute-done((f32[2,64,2,128]{3,1,2,0:T(8,128)S(1)}, f32[2,64,2,128]{3,1,2,0:T(8,128)S(1)}, u32[]{:S(2)}, u32[]{:S(2)}) %collective-permute-start.9) | collective-permute-done | bytes 131104 | tf_op jit(solution)/shard_map/ppermute | solution.py:34
  222.6 2.5 fusion.4
  225.9 3.0 collective-permute-start.12
  233.2 2.4 collective-permute-done.12
  237.0 3.9 %pad_maximum_fusion = bf16[512,8192]{1,0:T(8,128)(2,1)} fusion(bf16[256,8192]{1,0:T(8,128)(2,1)S(1)} %fusion, bf16[128,8192]{1,0:T(8,128)(2,1)S(1)} %pad_select_fusion, bf16[128,8192]{1,0:T(8,128)(2,1)S(1)} %pad_select_fusion.1), kind=kLoop, calls=%fused_computation.4 | loop fusion | flops 25165824 | bytes 16777216 | tf_op jit(solution)/shard_map/concatenate | solution.py:181
  240.9 90.5 %reduce-scatter.2.cloned.1.call-done = bf16[512,512]{1,0:T(8,128)(2,1)} async-done(((bf16[512,8192]{1,0:T(8,128)(2,1)}), bf16[512,512]{1,0:T(8,128)(2,1)}) %reduce-scatter.2.cloned.1.call-update) | async-done | bytes 524304 | tf_op jit(solution)/shard_map/reduce_scatter | solution.py:189
  334.4 14.2 %collective-permute-done.13 = bf16[256,512]{1,0:T(8,128)(2,1)S(1)} collective-permute-done((bf16[256,512]{1,0:T(8,128)(2,1)S(1)}, bf16[256,512]{1,0:T(8,128)(2,1)S(1)}, u32[]{:S(2)}, u32[]{:S(2)}) %collective-permute-start.13) | collective-permute-done | bytes 262176 | tf_op jit(solution)/shard_map/ppermute | solution.py:191
  (117 shorter events, 50.4 us)
Async XLA Ops:
  7.2 170.9 %copy-start = (bf16[256,4096]{1,0:T(8,128)(2,1)S(1)}, bf16[256,4096]{1,0:T(8,128)(2,1)}, u32[]{:S(2)}) copy-start(bf16[256,4096]{1,0:T(8,128)(2,1)} %param.16) | copy-start | bytes 6291460
  8.6 10.6 %all-to-all-start = ((f32[16,1,256]{2,1,0:T(1,128)}), f32[16,1,256]{2,1,0:T(1,128)S(1)}, u32[]{:S(2)}, u32[]{:S(2)}) async-start(f32[16,1,256]{2,1,0:T(1,128)} %broadcast_in_dim.21), calls=%async_computation | async-start | bytes 32768 | tf_op jit(solution)/shard_map/all_to_all | solution.py:90
  28.4 7.3 %copy-start.10 = (s32[2,1,128]{2,1,0:T(1,128)S(1)}, s32[2,1,128]{2,1,0:T(1,128)}, u32[]{:S(2)}) copy-start(s32[2,1,128]{2,1,0:T(1,128)} %param.10) | copy-start | bytes 3076
  28.5 30.5 %all-to-all-start.1 = ((bf16[16,64,512]{2,1,0:T(8,128)(2,1)}), bf16[16,64,512]{2,1,0:T(8,128)(2,1)S(1)}, u32[]{:S(2)}, u32[]{:S(2)}) async-start(bf16[16,64,512]{2,1,0:T(8,128)(2,1)} %bitcast.121), calls=%async_computation.1 | async-start | bytes 2097152 | tf_op jit(solution)/shard_map/all_to_all | solution.py:98
  35.7 160.5 %all-gather.3.cloned.1.call-start = ((), (), s32[]{:S(2)}) async-start(), calls=%async_computation.4 | async-start | bytes 4456448 | tf_op jit(solution)/shard_map/all_gather | solution.py:105
  60.8 270.6 %reduce-scatter.2.cloned.1.call-start = ((), (), s32[]{:S(2)}) async-start(), calls=%async_computation.3 | async-start | bytes 8912896 | tf_op jit(solution)/shard_map/reduce_scatter | solution.py:189
  60.9 5.7 %copy-start.8 = (bf16[128,512]{1,0:T(8,128)(2,1)S(1)}, bf16[128,512]{1,0:T(8,128)(2,1)}, u32[]{:S(2)}) copy-start(bf16[128,512]{1,0:T(8,128)(2,1)} %param.9) | copy-start | bytes 393220
  60.9 5.8 %copy-start.9 = (bf16[128,512]{1,0:T(8,128)(2,1)S(1)}, bf16[128,512]{1,0:T(8,128)(2,1)}, u32[]{:S(2)}) copy-start(bf16[128,512]{1,0:T(8,128)(2,1)} %param.17) | copy-start | bytes 393220
  62.0 19.3 %collective-permute-start = (bf16[512,512]{1,0:T(8,128)(2,1)S(1)}, bf16[512,512]{1,0:T(8,128)(2,1)S(1)}, u32[]{:S(2)}, u32[]{:S(2)}) collective-permute-start(bf16[512,512]{1,0:T(8,128)(2,1)S(1)} %fusion.42), channel_id=1, source_target_pairs={{0,1},{1,0},{2,3},{3,2},{4,5},{5,4},{6,7},{7,6},{8,9},{9,8},{10,11... | collective-permute-start | bytes 1572872 | tf_op jit(solution)/shard_map/ppermute | solution.py:67
  66.7 26.8 %collective-permute-start.4 = (bf16[2,128,512]{2,1,0:T(8,128)(2,1)S(1)}, bf16[2,128,512]{2,1,0:T(8,128)(2,1)}, u32[]{:S(2)}, u32[]{:S(2)}) collective-permute-start(bf16[2,128,512]{2,1,0:T(8,128)(2,1)S(1)} %pad_maximum_fusion.1), channel_id=1, source_target_pairs={{0,16},{2,18},{4,20},{6,22},{8,24},{10,26},{12,28},{14,30},{16,0},... | collective-permute-start | bytes 786440 | tf_op jit(solution)/shard_map/ppermute | solution.py:42
  81.3 14.8 %copy-start.7 = (bf16[512,512]{1,0:T(8,128)(2,1)}, bf16[512,512]{1,0:T(8,128)(2,1)S(1)}, u32[]{:S(2)}) copy-start(bf16[512,512]{1,0:T(8,128)(2,1)S(1)} %collective-permute-done) | copy-start | bytes 1572868
  81.3 34.3 %collective-permute-start.1 = (bf16[1,512,512]{2,1,0:T(8,128)(2,1)S(1)}, bf16[1,512,512]{2,1,0:T(8,128)(2,1)}, u32[]{:S(2)}, u32[]{:S(2)}) collective-permute-start(bf16[1,512,512]{2,1,0:T(8,128)(2,1)S(1)} %bitcast.129), channel_id=1, source_target_pairs={{0,128},{32,160},{64,192},{96,224},{128,0},{160,32},{192,64},{224,... | collective-permute-start | bytes 1572872 | tf_op jit(solution)/shard_map/ppermute | solution.py:72
  94.5 25.2 %collective-permute-start.5 = (bf16[1,2,128,512]{3,2,1,0:T(8,128)(2,1)S(1)}, bf16[1,2,128,512]{3,2,1,0:T(8,128)(2,1)}, u32[]{:S(2)}, u32[]{:S(2)}) collective-permute-start(bf16[1,2,128,512]{3,2,1,0:T(8,128)(2,1)S(1)} %select_bitcast_fusion), channel_id=1, source_target_pairs={{0,8},{2,10},{4,12},{6,14},{8,0},{10,2},{12,4},{14,6},{16,24},{18,... | collective-permute-start | bytes 786440 | tf_op jit(solution)/shard_map/ppermute | solution.py:47
  117.4 25.9 %collective-permute-start.2 = (bf16[2,512,512]{2,1,0:T(8,128)(2,1)S(1)}, bf16[2,512,512]{2,1,0:T(8,128)(2,1)}, u32[]{:S(2)}, u32[]{:S(2)}) collective-permute-start(bf16[2,512,512]{2,1,0:T(8,128)(2,1)S(1)} %maximum_select_fusion.5), channel_id=1, source_target_pairs={{0,64},{32,96},{64,0},{96,32},{128,192},{160,224},{192,128},{224,1... | collective-permute-start | bytes 3145736 | tf_op jit(solution)/shard_map/ppermute | solution.py:72
  121.7 15.4 %collective-permute-start.6 = (bf16[2,2,128,512]{3,2,1,0:T(8,128)(2,1)}, bf16[2,2,128,512]{3,2,1,0:T(8,128)(2,1)}, u32[]{:S(2)}, u32[]{:S(2)}) collective-permute-start(bf16[2,2,128,512]{3,2,1,0:T(8,128)(2,1)} %maximum_select_fusion.6), channel_id=1, source_target_pairs={{0,4},{2,6},{4,0},{6,2},{8,12},{10,14},{12,8},{14,10},{16,20},{18,... | collective-permute-start | bytes 1572872 | tf_op jit(solution)/shard_map/ppermute | solution.py:47
  139.8 24.2 %collective-permute-start.7 = (bf16[4,2,128,512]{3,2,1,0:T(8,128)(2,1)}, bf16[4,2,128,512]{3,2,1,0:T(8,128)(2,1)}, u32[]{:S(2)}, u32[]{:S(2)}) collective-permute-start(bf16[4,2,128,512]{3,2,1,0:T(8,128)(2,1)} %maximum_select_fusion.4), channel_id=1, source_target_pairs={{0,2},{2,0},{4,6},{6,4},{8,10},{10,8},{12,14},{14,12},{16,18},{18,... | collective-permute-start | bytes 3145736 | tf_op jit(solution)/shard_map/ppermute | solution.py:47
  141.5 5.0 %copy-start.11 = (s32[2]{0:T(128)S(1)}, s32[2]{0:T(128)}, u32[]{:S(2)}) copy-start(s32[2]{0:T(128)} %param.11) | copy-start | bytes 28
  146.5 43.3 %collective-permute-start.3 = (bf16[4,512,512]{2,1,0:T(8,128)(2,1)}, bf16[4,512,512]{2,1,0:T(8,128)(2,1)}, u32[]{:S(2)}, u32[]{:S(2)}) collective-permute-start(bf16[4,512,512]{2,1,0:T(8,128)(2,1)} %maximum_select_fusion.3), channel_id=1, source_target_pairs={{0,32},{32,0},{64,96},{96,64},{128,160},{160,128},{192,224},{224,1... | collective-permute-start | bytes 6291464 | tf_op jit(solution)/shard_map/ppermute | solution.py:72
  172.1 11.6 %collective-permute-start.8 = (f32[128,256]{1,0:T(8,128)S(1)}, f32[128,256]{1,0:T(8,128)S(1)}, u32[]{:S(2)}, u32[]{:S(2)}) collective-permute-start(f32[128,256]{1,0:T(8,128)S(1)} %fusion.78), channel_id=1, source_target_pairs={{0,1},{1,0},{2,3},{3,2},{4,5},{5,4},{6,7},{7,6},{8,9},{9,8},{10,11... | collective-permute-start | bytes 393224 | tf_op jit(solution)/shard_map/ppermute | solution.py:34
  178.9 10.8 %collective-permute-start.11 = (f32[128,256]{1,0:T(8,128)S(1)}, f32[128,256]{1,0:T(8,128)S(1)}, u32[]{:S(2)}, u32[]{:S(2)}) collective-permute-start(f32[128,256]{1,0:T(8,128)S(1)} %fusion.79), channel_id=1, source_target_pairs={{0,1},{1,0},{2,3},{3,2},{4,5},{5,4},{6,7},{7,6},{8,9},{9,8},{10,11... | collective-permute-start | bytes 393224 | tf_op jit(solution)/shard_map/ppermute | solution.py:34
  196.2 3.4 copy-start.3
  202.0 3.5 copy-start.4
  208.1 7.8 %collective-permute-start.10 = (f32[2,2,64]{2,1,0:T(2,128)S(1)}, f32[2,2,64]{2,1,0:T(2,128)S(1)}, u32[]{:S(2)}, u32[]{:S(2)}) collective-permute-start(f32[2,2,64]{2,1,0:T(2,128)S(1)} %get-tuple-element.28), channel_id=1, source_target_pairs={{0,1},{1,0},{2,3},{3,2},{4,5},{5,4},{6,7},{7,6},{8,9},{9,8},{10,11... | collective-permute-start | bytes 3080 | tf_op jit(solution)/shard_map/ppermute | solution.py:34
  212.0 9.7 %collective-permute-start.9 = (f32[2,64,2,128]{3,1,2,0:T(8,128)S(1)}, f32[2,64,2,128]{3,1,2,0:T(8,128)S(1)}, u32[]{:S(2)}, u32[]{:S(2)}) collective-permute-start(f32[2,64,2,128]{3,1,2,0:T(8,128)S(1)} %convolution_bitcast_fusion.1), channel_id=1, source_target_pairs={{0,1},{1,0},{2,3},{3,2},{4,5},{5,4},{6,7},{7,6},{8,9},{9,8},{10,11... | collective-permute-start | bytes 393224 | tf_op jit(solution)/shard_map/ppermute | solution.py:34
  222.6 2.5 copy-start.1
  225.1 4.3 %copy-start.5 = (bf16[2,2,2,512,512]{4,3,2,1,0:T(8,128)(2,1)S(1)}, bf16[2,2,2,512,512]{4,3,2,1,0:T(8,128)(2,1)}, u32[]{:S(2)}) copy-start(bf16[2,2,2,512,512]{4,3,2,1,0:T(8,128)(2,1)} %copy.83) | copy-start | bytes 12582916
  225.9 9.7 %collective-permute-start.12 = (f32[2,64,2,128]{3,1,2,0:T(8,128)S(1)}, f32[2,64,2,128]{3,1,2,0:T(8,128)S(1)}, u32[]{:S(2)}, u32[]{:S(2)}) collective-permute-start(f32[2,64,2,128]{3,1,2,0:T(8,128)S(1)} %convolution_bitcast_fusion), channel_id=1, source_target_pairs={{0,1},{1,0},{2,3},{3,2},{4,5},{5,4},{6,7},{7,6},{8,9},{9,8},{10,11... | collective-permute-start | bytes 393224 | tf_op jit(solution)/shard_map/ppermute | solution.py:34
  229.4 1.6 copy-start.2
  232.8 2.9 copy-start.6
  332.3 16.2 %collective-permute-start.13 = (bf16[256,512]{1,0:T(8,128)(2,1)S(1)}, bf16[256,512]{1,0:T(8,128)(2,1)S(1)}, u32[]{:S(2)}, u32[]{:S(2)}) collective-permute-start(bf16[256,512]{1,0:T(8,128)(2,1)S(1)} %slice.72), channel_id=1, source_target_pairs={{0,1},{1,0},{2,3},{3,2},{4,5},{5,4},{6,7},{7,6},{8,9},{9,8},{10,11... | collective-permute-start | bytes 786440 | tf_op jit(solution)/shard_map/ppermute | solution.py:191
Sparse Core Ops, SparseCore 0:
  60.9 65.2 all-gather.2
  241.0 90.3 reduce-scatter.1

commit v12 on v10

--- a/solution.py
+++ b/solution.py
@@ -36,10 +36,7 @@
     pad_rows = jnp.zeros((tail_rows, hidden.shape[1]), jnp.bfloat16)
     query_rows = jnp.concatenate([hidden[tail_rows:], pad_rows], 0)
     grad_rows = jnp.concatenate([grad_out[tail_rows:], pad_rows], 0)
-    full_query, full_grad = (
-        lax.all_gather(query_rows, "mp", axis=1, tiled=True),
-        lax.all_gather(grad_rows, "mp", axis=1, tiled=True),
-    )
+    full_query = lax.all_gather(query_rows, "mp", axis=1, tiled=True)
     piece_rows = half // lax.axis_size("dp")
     kv_local = jnp.concatenate([w_key, w_value], axis=1)
     kv_piece = lax.dynamic_slice_in_dim(kv_local, me_dp * piece_rows, piece_rows, 0)
@@ -82,6 +79,8 @@
     ) - 1
     own_cols = recv_buf.reshape(owners * cap, -1)[own_owner * cap + own_rank]
     neighbours = lax.all_gather(own_cols, "mp", axis=1, tiled=True)
+    grad_rows, neighbours = lax.optimization_barrier((grad_rows, neighbours))
+    full_grad = lax.all_gather(grad_rows, "mp", axis=1, tiled=True)
 
     def this_half(x):
         return lax.dynamic_slice_in_dim(x, me_group * half, half, 1)

time: 348 us -> 394 us (1.13)
  waiting for transfers between devices: 216 us -> 262 us
    all_gather x2, waiting for transfers between devices: 0.02 us -> 52.5 us  [the longest x1 33.2 us: per_device(): full_query = lax.all_gather(query_rows, 'mp', axis=1, tiled=True)]
    dot_general x6, matrix products: 7.59 us -> 14.5 us  [contract(): lax.dot_general(left, right, (((1,), (1,)), ((), ())), preferred_element_...]
    all_gather x1, waiting for transfers between devices: 5.56 us -> 0.01 us  [per_device(): neighbours = lax.all_gather(own_cols, 'mp', axis=1, tiled=True)]
    unnamed x21 -> x29, local copies, waits for them, and re-layouts: 1.6 us -> 6.16 us
  transfers between devices with their start and end apart: 16 -> 16, of which waited for: 13 -> 11; matrix products, arithmetic and copies ran while one was open for 10% -> 8% of each run, Pallas kernels for 0% -> 0%
where the time goes in v12:
time: 394 us; the launch traced here: 391 us
  waiting for transfers between devices  262 us (66%)
  starting transfers between devices  47.6 us (12%)
  matrix products  25.4 us (6%)
  local copies, waits for them, and re-layouts  21.5 us (5%)
  other arithmetic  20.6 us (5%)
  between operations  14.2 us (4%)
    reduce_scatter x1, waiting for transfers between devices, per_device(): reduced = lax.psum_scatter(stacked, 'mp', scatter_dimension=1, tiled=True)  90.5 us
    ppermute x3, waiting for transfers between devices, per_device(): other = lax.ppermute(held, 'dp', pairs)  45.6 us
    all_gather x1, waiting for transfers between devices, per_device(): full_query = lax.all_gather(query_rows, 'mp', axis=1, tiled=True)  33.2 us
    all_to_all x1, waiting for transfers between devices, per_device(): recv_buf = lax.all_to_all(send_buf, ('dp', 'group'), 0, 0, tiled=True)  22.2 us
    all_gather x1, waiting for transfers between devices, per_device(): full_grad = lax.all_gather(grad_rows, 'mp', axis=1, tiled=True)  19.3 us
    ppermute x5, waiting for transfers between devices, group_sum(): return x + lax.ppermute(x, 'group', swap)  18.1 us
    ppermute x1, waiting for transfers between devices, per_device(): held = lax.ppermute(kv_piece, 'group', swap)[None]  14.7 us
    ppermute x3, starting transfers between devices, per_device(): other = lax.ppermute(held, 'dp', pairs)  14.6 us
  transfers between devices with their start and end apart: 16, of which 11 were waited for; matrix products, arithmetic and copies ran while one was open for 8% of the time, Pallas kernels for 0%

profile of v12, /device:TPU:192, one launch (start us, length us, event | category | flops | bytes accessed | tf_op | source)
XLA Modules:
  0.0 391.5 jit_solution(11407241269646906533)
XLA Ops:
  8.6 6.3 %all-to-all-start = ((f32[16,1,256]{2,1,0:T(1,128)}), f32[16,1,256]{2,1,0:T(1,128)S(1)}, u32[]{:S(2)}, u32[]{:S(2)}) async-start(f32[16,1,256]{2,1,0:T(1,128)} %broadcast_in_dim.19), calls=%async_computation | async-start | bytes 32768 | tf_op jit(solution)/shard_map/all_to_all | solution.py:66
  14.9 4.2 %all-to-all-done = f32[16,1,256]{2,1,0:T(1,128)S(1)} async-done(((f32[16,1,256]{2,1,0:T(1,128)}), f32[16,1,256]{2,1,0:T(1,128)S(1)}, u32[]{:S(2)}, u32[]{:S(2)}) %all-to-all-start) | async-done | bytes 16416 | tf_op jit(solution)/shard_map/all_to_all | solution.py:66
  20.6 7.8 %gather_fusion = bf16[1024,512]{1,0:T(8,128)(2,1)} fusion(bf16[4096,512]{1,0:T(8,128)(2,1)} %param.12, s32[1024]{0:T(1024)S(1)} %broadcast_clamp_fusion), kind=kCustom, calls=%fused_computation | custom fusion | bytes 2101248 | tf_op jit(solution)/shard_map/gather | solution.py:73
  28.5 7.2 %all-to-all-start.1 = ((bf16[16,64,512]{2,1,0:T(8,128)(2,1)}), bf16[16,64,512]{2,1,0:T(8,128)(2,1)S(1)}, u32[]{:S(2)}, u32[]{:S(2)}) async-start(bf16[16,64,512]{2,1,0:T(8,128)(2,1)} %bitcast.103), calls=%async_computation.1 | async-start | bytes 2097152 | tf_op jit(solution)/shard_map/all_to_all | solution.py:74
  36.7 22.2 %all-to-all-done.1 = bf16[16,64,512]{2,1,0:T(8,128)(2,1)S(1)} async-done(((bf16[16,64,512]{2,1,0:T(8,128)(2,1)}), bf16[16,64,512]{2,1,0:T(8,128)(2,1)S(1)}, u32[]{:S(2)}, u32[]{:S(2)}) %all-to-all-start.1) | async-done | bytes 1048608 | tf_op jit(solution)/shard_map/all_to_all | solution.py:74
  62.7 4.6 %collective-permute-start = (bf16[512,512]{1,0:T(8,128)(2,1)S(1)}, bf16[512,512]{1,0:T(8,128)(2,1)S(1)}, u32[]{:S(2)}, u32[]{:S(2)}) collective-permute-start(bf16[512,512]{1,0:T(8,128)(2,1)S(1)} %fusion.46), channel_id=1, source_target_pairs={{0,1},{1,0},{2,3},{3,2},{4,5},{5,4},{6,7},{7,6},{8,9},{9,8},{10,11... | collective-permute-start | bytes 1572872 | tf_op jit(solution)/shard_map/ppermute | solution.py:43
  67.3 14.7 %collective-permute-done = bf16[512,512]{1,0:T(8,128)(2,1)S(1)} collective-permute-done((bf16[512,512]{1,0:T(8,128)(2,1)S(1)}, bf16[512,512]{1,0:T(8,128)(2,1)S(1)}, u32[]{:S(2)}, u32[]{:S(2)}) %collective-permute-start) | collective-permute-done | bytes 524320 | tf_op jit(solution)/shard_map/ppermute | solution.py:43
  82.1 12.2 %collective-permute-start.1 = (bf16[1,512,512]{2,1,0:T(8,128)(2,1)S(1)}, bf16[1,512,512]{2,1,0:T(8,128)(2,1)}, u32[]{:S(2)}, u32[]{:S(2)}) collective-permute-start(bf16[1,512,512]{2,1,0:T(8,128)(2,1)S(1)} %bitcast.109), channel_id=1, source_target_pairs={{0,128},{32,160},{64,192},{96,224},{128,0},{160,32},{192,64},{224,... | collective-permute-start | bytes 1572872 | tf_op jit(solution)/shard_map/ppermute | solution.py:48
  94.3 22.1 %collective-permute-done.1 = bf16[1,512,512]{2,1,0:T(8,128)(2,1)} collective-permute-done((bf16[1,512,512]{2,1,0:T(8,128)(2,1)S(1)}, bf16[1,512,512]{2,1,0:T(8,128)(2,1)}, u32[]{:S(2)}, u32[]{:S(2)}) %collective-permute-start.1) | collective-permute-done | bytes 524320 | tf_op jit(solution)/shard_map/ppermute | solution.py:48
  118.1 2.4 collective-permute-start.2
  120.5 23.5 %collective-permute-done.2 = bf16[2,512,512]{2,1,0:T(8,128)(2,1)} collective-permute-done((bf16[2,512,512]{2,1,0:T(8,128)(2,1)S(1)}, bf16[2,512,512]{2,1,0:T(8,128)(2,1)}, u32[]{:S(2)}, u32[]{:S(2)}) %collective-permute-start.2) | collective-permute-done | bytes 1048608 | tf_op jit(solution)/shard_map/ppermute | solution.py:48
  144.0 3.3 maximum_select_fusion.2
  148.1 33.2 %all-gather.5.cloned.1.call-done = bf16[128,8192]{1,0:T(8,128)(2,1)} async-done(((bf16[128,512]{1,0:T(8,128)(2,1)}), bf16[128,8192]{1,0:T(8,128)(2,1)}) %all-gather.5.cloned.1.call-update) | async-done | bytes 2097168 | tf_op jit(solution)/shard_map/all_gather | solution.py:39
  181.3 2.4 fusion.43
  183.7 2.1 collective-permute-start.4
  185.8 9.1 %collective-permute-done.4 = f32[128,256]{1,0:T(8,128)S(1)} collective-permute-done((f32[128,256]{1,0:T(8,128)S(1)}, f32[128,256]{1,0:T(8,128)S(1)}, u32[]{:S(2)}, u32[]{:S(2)}) %collective-permute-start.4) | collective-permute-done | bytes 131104 | tf_op jit(solution)/shard_map/ppermute | solution.py:34
  194.9 4.1 %maximum_select_fusion.1 = bf16[8,512,512]{2,1,0:T(8,128)(2,1)S(1)} fusion(bf16[4,512,512]{2,1,0:T(8,128)(2,1)} %collective-permute-done.3, bf16[4,512,512]{2,1,0:T(8,128)(2,1)} %maximum_select_fusion.2, pred[]{:T(512)S(6)} %eq.62), kind=kLoop, calls=%fused_computation.11 | loop fusion | flops 6291456 | bytes 8388609 | tf_op jit(solution)/shard_map/jit(_where)/select_n | solution.py:50
  204.6 3.1 fusion.10
  208.1 2.3 fusion.30
  210.8 2.1 collective-permute-start.6
  213.0 4.2 %collective-permute-start.5 = (f32[2,64,2,128]{3,1,2,0:T(8,128)S(1)}, f32[2,64,2,128]{3,1,2,0:T(8,128)S(1)}, u32[]{:S(2)}, u32[]{:S(2)}) collective-permute-start(f32[2,64,2,128]{3,1,2,0:T(8,128)S(1)} %convolution_bitcast_fusion.1), channel_id=1, source_target_pairs={{0,1},{1,0},{2,3},{3,2},{4,5},{5,4},{6,7},{7,6},{8,9},{9,8},{10,11... | collective-permute-start | bytes 393224 | tf_op jit(solution)/shard_map/ppermute | solution.py:34
  217.2 19.3 %all-gather.7.cloned.1.call-done = bf16[128,8192]{1,0:T(8,128)(2,1)} async-done(((bf16[128,512]{1,0:T(8,128)(2,1)}), bf16[128,8192]{1,0:T(8,128)(2,1)}) %all-gather.7.cloned.1.call-update) | async-done | bytes 2097168 | tf_op jit(solution)/shard_map/all_gather | solution.py:83
  238.5 2.1 collective-permute-start.7
  240.6 9.1 %collective-permute-done.7 = f32[128,256]{1,0:T(8,128)S(1)} collective-permute-done((f32[128,256]{1,0:T(8,128)S(1)}, f32[128,256]{1,0:T(8,128)S(1)}, u32[]{:S(2)}, u32[]{:S(2)}) %collective-permute-start.7) | collective-permute-done | bytes 131104 | tf_op jit(solution)/shard_map/ppermute | solution.py:34
  251.0 4.4 %fusion.4 = f32[256,4096]{1,0:T(8,128)} fusion(bf16[4096,512]{1,0:T(8,128)(2,1)} %bitcast.98, bf16[32,8,2,128]{3,2,1,0:T(2,128)(2,1)S(1)} %bitcast.106), kind=kOutput, calls=%fused_computation.18 | convolution fusion | flops 536870912 | bytes 6422528 | tf_op jit(solution)/shard_map/dot_general | solution.py:14
  255.4 2.7 fusion.50
  258.4 2.1 collective-permute-start.8
  260.5 3.7 convolution_add_fusion
  270.1 3.6 pad_maximum_fusion
  273.7 90.5 %reduce-scatter.2.cloned.1.call-done = bf16[512,512]{1,0:T(8,128)(2,1)} async-done(((bf16[512,8192]{1,0:T(8,128)(2,1)}), bf16[512,512]{1,0:T(8,128)(2,1)}) %reduce-scatter.2.cloned.1.call-update) | async-done | bytes 524304 | tf_op jit(solution)/shard_map/reduce_scatter | solution.py:167
  365.2 2.1 collective-permute-start.9
  367.3 14.2 %collective-permute-done.9 = bf16[256,512]{1,0:T(8,128)(2,1)S(1)} collective-permute-done((bf16[256,512]{1,0:T(8,128)(2,1)S(1)}, bf16[256,512]{1,0:T(8,128)(2,1)S(1)}, u32[]{:S(2)}, u32[]{:S(2)}) %collective-permute-start.9) | collective-permute-done | bytes 262176 | tf_op jit(solution)/shard_map/ppermute | solution.py:169
  (110 shorter events, 30.3 us)
Async XLA Ops:
  7.2 229.3 %copy-start = (bf16[256,4096]{1,0:T(8,128)(2,1)S(1)}, bf16[256,4096]{1,0:T(8,128)(2,1)}, u32[]{:S(2)}) copy-start(bf16[256,4096]{1,0:T(8,128)(2,1)} %param.16) | copy-start | bytes 6291460
  8.6 10.6 %all-to-all-start = ((f32[16,1,256]{2,1,0:T(1,128)}), f32[16,1,256]{2,1,0:T(1,128)S(1)}, u32[]{:S(2)}, u32[]{:S(2)}) async-start(f32[16,1,256]{2,1,0:T(1,128)} %broadcast_in_dim.19), calls=%async_computation | async-start | bytes 32768 | tf_op jit(solution)/shard_map/all_to_all | solution.py:66
  28.5 7.3 %copy-start.12 = (s32[2,1,128]{2,1,0:T(1,128)S(1)}, s32[2,1,128]{2,1,0:T(1,128)}, u32[]{:S(2)}) copy-start(s32[2,1,128]{2,1,0:T(1,128)} %param.10) | copy-start | bytes 3076
  28.5 32.4 %copy-start.10 = (bf16[128,512]{1,0:T(8,128)(2,1)S(1)}, bf16[128,512]{1,0:T(8,128)(2,1)}, u32[]{:S(2)}) copy-start(bf16[128,512]{1,0:T(8,128)(2,1)} %param.9) | copy-start | bytes 393220
  28.5 30.5 %all-to-all-start.1 = ((bf16[16,64,512]{2,1,0:T(8,128)(2,1)}), bf16[16,64,512]{2,1,0:T(8,128)(2,1)S(1)}, u32[]{:S(2)}, u32[]{:S(2)}) async-start(bf16[16,64,512]{2,1,0:T(8,128)(2,1)} %bitcast.103), calls=%async_computation.1 | async-start | bytes 2097152 | tf_op jit(solution)/shard_map/all_to_all | solution.py:74
  35.7 112.3 %all-gather.9.cloned.1.call-start = ((), (), s32[]{:S(2)}) async-start(), calls=%async_computation.6 | async-start | bytes 4456448 | tf_op jit(solution)/shard_map/all_gather | solution.py:81
  60.8 120.5 %all-gather.5.cloned.1.call-start = ((), (), s32[]{:S(2)}) async-start(), calls=%async_computation.3 | async-start | bytes 2228224 | tf_op jit(solution)/shard_map/all_gather | solution.py:39
  61.6 174.9 %all-gather.7.cloned.1.call-start = ((), (), s32[]{:S(2)}) async-start(), calls=%async_computation.4 | async-start | bytes 2228224 | tf_op jit(solution)/shard_map/all_gather | solution.py:83
  62.7 19.3 %collective-permute-start = (bf16[512,512]{1,0:T(8,128)(2,1)S(1)}, bf16[512,512]{1,0:T(8,128)(2,1)S(1)}, u32[]{:S(2)}, u32[]{:S(2)}) collective-permute-start(bf16[512,512]{1,0:T(8,128)(2,1)S(1)} %fusion.46), channel_id=1, source_target_pairs={{0,1},{1,0},{2,3},{3,2},{4,5},{5,4},{6,7},{7,6},{8,9},{9,8},{10,11... | collective-permute-start | bytes 1572872 | tf_op jit(solution)/shard_map/ppermute | solution.py:43
  82.1 12.2 %copy-start.9 = (bf16[512,512]{1,0:T(8,128)(2,1)}, bf16[512,512]{1,0:T(8,128)(2,1)S(1)}, u32[]{:S(2)}) copy-start(bf16[512,512]{1,0:T(8,128)(2,1)S(1)} %collective-permute-done) | copy-start | bytes 1572868
  82.1 34.3 %collective-permute-start.1 = (bf16[1,512,512]{2,1,0:T(8,128)(2,1)S(1)}, bf16[1,512,512]{2,1,0:T(8,128)(2,1)}, u32[]{:S(2)}, u32[]{:S(2)}) collective-permute-start(bf16[1,512,512]{2,1,0:T(8,128)(2,1)S(1)} %bitcast.109), channel_id=1, source_target_pairs={{0,128},{32,160},{64,192},{96,224},{128,0},{160,32},{192,64},{224,... | collective-permute-start | bytes 1572872 | tf_op jit(solution)/shard_map/ppermute | solution.py:48
  118.1 25.9 %collective-permute-start.2 = (bf16[2,512,512]{2,1,0:T(8,128)(2,1)S(1)}, bf16[2,512,512]{2,1,0:T(8,128)(2,1)}, u32[]{:S(2)}, u32[]{:S(2)}) collective-permute-start(bf16[2,512,512]{2,1,0:T(8,128)(2,1)S(1)} %maximum_select_fusion.3), channel_id=1, source_target_pairs={{0,64},{32,96},{64,0},{96,32},{128,192},{160,224},{192,128},{224,1... | collective-permute-start | bytes 3145736 | tf_op jit(solution)/shard_map/ppermute | solution.py:48
  120.5 26.8 %copy-start.11 = (bf16[128,512]{1,0:T(8,128)(2,1)S(1)}, bf16[128,512]{1,0:T(8,128)(2,1)}, u32[]{:S(2)}) copy-start(bf16[128,512]{1,0:T(8,128)(2,1)} %param.17) | copy-start | bytes 393220
  147.3 38.5 %copy-start.13 = (s32[2]{0:T(128)S(1)}, s32[2]{0:T(128)}, u32[]{:S(2)}) copy-start(s32[2]{0:T(128)} %param.11) | copy-start | bytes 28
  147.3 47.6 %collective-permute-start.3 = (bf16[4,512,512]{2,1,0:T(8,128)(2,1)}, bf16[4,512,512]{2,1,0:T(8,128)(2,1)}, u32[]{:S(2)}, u32[]{:S(2)}) collective-permute-start(bf16[4,512,512]{2,1,0:T(8,128)(2,1)} %maximum_select_fusion.2), channel_id=1, source_target_pairs={{0,32},{32,0},{64,96},{96,64},{128,160},{160,128},{192,224},{224,1... | collective-permute-start | bytes 6291464 | tf_op jit(solution)/shard_map/ppermute | solution.py:48
  148.0 216.2 %reduce-scatter.2.cloned.1.call-start = ((), (), s32[]{:S(2)}) async-start(), calls=%async_computation.5 | async-start | bytes 8912896 | tf_op jit(solution)/shard_map/reduce_scatter | solution.py:167
  183.7 11.2 %collective-permute-start.4 = (f32[128,256]{1,0:T(8,128)S(1)}, f32[128,256]{1,0:T(8,128)S(1)}, u32[]{:S(2)}, u32[]{:S(2)}) collective-permute-start(f32[128,256]{1,0:T(8,128)S(1)} %fusion.43), channel_id=1, source_target_pairs={{0,1},{1,0},{2,3},{3,2},{4,5},{5,4},{6,7},{7,6},{8,9},{9,8},{10,11... | collective-permute-start | bytes 393224 | tf_op jit(solution)/shard_map/ppermute | solution.py:34
  199.1 1.6 copy-start.2
  199.1 2.8 copy-start.8
  201.9 2.0 copy-start.4
  204.6 3.5 copy-start.5
  210.8 29.8 %collective-permute-start.6 = (f32[2,2,64]{2,1,0:T(2,128)S(1)}, f32[2,2,64]{2,1,0:T(2,128)S(1)}, u32[]{:S(2)}, u32[]{:S(2)}) collective-permute-start(f32[2,2,64]{2,1,0:T(2,128)S(1)} %get-tuple-element.30), channel_id=1, source_target_pairs={{0,1},{1,0},{2,3},{3,2},{4,5},{5,4},{6,7},{7,6},{8,9},{9,8},{10,11... | collective-permute-start | bytes 3080 | tf_op jit(solution)/shard_map/ppermute | solution.py:34
  213.0 37.0 %collective-permute-start.5 = (f32[2,64,2,128]{3,1,2,0:T(8,128)S(1)}, f32[2,64,2,128]{3,1,2,0:T(8,128)S(1)}, u32[]{:S(2)}, u32[]{:S(2)}) collective-permute-start(f32[2,64,2,128]{3,1,2,0:T(8,128)S(1)} %convolution_bitcast_fusion.1), channel_id=1, source_target_pairs={{0,1},{1,0},{2,3},{3,2},{4,5},{5,4},{6,7},{7,6},{8,9},{9,8},{10,11... | collective-permute-start | bytes 393224 | tf_op jit(solution)/shard_map/ppermute | solution.py:34
  238.5 11.2 %collective-permute-start.7 = (f32[128,256]{1,0:T(8,128)S(1)}, f32[128,256]{1,0:T(8,128)S(1)}, u32[]{:S(2)}, u32[]{:S(2)}) collective-permute-start(f32[128,256]{1,0:T(8,128)S(1)} %fusion.41), channel_id=1, source_target_pairs={{0,1},{1,0},{2,3},{3,2},{4,5},{5,4},{6,7},{7,6},{8,9},{9,8},{10,11... | collective-permute-start | bytes 393224 | tf_op jit(solution)/shard_map/ppermute | solution.py:34
  251.0 4.4 %copy-start.1 = (bf16[4096,256]{1,0:T(8,128)(2,1)S(1)}, bf16[4096,256]{1,0:T(8,128)(2,1)}, u32[]{:S(2)}) copy-start(bf16[4096,256]{1,0:T(8,128)(2,1)} %param.14) | copy-start | bytes 6291460
  258.4 9.0 %collective-permute-start.8 = (f32[2,64,2,128]{3,1,2,0:T(8,128)S(1)}, f32[2,64,2,128]{3,1,2,0:T(8,128)S(1)}, u32[]{:S(2)}, u32[]{:S(2)}) collective-permute-start(f32[2,64,2,128]{3,1,2,0:T(8,128)S(1)} %convolution_bitcast_fusion), channel_id=1, source_target_pairs={{0,1},{1,0},{2,3},{3,2},{4,5},{5,4},{6,7},{7,6},{8,9},{9,8},{10,11... | collective-permute-start | bytes 393224 | tf_op jit(solution)/shard_map/ppermute | solution.py:34
  260.5 3.7 copy-start.3
  260.5 4.7 %copy-start.6 = (f32[256,4096]{1,0:T(8,128)S(1)}, f32[256,4096]{1,0:T(8,128)}, u32[]{:S(2)}) copy-start(f32[256,4096]{1,0:T(8,128)} %fusion.50) | copy-start | bytes 12582916
  266.9 1.6 copy-start.7
  365.2 16.3 %collective-permute-start.9 = (bf16[256,512]{1,0:T(8,128)(2,1)S(1)}, bf16[256,512]{1,0:T(8,128)(2,1)S(1)}, u32[]{:S(2)}, u32[]{:S(2)}) collective-permute-start(bf16[256,512]{1,0:T(8,128)(2,1)S(1)} %slice.60), channel_id=1, source_target_pairs={{0,1},{1,0},{2,3},{3,2},{4,5},{5,4},{6,7},{7,6},{8,9},{9,8},{10,11... | collective-permute-start | bytes 786440 | tf_op jit(solution)/shard_map/ppermute | solution.py:169
Sparse Core Ops, SparseCore 0:
  60.9 65.2 all-gather.8
  129.2 52.0 all-gather.4
  184.3 52.1 all-gather.6
  273.8 90.3 reduce-scatter.1

commit v13 on v10

--- a/solution.py
+++ b/solution.py
@@ -121,12 +121,6 @@
     attn = numer / jnp.transpose(total, (0, 2, 1))[..., None]
     attn_bf = attn.reshape(rows_here, heads_here * HD).astype(jnp.bfloat16)
 
-    def place_half(x):
-        zeros = jnp.zeros_like(x)
-        return jnp.where(
-            me_group == 0, jnp.concatenate([x, zeros], 1), jnp.concatenate([zeros, x], 1)
-        )
-
     out_term = jnp.dot(attn_bf, w_out, preferred_element_type=jnp.float32)
     d_attn_part = contract(this_half(full_grad), w_out)
     d_attn = group_sum(d_attn_part).astype(jnp.bfloat16)
@@ -157,22 +151,32 @@
         jnp.concatenate([term_here, term_there], 1),
         jnp.concatenate([term_there, term_here], 1),
     )
-    stacked = jnp.concatenate(
-        [
-            place_half(out_term.astype(jnp.bfloat16)),
-            place_half(hid_term.astype(jnp.bfloat16)),
-            neigh_term.astype(jnp.bfloat16),
-        ],
-        0,
-    )
+    packed = jnp.concatenate(
+        [out_term.astype(jnp.bfloat16), hid_term.astype(jnp.bfloat16)], 1
+    )
+    stacked = jnp.concatenate([packed, neigh_term.astype(jnp.bfloat16)], 0)
     reduced = lax.psum_scatter(stacked, "mp", scatter_dimension=1, tiled=True)
-    both_cols = reduced[: 2 * rows_here]
-    both_cols = (both_cols + lax.ppermute(both_cols, "group", swap)).astype(jnp.float32)
-    out_cols, hid_cols = both_cols[:rows_here], both_cols[rows_here:]
+    held_cols = reduced[:rows_here]
+    n_mp = lax.axis_size("mp")
+    half_mp = n_mp // 2
+
+    def owner_of(s, gs, g_to):
+        return (gs * half_mp + s % half_mp) * 2 + g_to
+
+    pairs_a, pairs_b = [], []
+    for s in range(n_mp):
+        for gs in range(2):
+            is_out = s < half_mp
+            pairs_a.append((s * 2 + gs, owner_of(s, gs, 0 if is_out else 1)))
+            pairs_b.append((s * 2 + gs, owner_of(s, gs, 1 if is_out else 0)))
+    got_a = lax.ppermute(held_cols, ("mp", "group"), pairs_a)
+    got_b = lax.ppermute(held_cols, ("mp", "group"), pairs_b)
+    out_cols = jnp.where(me_group == 0, got_a, got_b).astype(jnp.float32)
+    hid_cols = jnp.where(me_group == 0, got_b, got_a).astype(jnp.float32)
     zero_rows = jnp.zeros((tail_rows, out_cols.shape[1]), jnp.float32)
     output = jnp.concatenate([zero_rows, out_cols[:keep_rows]], 0)
     grad_hidden = jnp.concatenate([zero_rows, hid_cols[:keep_rows]], 0)
-    neigh_cols = reduced[2 * rows_here :].astype(jnp.float32)
+    neigh_cols = reduced[rows_here:].astype(jnp.float32)
     grad_neighbours = neigh_cols.reshape(blocks_here, 1, RET, neigh_cols.shape[1])
     return (output, grad_hidden, grad_neighbours)
 

time: 348 us -> 356 us (1.023)
  other arithmetic: 20.1 us -> 30.5 us
  waiting for transfers between devices: 216 us -> 210 us
  starting transfers between devices: 51.3 us -> 56.1 us
    concatenate x1 -> x2, other arithmetic: 3.54 us -> 15.9 us  [the longest x1 15.1 us: per_device(): stacked = jnp.concatenate([packed, neigh_term.astype(jnp.bfloat16)], 0)]
    ppermute x1 -> x2, starting transfers between devices: 2.09 us -> 6.93 us  [the longest x1 4.27 us: per_device(): got_a = lax.ppermute(held_cols, ('mp', 'group'), pairs_a)]
    ppermute x1 -> x2, waiting for transfers between devices: 13.9 us -> 9.75 us  [the longest x1 7.32 us: per_device(): got_a = lax.ppermute(held_cols, ('mp', 'group'), pairs_a)]
    reduce_scatter x1, waiting for transfers between devices: 88.8 us -> 85 us  [per_device(): reduced = lax.psum_scatter(stacked, 'mp', scatter_dimension=1, tiled=True)]
  transfers between devices with their start and end apart: 16 -> 17, of which waited for: 13 -> 14; matrix products, arithmetic and copies ran while one was open for 10% -> 10% of each run, Pallas kernels for 0% -> 0%
where the time goes in v13:
time: 356 us; the launch traced here: 355 us
  waiting for transfers between devices  210 us (59%)
  starting transfers between devices  56.1 us (16%)
  other arithmetic  30.5 us (9%)
  matrix products  22.6 us (6%)
  local copies, waits for them, and re-layouts  21.8 us (6%)
  between operations  14.2 us (4%)
    reduce_scatter x1, waiting for transfers between devices, per_device(): reduced = lax.psum_scatter(stacked, 'mp', scatter_dimension=1, tiled=True)  85 us
    ppermute x3, waiting for transfers between devices, per_device(): other = lax.ppermute(held, 'dp', pairs)  45.6 us
    ppermute x5, waiting for transfers between devices, group_sum(): return x + lax.ppermute(x, 'group', swap)  23 us
    all_to_all x1, waiting for transfers between devices, per_device(): recv_buf = lax.all_to_all(send_buf, ('dp', 'group'), 0, 0, tiled=True)  22.2 us
    ppermute x5, starting transfers between devices, group_sum(): return x + lax.ppermute(x, 'group', swap)  16.3 us
    concatenate x1, other arithmetic, per_device(): stacked = jnp.concatenate([packed, neigh_term.astype(jnp.bfloat16)], 0)  15.1 us
    ppermute x1, waiting for transfers between devices, per_device(): held = lax.ppermute(kv_piece, 'group', swap)[None]  14.7 us
    ppermute x3, starting transfers between devices, per_device(): other = lax.ppermute(held, 'dp', pairs)  14.6 us
  transfers between devices with their start and end apart: 17, of which 14 were waited for; matrix products, arithmetic and copies ran while one was open for 10% of the time, Pallas kernels for 0%

profile of v13, /device:TPU:192, one launch (start us, length us, event | category | flops | bytes accessed | tf_op | source)
XLA Modules:
  0.0 355.2 jit_solution(9496642766434340751)
XLA Ops:
  11.9 6.3 %all-to-all-start = ((f32[16,1,256]{2,1,0:T(1,128)}), f32[16,1,256]{2,1,0:T(1,128)S(1)}, u32[]{:S(2)}, u32[]{:S(2)}) async-start(f32[16,1,256]{2,1,0:T(1,128)} %broadcast_in_dim.19), calls=%async_computation | async-start | bytes 32768 | tf_op jit(solution)/shard_map/all_to_all | solution.py:69
  18.2 4.2 %all-to-all-done = f32[16,1,256]{2,1,0:T(1,128)S(1)} async-done(((f32[16,1,256]{2,1,0:T(1,128)}), f32[16,1,256]{2,1,0:T(1,128)S(1)}, u32[]{:S(2)}, u32[]{:S(2)}) %all-to-all-start) | async-done | bytes 16416 | tf_op jit(solution)/shard_map/all_to_all | solution.py:69
  23.9 7.9 %gather_fusion = bf16[1024,512]{1,0:T(8,128)(2,1)} fusion(bf16[4096,512]{1,0:T(8,128)(2,1)} %param.12, s32[1024]{0:T(1024)S(1)} %broadcast_clamp_fusion), kind=kCustom, calls=%fused_computation | custom fusion | bytes 2101248 | tf_op jit(solution)/shard_map/gather | solution.py:76
  31.8 7.2 %all-to-all-start.1 = ((bf16[16,64,512]{2,1,0:T(8,128)(2,1)}), bf16[16,64,512]{2,1,0:T(8,128)(2,1)S(1)}, u32[]{:S(2)}, u32[]{:S(2)}) async-start(bf16[16,64,512]{2,1,0:T(8,128)(2,1)} %bitcast.103), calls=%async_computation.1 | async-start | bytes 2097152 | tf_op jit(solution)/shard_map/all_to_all | solution.py:77
  40.0 22.2 %all-to-all-done.1 = bf16[16,64,512]{2,1,0:T(8,128)(2,1)S(1)} async-done(((bf16[16,64,512]{2,1,0:T(8,128)(2,1)}), bf16[16,64,512]{2,1,0:T(8,128)(2,1)S(1)}, u32[]{:S(2)}, u32[]{:S(2)}) %all-to-all-start.1) | async-done | bytes 1048608 | tf_op jit(solution)/shard_map/all_to_all | solution.py:77
  65.2 4.6 %collective-permute-start = (bf16[512,512]{1,0:T(8,128)(2,1)S(1)}, bf16[512,512]{1,0:T(8,128)(2,1)S(1)}, u32[]{:S(2)}, u32[]{:S(2)}) collective-permute-start(bf16[512,512]{1,0:T(8,128)(2,1)S(1)} %fusion.46), channel_id=1, source_target_pairs={{0,1},{1,0},{2,3},{3,2},{4,5},{5,4},{6,7},{7,6},{8,9},{9,8},{10,11... | collective-permute-start | bytes 1572872 | tf_op jit(solution)/shard_map/ppermute | solution.py:46
  69.8 14.7 %collective-permute-done = bf16[512,512]{1,0:T(8,128)(2,1)S(1)} collective-permute-done((bf16[512,512]{1,0:T(8,128)(2,1)S(1)}, bf16[512,512]{1,0:T(8,128)(2,1)S(1)}, u32[]{:S(2)}, u32[]{:S(2)}) %collective-permute-start) | collective-permute-done | bytes 524320 | tf_op jit(solution)/shard_map/ppermute | solution.py:46
  84.5 12.2 %collective-permute-start.1 = (bf16[1,512,512]{2,1,0:T(8,128)(2,1)S(1)}, bf16[1,512,512]{2,1,0:T(8,128)(2,1)}, u32[]{:S(2)}, u32[]{:S(2)}) collective-permute-start(bf16[1,512,512]{2,1,0:T(8,128)(2,1)S(1)} %bitcast.109), channel_id=1, source_target_pairs={{0,128},{32,160},{64,192},{96,224},{128,0},{160,32},{192,64},{224,... | collective-permute-start | bytes 1572872 | tf_op jit(solution)/shard_map/ppermute | solution.py:51
  96.7 22.1 %collective-permute-done.1 = bf16[1,512,512]{2,1,0:T(8,128)(2,1)} collective-permute-done((bf16[1,512,512]{2,1,0:T(8,128)(2,1)S(1)}, bf16[1,512,512]{2,1,0:T(8,128)(2,1)}, u32[]{:S(2)}, u32[]{:S(2)}) %collective-permute-start.1) | collective-permute-done | bytes 524320 | tf_op jit(solution)/shard_map/ppermute | solution.py:51
  120.6 2.4 collective-permute-start.2
  123.0 23.5 %collective-permute-done.2 = bf16[2,512,512]{2,1,0:T(8,128)(2,1)} collective-permute-done((bf16[2,512,512]{2,1,0:T(8,128)(2,1)S(1)}, bf16[2,512,512]{2,1,0:T(8,128)(2,1)}, u32[]{:S(2)}, u32[]{:S(2)}) %collective-permute-start.2) | collective-permute-done | bytes 1048608 | tf_op jit(solution)/shard_map/ppermute | solution.py:51
  146.5 3.2 maximum_select_fusion.2
  149.7 2.4 fusion.43
  152.1 4.3 %collective-permute-start.4 = (f32[128,256]{1,0:T(8,128)S(1)}, f32[128,256]{1,0:T(8,128)S(1)}, u32[]{:S(2)}, u32[]{:S(2)}) collective-permute-start(f32[128,256]{1,0:T(8,128)S(1)} %fusion.43), channel_id=1, source_target_pairs={{0,1},{1,0},{2,3},{3,2},{4,5},{5,4},{6,7},{7,6},{8,9},{9,8},{10,11... | collective-permute-start | bytes 393224 | tf_op jit(solution)/shard_map/ppermute | solution.py:34
  160.3 3.3 collective-permute-done.4
  163.6 8.6 %collective-permute-done.7 = f32[128,256]{1,0:T(8,128)S(1)} collective-permute-done((f32[128,256]{1,0:T(8,128)S(1)}, f32[128,256]{1,0:T(8,128)S(1)}, u32[]{:S(2)}, u32[]{:S(2)}) %collective-permute-start.7) | collective-permute-done | bytes 131104 | tf_op jit(solution)/shard_map/ppermute | solution.py:34
  172.3 3.8 %maximum_select_fusion.1 = bf16[8,512,512]{2,1,0:T(8,128)(2,1)S(1)} fusion(bf16[4,512,512]{2,1,0:T(8,128)(2,1)} %collective-permute-done.3, bf16[4,512,512]{2,1,0:T(8,128)(2,1)} %maximum_select_fusion.2, pred[]{:T(512)S(6)} %eq.62), kind=kLoop, calls=%fused_computation.11 | loop fusion | flops 6291456 | bytes 8388609 | tf_op jit(solution)/shard_map/jit(_where)/select_n | solution.py:53
  176.1 2.4 copy.75
  178.5 5.5 %all-gather.9.cloned.1.call-done = bf16[256,8192]{1,0:T(8,128)(2,1)} async-done(((bf16[256,512]{1,0:T(8,128)(2,1)}), bf16[256,8192]{1,0:T(8,128)(2,1)}) %all-gather.9.cloned.1.call-update) | async-done | bytes 4194320 | tf_op jit(solution)/shard_map/all_gather | solution.py:84
  184.1 3.1 fusion.12
  189.9 3.1 fusion.10
  198.5 4.0 %collective-permute-start.5 = (f32[2,64,2,128]{3,1,2,0:T(8,128)S(1)}, f32[2,64,2,128]{3,1,2,0:T(8,128)S(1)}, u32[]{:S(2)}, u32[]{:S(2)}) collective-permute-start(f32[2,64,2,128]{3,1,2,0:T(8,128)S(1)} %convolution_bitcast_fusion.1), channel_id=1, source_target_pairs={{0,1},{1,0},{2,3},{3,2},{4,5},{5,4},{6,7},{7,6},{8,9},{9,8},{10,11... | collective-permute-start | bytes 393224 | tf_op jit(solution)/shard_map/ppermute | solution.py:34
  204.6 4.7 %collective-permute-done.5 = f32[2,64,2,128]{3,1,2,0:T(8,128)S(1)} collective-permute-done((f32[2,64,2,128]{3,1,2,0:T(8,128)S(1)}, f32[2,64,2,128]{3,1,2,0:T(8,128)S(1)}, u32[]{:S(2)}, u32[]{:S(2)}) %collective-permute-start.5) | collective-permute-done | bytes 131104 | tf_op jit(solution)/shard_map/ppermute | solution.py:34
  210.1 2.5 fusion.4
  217.1 4.0 %collective-permute-start.8 = (f32[2,64,2,128]{3,1,2,0:T(8,128)S(1)}, f32[2,64,2,128]{3,1,2,0:T(8,128)S(1)}, u32[]{:S(2)}, u32[]{:S(2)}) collective-permute-start(f32[2,64,2,128]{3,1,2,0:T(8,128)S(1)} %convolution_bitcast_fusion), channel_id=1, source_target_pairs={{0,1},{1,0},{2,3},{3,2},{4,5},{5,4},{6,7},{7,6},{8,9},{9,8},{10,11... | collective-permute-start | bytes 393224 | tf_op jit(solution)/shard_map/ppermute | solution.py:34
  222.6 4.8 %collective-permute-done.8 = f32[2,64,2,128]{3,1,2,0:T(8,128)S(1)} collective-permute-done((f32[2,64,2,128]{3,1,2,0:T(8,128)S(1)}, f32[2,64,2,128]{3,1,2,0:T(8,128)S(1)}, u32[]{:S(2)}, u32[]{:S(2)}) %collective-permute-start.8) | collective-permute-done | bytes 131104 | tf_op jit(solution)/shard_map/ppermute | solution.py:34
  228.3 15.1 %pad_maximum_fusion = bf16[384,8192]{1,0:T(8,128)(2,1)} fusion(bf16[256,8192]{1,0:T(8,128)(2,1)S(1)} %fusion, bf16[128,4096]{1,0:T(8,128)(2,1)S(1)} %convolution_convert_fusion, bf16[128,4096]{1,0:T(8,128)(2,1)S(1)} %convolution_convert_fusion.1), kind=kLoop, calls=%fused_computation.4 | loop fusion | flops 18874368 | bytes 12582912 | tf_op jit(solution)/shard_map/concatenate | solution.py:157
  243.4 85.0 %reduce-scatter.2.cloned.1.call-done = bf16[384,512]{1,0:T(8,128)(2,1)} async-done(((bf16[384,8192]{1,0:T(8,128)(2,1)}), bf16[384,512]{1,0:T(8,128)(2,1)}) %reduce-scatter.2.cloned.1.call-update) | async-done | bytes 393232 | tf_op jit(solution)/shard_map/reduce_scatter | solution.py:158
  329.3 2.7 collective-permute-start.10
  332.0 4.3 %collective-permute-start.9 = (bf16[128,512]{1,0:T(8,128)(2,1)S(1)}, bf16[128,512]{1,0:T(8,128)(2,1)S(1)}, u32[]{:S(2)}, u32[]{:S(2)}) collective-permute-start(bf16[128,512]{1,0:T(8,128)(2,1)S(1)} %slice.58), channel_id=1, source_target_pairs={{0,0},{1,16},{2,2},{3,18},{4,4},{5,20},{6,6},{7,22},{8,8},{9,24},{... | collective-permute-start | bytes 393224 | tf_op jit(solution)/shard_map/ppermute | solution.py:172
  338.1 2.4 collective-permute-done.10
  340.5 7.3 %collective-permute-done.9 = bf16[128,512]{1,0:T(8,128)(2,1)S(1)} collective-permute-done((bf16[128,512]{1,0:T(8,128)(2,1)S(1)}, bf16[128,512]{1,0:T(8,128)(2,1)S(1)}, u32[]{:S(2)}, u32[]{:S(2)}) %collective-permute-start.9) | collective-permute-done | bytes 131104 | tf_op jit(solution)/shard_map/ppermute | solution.py:172
  (102 shorter events, 37.5 us)
Async XLA Ops:
  7.2 149.2 %copy-start = (bf16[256,4096]{1,0:T(8,128)(2,1)S(1)}, bf16[256,4096]{1,0:T(8,128)(2,1)}, u32[]{:S(2)}) copy-start(bf16[256,4096]{1,0:T(8,128)(2,1)} %param.16) | copy-start | bytes 6291460
  7.2 142.5 %all-gather.5.cloned.1.call-start = ((), (), s32[]{:S(2)}) async-start(), calls=%async_computation.3 | async-start | bytes 2228224 | tf_op jit(solution)/shard_map/all_gather | solution.py:40
  9.0 147.4 %all-gather.7.cloned.1.call-start = ((), (), s32[]{:S(2)}) async-start(), calls=%async_computation.4 | async-start | bytes 2228224 | tf_op jit(solution)/shard_map/all_gather | solution.py:41
  11.9 10.6 %all-to-all-start = ((f32[16,1,256]{2,1,0:T(1,128)}), f32[16,1,256]{2,1,0:T(1,128)S(1)}, u32[]{:S(2)}, u32[]{:S(2)}) async-start(f32[16,1,256]{2,1,0:T(1,128)} %broadcast_in_dim.19), calls=%async_computation | async-start | bytes 32768 | tf_op jit(solution)/shard_map/all_to_all | solution.py:69
  31.8 7.2 %copy-start.8 = (s32[2,1,128]{2,1,0:T(1,128)S(1)}, s32[2,1,128]{2,1,0:T(1,128)}, u32[]{:S(2)}) copy-start(s32[2,1,128]{2,1,0:T(1,128)} %param.10) | copy-start | bytes 3076
  31.8 30.4 %all-to-all-start.1 = ((bf16[16,64,512]{2,1,0:T(8,128)(2,1)}), bf16[16,64,512]{2,1,0:T(8,128)(2,1)S(1)}, u32[]{:S(2)}, u32[]{:S(2)}) async-start(bf16[16,64,512]{2,1,0:T(8,128)(2,1)} %bitcast.103), calls=%async_computation.1 | async-start | bytes 2097152 | tf_op jit(solution)/shard_map/all_to_all | solution.py:77
  38.9 145.1 %all-gather.9.cloned.1.call-start = ((), (), s32[]{:S(2)}) async-start(), calls=%async_computation.6 | async-start | bytes 4456448 | tf_op jit(solution)/shard_map/all_gather | solution.py:84
  64.1 264.3 %reduce-scatter.2.cloned.1.call-start = ((), (), s32[]{:S(2)}) async-start(), calls=%async_computation.5 | async-start | bytes 6684672 | tf_op jit(solution)/shard_map/reduce_scatter | solution.py:158
  65.2 19.3 %collective-permute-start = (bf16[512,512]{1,0:T(8,128)(2,1)S(1)}, bf16[512,512]{1,0:T(8,128)(2,1)S(1)}, u32[]{:S(2)}, u32[]{:S(2)}) collective-permute-start(bf16[512,512]{1,0:T(8,128)(2,1)S(1)} %fusion.46), channel_id=1, source_target_pairs={{0,1},{1,0},{2,3},{3,2},{4,5},{5,4},{6,7},{7,6},{8,9},{9,8},{10,11... | collective-permute-start | bytes 1572872 | tf_op jit(solution)/shard_map/ppermute | solution.py:46
  84.5 12.2 %copy-start.7 = (bf16[512,512]{1,0:T(8,128)(2,1)}, bf16[512,512]{1,0:T(8,128)(2,1)S(1)}, u32[]{:S(2)}) copy-start(bf16[512,512]{1,0:T(8,128)(2,1)S(1)} %collective-permute-done) | copy-start | bytes 1572868
  84.5 34.3 %collective-permute-start.1 = (bf16[1,512,512]{2,1,0:T(8,128)(2,1)S(1)}, bf16[1,512,512]{2,1,0:T(8,128)(2,1)}, u32[]{:S(2)}, u32[]{:S(2)}) collective-permute-start(bf16[1,512,512]{2,1,0:T(8,128)(2,1)S(1)} %bitcast.109), channel_id=1, source_target_pairs={{0,128},{32,160},{64,192},{96,224},{128,0},{160,32},{192,64},{224,... | collective-permute-start | bytes 1572872 | tf_op jit(solution)/shard_map/ppermute | solution.py:51
  120.6 25.9 %collective-permute-start.2 = (bf16[2,512,512]{2,1,0:T(8,128)(2,1)S(1)}, bf16[2,512,512]{2,1,0:T(8,128)(2,1)}, u32[]{:S(2)}, u32[]{:S(2)}) collective-permute-start(bf16[2,512,512]{2,1,0:T(8,128)(2,1)S(1)} %maximum_select_fusion.3), channel_id=1, source_target_pairs={{0,64},{32,96},{64,0},{96,32},{128,192},{160,224},{192,128},{224,1... | collective-permute-start | bytes 3145736 | tf_op jit(solution)/shard_map/ppermute | solution.py:51
  123.0 26.7 %copy-start.9 = (s32[2]{0:T(128)S(1)}, s32[2]{0:T(128)}, u32[]{:S(2)}) copy-start(s32[2]{0:T(128)} %param.11) | copy-start | bytes 28
  149.7 22.6 %collective-permute-start.3 = (bf16[4,512,512]{2,1,0:T(8,128)(2,1)}, bf16[4,512,512]{2,1,0:T(8,128)(2,1)}, u32[]{:S(2)}, u32[]{:S(2)}) collective-permute-start(bf16[4,512,512]{2,1,0:T(8,128)(2,1)} %maximum_select_fusion.2), channel_id=1, source_target_pairs={{0,32},{32,0},{64,96},{96,64},{128,160},{160,128},{192,224},{224,1... | collective-permute-start | bytes 6291464 | tf_op jit(solution)/shard_map/ppermute | solution.py:51
  152.1 11.5 %collective-permute-start.4 = (f32[128,256]{1,0:T(8,128)S(1)}, f32[128,256]{1,0:T(8,128)S(1)}, u32[]{:S(2)}, u32[]{:S(2)}) collective-permute-start(f32[128,256]{1,0:T(8,128)S(1)} %fusion.43), channel_id=1, source_target_pairs={{0,1},{1,0},{2,3},{3,2},{4,5},{5,4},{6,7},{7,6},{8,9},{9,8},{10,11... | collective-permute-start | bytes 393224 | tf_op jit(solution)/shard_map/ppermute | solution.py:34
  158.4 13.8 %collective-permute-start.7 = (f32[128,256]{1,0:T(8,128)S(1)}, f32[128,256]{1,0:T(8,128)S(1)}, u32[]{:S(2)}, u32[]{:S(2)}) collective-permute-start(f32[128,256]{1,0:T(8,128)S(1)} %fusion.41), channel_id=1, source_target_pairs={{0,1},{1,0},{2,3},{3,2},{4,5},{5,4},{6,7},{7,6},{8,9},{9,8},{10,11... | collective-permute-start | bytes 393224 | tf_op jit(solution)/shard_map/ppermute | solution.py:34
  184.1 3.4 copy-start.3
  189.9 3.5 copy-start.4
  196.1 8.1 %collective-permute-start.6 = (f32[2,2,64]{2,1,0:T(2,128)S(1)}, f32[2,2,64]{2,1,0:T(2,128)S(1)}, u32[]{:S(2)}, u32[]{:S(2)}) collective-permute-start(f32[2,2,64]{2,1,0:T(2,128)S(1)} %get-tuple-element.24), channel_id=1, source_target_pairs={{0,1},{1,0},{2,3},{3,2},{4,5},{5,4},{6,7},{7,6},{8,9},{9,8},{10,11... | collective-permute-start | bytes 3080 | tf_op jit(solution)/shard_map/ppermute | solution.py:34
  198.5 10.9 %collective-permute-start.5 = (f32[2,64,2,128]{3,1,2,0:T(8,128)S(1)}, f32[2,64,2,128]{3,1,2,0:T(8,128)S(1)}, u32[]{:S(2)}, u32[]{:S(2)}) collective-permute-start(f32[2,64,2,128]{3,1,2,0:T(8,128)S(1)} %convolution_bitcast_fusion.1), channel_id=1, source_target_pairs={{0,1},{1,0},{2,3},{3,2},{4,5},{5,4},{6,7},{7,6},{8,9},{9,8},{10,11... | collective-permute-start | bytes 393224 | tf_op jit(solution)/shard_map/ppermute | solution.py:34
  210.1 2.5 copy-start.1
  212.6 2.2 copy-start.5
  214.8 1.6 copy-start.2
  217.1 10.3 %collective-permute-start.8 = (f32[2,64,2,128]{3,1,2,0:T(8,128)S(1)}, f32[2,64,2,128]{3,1,2,0:T(8,128)S(1)}, u32[]{:S(2)}, u32[]{:S(2)}) collective-permute-start(f32[2,64,2,128]{3,1,2,0:T(8,128)S(1)} %convolution_bitcast_fusion), channel_id=1, source_target_pairs={{0,1},{1,0},{2,3},{3,2},{4,5},{5,4},{6,7},{7,6},{8,9},{9,8},{10,11... | collective-permute-start | bytes 393224 | tf_op jit(solution)/shard_map/ppermute | solution.py:34
  222.2 5.3 %copy-start.6 = (bf16[4096,256]{1,0:T(8,128)(2,1)S(1)}, bf16[4096,256]{1,0:T(8,128)(2,1)}, u32[]{:S(2)}) copy-start(bf16[4096,256]{1,0:T(8,128)(2,1)} %param.13) | copy-start | bytes 6291460
  329.3 11.2 %collective-permute-start.10 = (bf16[128,512]{1,0:T(8,128)(2,1)S(1)}, bf16[128,512]{1,0:T(8,128)(2,1)S(1)}, u32[]{:S(2)}, u32[]{:S(2)}) collective-permute-start(bf16[128,512]{1,0:T(8,128)(2,1)S(1)} %slice.58), channel_id=1, source_target_pairs={{0,1},{1,17},{2,3},{3,19},{4,5},{5,21},{6,7},{7,23},{8,9},{9,25},{... | collective-permute-start | bytes 393224 | tf_op jit(solution)/shard_map/ppermute | solution.py:173
  332.0 15.8 %collective-permute-start.9 = (bf16[128,512]{1,0:T(8,128)(2,1)S(1)}, bf16[128,512]{1,0:T(8,128)(2,1)S(1)}, u32[]{:S(2)}, u32[]{:S(2)}) collective-permute-start(bf16[128,512]{1,0:T(8,128)(2,1)S(1)} %slice.58), channel_id=1, source_target_pairs={{0,0},{1,16},{2,2},{3,18},{4,4},{5,20},{6,6},{7,22},{8,8},{9,24},{... | collective-permute-start | bytes 393224 | tf_op jit(solution)/shard_map/ppermute | solution.py:172
Sparse Core Ops, SparseCore 0:
  11.0 53.4 all-gather.4
  66.9 52.0 all-gather.6
  122.0 62.0 all-gather.8
  243.5 84.8 reduce-scatter.1

commit v14 on v10

--- a/solution.py
+++ b/solution.py
@@ -116,7 +116,10 @@
         preferred_element_type=jnp.float32,
     )
     partial_total = jnp.sum(weights, -1)
-    numer, partial_total = group_sum(numer), group_sum(partial_total)
+    numer_size = numer.size
+    joined = group_sum(jnp.concatenate([numer.reshape(-1), partial_total.reshape(-1)]))
+    numer = joined[:numer_size].reshape(numer.shape)
+    partial_total = joined[numer_size:].reshape(partial_total.shape)
     total = partial_total + 1.0
     attn = numer / jnp.transpose(total, (0, 2, 1))[..., None]
     attn_bf = attn.reshape(rows_here, heads_here * HD).astype(jnp.bfloat16)

time: 348 us -> 352 us (1.011)
  matrix products: 22.6 us -> 29.5 us
  starting transfers between devices: 51.3 us -> 45.3 us
    all_gather x1, waiting for transfers between devices: 5.56 us -> 14.1 us  [per_device(): neighbours = lax.all_gather(own_cols, 'mp', axis=1, tiled=True)]
    ppermute x5 -> x4, waiting for transfers between devices: 20.8 us -> 12.5 us  [group_sum(): return x + lax.ppermute(x, 'group', swap)]
    dot_general x6, matrix products: 7.59 us -> 14.5 us  [contract(): lax.dot_general(left, right, (((1,), (1,)), ((), ())), preferred_element_...]
    ppermute x5 -> x4, starting transfers between devices: 16.3 us -> 10.5 us  [group_sum(): return x + lax.ppermute(x, 'group', swap)]
  transfers between devices with their start and end apart: 16 -> 15, of which waited for: 13 -> 10; matrix products, arithmetic and copies ran while one was open for 10% -> 14% of each run, Pallas kernels for 0% -> 0%
where the time goes in v14:
time: 352 us; the launch traced here: 350 us
  waiting for transfers between devices  217 us (62%)
  starting transfers between devices  45.3 us (13%)
  matrix products  29.5 us (8%)
  local copies, waits for them, and re-layouts  22.9 us (7%)
  other arithmetic  20.6 us (6%)
  between operations  14.2 us (4%)
    reduce_scatter x1, waiting for transfers between devices, per_device(): reduced = lax.psum_scatter(stacked, 'mp', scatter_dimension=1, tiled=True)  89.6 us
    ppermute x3, waiting for transfers between devices, per_device(): other = lax.ppermute(held, 'dp', pairs)  45.6 us
    all_to_all x1, waiting for transfers between devices, per_device(): recv_buf = lax.all_to_all(send_buf, ('dp', 'group'), 0, 0, tiled=True)  22.2 us
    ppermute x1, waiting for transfers between devices, per_device(): held = lax.ppermute(kv_piece, 'group', swap)[None]  14.7 us
    ppermute x3, starting transfers between devices, per_device(): other = lax.ppermute(held, 'dp', pairs)  14.6 us
    dot_general x6, matrix products, contract(): lax.dot_general(left, right, (((1,), (1,)), ((), ())), preferred_element_...  14.5 us
    all_gather x1, waiting for transfers between devices, per_device(): neighbours = lax.all_gather(own_cols, 'mp', axis=1, tiled=True)  14.1 us
    ppermute x1, waiting for transfers between devices, per_device(): lax.ppermute(both_cols, 'group', swap)  14.1 us
  transfers between devices with their start and end apart: 15, of which 10 were waited for; matrix products, arithmetic and copies ran while one was open for 14% of the time, Pallas kernels for 0%

profile of v14, /device:TPU:192, one launch (start us, length us, event | category | flops | bytes accessed | tf_op | source)
XLA Modules:
  0.0 349.7 jit_solution(14869014002450996128)
XLA Ops:
  11.9 6.3 %all-to-all-start = ((f32[16,1,256]{2,1,0:T(1,128)}), f32[16,1,256]{2,1,0:T(1,128)S(1)}, u32[]{:S(2)}, u32[]{:S(2)}) async-start(f32[16,1,256]{2,1,0:T(1,128)} %broadcast_in_dim.19), calls=%async_computation | async-start | bytes 32768 | tf_op jit(solution)/shard_map/all_to_all | solution.py:69
  18.2 4.2 %all-to-all-done = f32[16,1,256]{2,1,0:T(1,128)S(1)} async-done(((f32[16,1,256]{2,1,0:T(1,128)}), f32[16,1,256]{2,1,0:T(1,128)S(1)}, u32[]{:S(2)}, u32[]{:S(2)}) %all-to-all-start) | async-done | bytes 16416 | tf_op jit(solution)/shard_map/all_to_all | solution.py:69
  23.9 7.9 %gather_fusion = bf16[1024,512]{1,0:T(8,128)(2,1)} fusion(bf16[4096,512]{1,0:T(8,128)(2,1)} %param.12, s32[1024]{0:T(1024)S(1)} %broadcast_clamp_fusion), kind=kCustom, calls=%fused_computation | custom fusion | bytes 2101248 | tf_op jit(solution)/shard_map/gather | solution.py:76
  31.8 7.2 %all-to-all-start.1 = ((bf16[16,64,512]{2,1,0:T(8,128)(2,1)}), bf16[16,64,512]{2,1,0:T(8,128)(2,1)S(1)}, u32[]{:S(2)}, u32[]{:S(2)}) async-start(bf16[16,64,512]{2,1,0:T(8,128)(2,1)} %bitcast.107), calls=%async_computation.1 | async-start | bytes 2097152 | tf_op jit(solution)/shard_map/all_to_all | solution.py:77
  40.0 22.2 %all-to-all-done.1 = bf16[16,64,512]{2,1,0:T(8,128)(2,1)S(1)} async-done(((bf16[16,64,512]{2,1,0:T(8,128)(2,1)}), bf16[16,64,512]{2,1,0:T(8,128)(2,1)S(1)}, u32[]{:S(2)}, u32[]{:S(2)}) %all-to-all-start.1) | async-done | bytes 1048608 | tf_op jit(solution)/shard_map/all_to_all | solution.py:77
  65.2 4.6 %collective-permute-start = (bf16[512,512]{1,0:T(8,128)(2,1)S(1)}, bf16[512,512]{1,0:T(8,128)(2,1)S(1)}, u32[]{:S(2)}, u32[]{:S(2)}) collective-permute-start(bf16[512,512]{1,0:T(8,128)(2,1)S(1)} %fusion.46), channel_id=1, source_target_pairs={{0,1},{1,0},{2,3},{3,2},{4,5},{5,4},{6,7},{7,6},{8,9},{9,8},{10,11... | collective-permute-start | bytes 1572872 | tf_op jit(solution)/shard_map/ppermute | solution.py:46
  69.8 14.7 %collective-permute-done = bf16[512,512]{1,0:T(8,128)(2,1)S(1)} collective-permute-done((bf16[512,512]{1,0:T(8,128)(2,1)S(1)}, bf16[512,512]{1,0:T(8,128)(2,1)S(1)}, u32[]{:S(2)}, u32[]{:S(2)}) %collective-permute-start) | collective-permute-done | bytes 524320 | tf_op jit(solution)/shard_map/ppermute | solution.py:46
  84.5 12.2 %collective-permute-start.1 = (bf16[1,512,512]{2,1,0:T(8,128)(2,1)S(1)}, bf16[1,512,512]{2,1,0:T(8,128)(2,1)}, u32[]{:S(2)}, u32[]{:S(2)}) collective-permute-start(bf16[1,512,512]{2,1,0:T(8,128)(2,1)S(1)} %bitcast.116), channel_id=1, source_target_pairs={{0,128},{32,160},{64,192},{96,224},{128,0},{160,32},{192,64},{224,... | collective-permute-start | bytes 1572872 | tf_op jit(solution)/shard_map/ppermute | solution.py:51
  96.7 22.1 %collective-permute-done.1 = bf16[1,512,512]{2,1,0:T(8,128)(2,1)} collective-permute-done((bf16[1,512,512]{2,1,0:T(8,128)(2,1)S(1)}, bf16[1,512,512]{2,1,0:T(8,128)(2,1)}, u32[]{:S(2)}, u32[]{:S(2)}) %collective-permute-start.1) | collective-permute-done | bytes 524320 | tf_op jit(solution)/shard_map/ppermute | solution.py:51
  120.6 2.4 collective-permute-start.2
  123.0 23.5 %collective-permute-done.2 = bf16[2,512,512]{2,1,0:T(8,128)(2,1)} collective-permute-done((bf16[2,512,512]{2,1,0:T(8,128)(2,1)S(1)}, bf16[2,512,512]{2,1,0:T(8,128)(2,1)}, u32[]{:S(2)}, u32[]{:S(2)}) %collective-permute-start.2) | collective-permute-done | bytes 1048608 | tf_op jit(solution)/shard_map/ppermute | solution.py:51
  146.5 3.2 maximum_select_fusion.2
  149.8 2.4 fusion.43
  152.1 4.3 %collective-permute-start.4 = (f32[128,256]{1,0:T(8,128)S(1)}, f32[128,256]{1,0:T(8,128)S(1)}, u32[]{:S(2)}, u32[]{:S(2)}) collective-permute-start(f32[128,256]{1,0:T(8,128)S(1)} %fusion.43), channel_id=1, source_target_pairs={{0,1},{1,0},{2,3},{3,2},{4,5},{5,4},{6,7},{7,6},{8,9},{9,8},{10,11... | collective-permute-start | bytes 393224 | tf_op jit(solution)/shard_map/ppermute | solution.py:34
  156.4 2.1 fusion.41
  160.3 3.3 collective-permute-done.4
  163.7 3.8 %maximum_select_fusion.1 = bf16[8,512,512]{2,1,0:T(8,128)(2,1)S(1)} fusion(bf16[4,512,512]{2,1,0:T(8,128)(2,1)} %collective-permute-done.3, bf16[4,512,512]{2,1,0:T(8,128)(2,1)} %maximum_select_fusion.2, pred[]{:T(512)S(6)} %eq.62), kind=kLoop, calls=%fused_computation.11 | loop fusion | flops 6291456 | bytes 8388609 | tf_op jit(solution)/shard_map/jit(_where)/select_n | solution.py:53
  167.5 2.4 copy.79
  169.9 14.1 %all-gather.9.cloned.1.call-done = bf16[256,8192]{1,0:T(8,128)(2,1)} async-done(((bf16[256,512]{1,0:T(8,128)(2,1)}), bf16[256,8192]{1,0:T(8,128)(2,1)}) %all-gather.9.cloned.1.call-update) | async-done | bytes 4194320 | tf_op jit(solution)/shard_map/all_gather | solution.py:84
  184.1 3.1 fusion.12
  187.5 2.4 fusion.25
  189.9 3.1 fusion.10
  193.4 2.3 fusion.30
  196.4 2.2 collective-permute-start.5
  198.7 9.2 %collective-permute-done.5 = f32[33024]{0:T(1024)S(1)} collective-permute-done((f32[33024]{0:T(1024)S(1)}, f32[33024]{0:T(1024)S(1)}, u32[]{:S(2)}, u32[]{:S(2)}) %collective-permute-start.5) | collective-permute-done | bytes 132128 | tf_op jit(solution)/shard_map/ppermute | solution.py:34
  209.7 4.4 %fusion.4 = f32[256,4096]{1,0:T(8,128)} fusion(bf16[4096,512]{1,0:T(8,128)(2,1)} %bitcast.101, bf16[32,8,2,128]{3,2,1,0:T(2,128)(2,1)S(1)} %bitcast.110), kind=kOutput, calls=%fused_computation.18 | convolution fusion | flops 536870912 | bytes 6422528 | tf_op jit(solution)/shard_map/dot_general | solution.py:14
  214.1 2.7 fusion.50
  217.0 2.1 collective-permute-start.7
  219.1 3.7 %convolution_add_fusion = bf16[256,4096]{1,0:T(8,128)(2,1)S(1)} fusion(f32[256,4096]{1,0:T(8,128)} %fusion.4, bf16[4096,512]{1,0:T(8,128)(2,1)} %bitcast.102, bf16[32,8,2,128]{3,2,1,0:T(2,128)(2,1)S(1)} %bitcast.108), kind=kOutput, calls=%fused_computation.5 | convolution fusion | flops 538968064 | bytes 8519680 | tf_op jit(solution)/shard_map/dot_general | solution.py:14
  229.0 3.9 %pad_maximum_fusion = bf16[512,8192]{1,0:T(8,128)(2,1)} fusion(bf16[256,8192]{1,0:T(8,128)(2,1)S(1)} %fusion, bf16[128,8192]{1,0:T(8,128)(2,1)S(1)} %pad_select_fusion, bf16[128,8192]{1,0:T(8,128)(2,1)S(1)} %pad_select_fusion.1), kind=kLoop, calls=%fused_computation.4 | loop fusion | flops 25165824 | bytes 16777216 | tf_op jit(solution)/shard_map/concatenate | solution.py:163
  233.0 89.6 %reduce-scatter.2.cloned.1.call-done = bf16[512,512]{1,0:T(8,128)(2,1)} async-done(((bf16[512,8192]{1,0:T(8,128)(2,1)}), bf16[512,512]{1,0:T(8,128)(2,1)}) %reduce-scatter.2.cloned.1.call-update) | async-done | bytes 524304 | tf_op jit(solution)/shard_map/reduce_scatter | solution.py:171
  325.6 14.1 %collective-permute-done.8 = bf16[256,512]{1,0:T(8,128)(2,1)S(1)} collective-permute-done((bf16[256,512]{1,0:T(8,128)(2,1)S(1)}, bf16[256,512]{1,0:T(8,128)(2,1)S(1)}, u32[]{:S(2)}, u32[]{:S(2)}) %collective-permute-start.8) | collective-permute-done | bytes 262176 | tf_op jit(solution)/shard_map/ppermute | solution.py:173
  (110 shorter events, 29.7 us)
Async XLA Ops:
  7.2 149.2 %copy-start = (bf16[256,4096]{1,0:T(8,128)(2,1)S(1)}, bf16[256,4096]{1,0:T(8,128)(2,1)}, u32[]{:S(2)}) copy-start(bf16[256,4096]{1,0:T(8,128)(2,1)} %param.16) | copy-start | bytes 6291460
  7.2 142.6 %all-gather.5.cloned.1.call-start = ((), (), s32[]{:S(2)}) async-start(), calls=%async_computation.3 | async-start | bytes 2228224 | tf_op jit(solution)/shard_map/all_gather | solution.py:40
  9.0 147.4 %all-gather.7.cloned.1.call-start = ((), (), s32[]{:S(2)}) async-start(), calls=%async_computation.4 | async-start | bytes 2228224 | tf_op jit(solution)/shard_map/all_gather | solution.py:41
  11.9 10.6 %all-to-all-start = ((f32[16,1,256]{2,1,0:T(1,128)}), f32[16,1,256]{2,1,0:T(1,128)S(1)}, u32[]{:S(2)}, u32[]{:S(2)}) async-start(f32[16,1,256]{2,1,0:T(1,128)} %broadcast_in_dim.19), calls=%async_computation | async-start | bytes 32768 | tf_op jit(solution)/shard_map/all_to_all | solution.py:69
  31.8 7.2 %copy-start.8 = (s32[2,1,128]{2,1,0:T(1,128)S(1)}, s32[2,1,128]{2,1,0:T(1,128)}, u32[]{:S(2)}) copy-start(s32[2,1,128]{2,1,0:T(1,128)} %param.10) | copy-start | bytes 3076
  31.8 30.4 %all-to-all-start.1 = ((bf16[16,64,512]{2,1,0:T(8,128)(2,1)}), bf16[16,64,512]{2,1,0:T(8,128)(2,1)S(1)}, u32[]{:S(2)}, u32[]{:S(2)}) async-start(bf16[16,64,512]{2,1,0:T(8,128)(2,1)} %bitcast.107), calls=%async_computation.1 | async-start | bytes 2097152 | tf_op jit(solution)/shard_map/all_to_all | solution.py:77
  38.9 145.1 %all-gather.9.cloned.1.call-start = ((), (), s32[]{:S(2)}) async-start(), calls=%async_computation.6 | async-start | bytes 4456448 | tf_op jit(solution)/shard_map/all_gather | solution.py:84
  64.1 258.5 %reduce-scatter.2.cloned.1.call-start = ((), (), s32[]{:S(2)}) async-start(), calls=%async_computation.5 | async-start | bytes 8912896 | tf_op jit(solution)/shard_map/reduce_scatter | solution.py:171
  65.2 19.3 %collective-permute-start = (bf16[512,512]{1,0:T(8,128)(2,1)S(1)}, bf16[512,512]{1,0:T(8,128)(2,1)S(1)}, u32[]{:S(2)}, u32[]{:S(2)}) collective-permute-start(bf16[512,512]{1,0:T(8,128)(2,1)S(1)} %fusion.46), channel_id=1, source_target_pairs={{0,1},{1,0},{2,3},{3,2},{4,5},{5,4},{6,7},{7,6},{8,9},{9,8},{10,11... | collective-permute-start | bytes 1572872 | tf_op jit(solution)/shard_map/ppermute | solution.py:46
  84.5 12.2 %copy-start.7 = (bf16[512,512]{1,0:T(8,128)(2,1)}, bf16[512,512]{1,0:T(8,128)(2,1)S(1)}, u32[]{:S(2)}) copy-start(bf16[512,512]{1,0:T(8,128)(2,1)S(1)} %collective-permute-done) | copy-start | bytes 1572868
  84.5 34.3 %collective-permute-start.1 = (bf16[1,512,512]{2,1,0:T(8,128)(2,1)S(1)}, bf16[1,512,512]{2,1,0:T(8,128)(2,1)}, u32[]{:S(2)}, u32[]{:S(2)}) collective-permute-start(bf16[1,512,512]{2,1,0:T(8,128)(2,1)S(1)} %bitcast.116), channel_id=1, source_target_pairs={{0,128},{32,160},{64,192},{96,224},{128,0},{160,32},{192,64},{224,... | collective-permute-start | bytes 1572872 | tf_op jit(solution)/shard_map/ppermute | solution.py:51
  120.6 25.9 %collective-permute-start.2 = (bf16[2,512,512]{2,1,0:T(8,128)(2,1)S(1)}, bf16[2,512,512]{2,1,0:T(8,128)(2,1)}, u32[]{:S(2)}, u32[]{:S(2)}) collective-permute-start(bf16[2,512,512]{2,1,0:T(8,128)(2,1)S(1)} %maximum_select_fusion.3), channel_id=1, source_target_pairs={{0,64},{32,96},{64,0},{96,32},{128,192},{160,224},{192,128},{224,1... | collective-permute-start | bytes 3145736 | tf_op jit(solution)/shard_map/ppermute | solution.py:51
  123.0 26.7 %copy-start.9 = (s32[2]{0:T(128)S(1)}, s32[2]{0:T(128)}, u32[]{:S(2)}) copy-start(s32[2]{0:T(128)} %param.11) | copy-start | bytes 28
  149.7 13.9 %collective-permute-start.3 = (bf16[4,512,512]{2,1,0:T(8,128)(2,1)}, bf16[4,512,512]{2,1,0:T(8,128)(2,1)}, u32[]{:S(2)}, u32[]{:S(2)}) collective-permute-start(bf16[4,512,512]{2,1,0:T(8,128)(2,1)} %maximum_select_fusion.2), channel_id=1, source_target_pairs={{0,32},{32,0},{64,96},{96,64},{128,160},{160,128},{192,224},{224,1... | collective-permute-start | bytes 6291464 | tf_op jit(solution)/shard_map/ppermute | solution.py:51
  152.1 11.5 %collective-permute-start.4 = (f32[128,256]{1,0:T(8,128)S(1)}, f32[128,256]{1,0:T(8,128)S(1)}, u32[]{:S(2)}, u32[]{:S(2)}) collective-permute-start(f32[128,256]{1,0:T(8,128)S(1)} %fusion.43), channel_id=1, source_target_pairs={{0,1},{1,0},{2,3},{3,2},{4,5},{5,4},{6,7},{7,6},{8,9},{9,8},{10,11... | collective-permute-start | bytes 393224 | tf_op jit(solution)/shard_map/ppermute | solution.py:34
  158.5 40.2 %collective-permute-start.6 = (f32[128,256]{1,0:T(8,128)S(1)}, f32[128,256]{1,0:T(8,128)S(1)}, u32[]{:S(2)}, u32[]{:S(2)}) collective-permute-start(f32[128,256]{1,0:T(8,128)S(1)} %fusion.41), channel_id=1, source_target_pairs={{0,1},{1,0},{2,3},{3,2},{4,5},{5,4},{6,7},{7,6},{8,9},{9,8},{10,11... | collective-permute-start | bytes 393224 | tf_op jit(solution)/shard_map/ppermute | solution.py:34
  184.1 3.4 copy-start.3
  189.9 3.5 copy-start.4
  196.4 11.5 %collective-permute-start.5 = (f32[33024]{0:T(1024)S(1)}, f32[33024]{0:T(1024)S(1)}, u32[]{:S(2)}, u32[]{:S(2)}) collective-permute-start(f32[33024]{0:T(1024)S(1)} %pad_maximum_fusion.1), channel_id=1, source_target_pairs={{0,1},{1,0},{2,3},{3,2},{4,5},{5,4},{6,7},{7,6},{8,9},{9,8},{10,11... | collective-permute-start | bytes 396296 | tf_op jit(solution)/shard_map/ppermute | solution.py:34
  209.7 4.4 %copy-start.1 = (bf16[4096,256]{1,0:T(8,128)(2,1)S(1)}, bf16[4096,256]{1,0:T(8,128)(2,1)}, u32[]{:S(2)}) copy-start(bf16[4096,256]{1,0:T(8,128)(2,1)} %param.14) | copy-start | bytes 6291460
  217.0 9.7 %collective-permute-start.7 = (f32[2,64,2,128]{3,1,2,0:T(8,128)S(1)}, f32[2,64,2,128]{3,1,2,0:T(8,128)S(1)}, u32[]{:S(2)}, u32[]{:S(2)}) collective-permute-start(f32[2,64,2,128]{3,1,2,0:T(8,128)S(1)} %convolution_bitcast_fusion), channel_id=1, source_target_pairs={{0,1},{1,0},{2,3},{3,2},{4,5},{5,4},{6,7},{7,6},{8,9},{9,8},{10,11... | collective-permute-start | bytes 393224 | tf_op jit(solution)/shard_map/ppermute | solution.py:34
  219.1 3.7 %copy-start.2 = (bf16[4096,256]{1,0:T(8,128)(2,1)S(1)}, bf16[4096,256]{1,0:T(8,128)(2,1)}, u32[]{:S(2)}) copy-start(bf16[4096,256]{1,0:T(8,128)(2,1)} %param.15) | copy-start | bytes 6291460
  219.1 4.7 %copy-start.5 = (f32[256,4096]{1,0:T(8,128)S(1)}, f32[256,4096]{1,0:T(8,128)}, u32[]{:S(2)}) copy-start(f32[256,4096]{1,0:T(8,128)} %fusion.50) | copy-start | bytes 12582916
  226.2 1.6 copy-start.6
  323.6 16.2 %collective-permute-start.8 = (bf16[256,512]{1,0:T(8,128)(2,1)S(1)}, bf16[256,512]{1,0:T(8,128)(2,1)S(1)}, u32[]{:S(2)}, u32[]{:S(2)}) collective-permute-start(bf16[256,512]{1,0:T(8,128)(2,1)S(1)} %slice.89), channel_id=1, source_target_pairs={{0,1},{1,0},{2,3},{3,2},{4,5},{5,4},{6,7},{7,6},{8,9},{9,8},{10,11... | collective-permute-start | bytes 786440 | tf_op jit(solution)/shard_map/ppermute | solution.py:173
Sparse Core Ops, SparseCore 0:
  11.0 53.4 all-gather.4
  66.9 52.0 all-gather.6
  122.0 62.0 all-gather.8
  233.1 89.4 reduce-scatter.1

commit v15 on v11

--- a/solution.py
+++ b/solution.py
@@ -36,11 +36,11 @@
     pad_rows = jnp.zeros((tail_rows, hidden.shape[1]), jnp.bfloat16)
     query_rows = jnp.concatenate([hidden[tail_rows:], pad_rows], 0)
     grad_rows = jnp.concatenate([grad_out[tail_rows:], pad_rows], 0)
+    full_query = lax.all_gather(query_rows, "mp", axis=1, tiled=True)
     n_mp = lax.axis_size("mp")
     me_mp = lax.axis_index("mp")
-    rows2 = jnp.stack([query_rows, grad_rows])
-    across = lax.ppermute(rows2, "mp", [(i, i ^ (n_mp // 2)) for i in range(n_mp)])
-    held_rows = jnp.where(me_mp // (n_mp // 2) == me_group, rows2, across)[None]
+    across = lax.ppermute(grad_rows, "mp", [(i, i ^ (n_mp // 2)) for i in range(n_mp)])
+    held_rows = jnp.where(me_mp // (n_mp // 2) == me_group, grad_rows, across)[None]
     bit = n_mp // 4
     while bit >= 1:
         pairs = [(i, i ^ bit) for i in range(n_mp)]
@@ -54,13 +54,10 @@
         bit //= 2
     m_bits = (n_mp // 2).bit_length() - 1
     held_rows = held_rows.reshape((2,) * m_bits + held_rows.shape[1:])
-    held_rows = jnp.transpose(
-        held_rows, (m_bits,) + tuple(reversed(range(m_bits))) + (m_bits + 1, m_bits + 2)
-    )
-    halves = jnp.transpose(
-        held_rows.reshape((2, n_mp // 2) + held_rows.shape[-2:]), (0, 2, 1, 3)
-    ).reshape(2, rows_here, half)
-    query_half, grad_half = halves[0], halves[1]
+    held_rows = jnp.transpose(held_rows, tuple(reversed(range(m_bits))) + (m_bits, m_bits + 1))
+    grad_half = jnp.transpose(
+        held_rows.reshape((n_mp // 2,) + held_rows.shape[-2:]), (1, 0, 2)
+    ).reshape(rows_here, half)
     piece_rows = half // lax.axis_size("dp")
     kv_local = jnp.concatenate([w_key, w_value], axis=1)
     kv_piece = lax.dynamic_slice_in_dim(kv_local, me_dp * piece_rows, piece_rows, 0)
@@ -110,7 +107,7 @@
     def other_half(x):
         return lax.dynamic_slice_in_dim(x, (1 - me_group) * half, half, 1)
 
-    query_part = jnp.dot(query_half, w_query, preferred_element_type=jnp.float32)
+    query_part = jnp.dot(this_half(full_query), w_query, preferred_element_type=jnp.float32)
     query = group_sum(query_part).astype(jnp.bfloat16)
     n_here, n_there = this_half(neighbours), other_half(neighbours)
     keys = (

time: 362 us -> 358 us (0.989)
  other arithmetic: 29 us -> 22.5 us
  waiting for transfers between devices: 212 us -> 216 us
    ppermute x3, waiting for transfers between devices: 29.8 us -> 16.7 us  [per_device(): other = lax.ppermute(held_rows, 'mp', pairs)]
    ppermute x1, waiting for transfers between devices: 0.01 us -> 6.89 us  [per_device(): lax.ppermute(grad_rows, 'mp', [(i, i ^ n_mp // 2) for i in range(n_mp)])]
    ppermute x3, waiting for transfers between devices: 21.3 us -> 26.8 us  [per_device(): other = lax.ppermute(held, 'dp', pairs)]
    select_n x3, other arithmetic: 7.28 us -> 2.29 us  [per_device(): jnp.where(low, jnp.concatenate([held_rows, other], 0), jnp.concatenate([o...]
    slice x4 -> x1, local copies, waits for them, and re-layouts: 4.97 us -> 0.18 us  [the longest x3 4.79 us: per_device(): query_half, grad_half = (halves[0], halves[1])]
  transfers between devices with their start and end apart: 18 -> 19, of which waited for: 14 -> 15; matrix products, arithmetic and copies ran while one was open for 9% -> 11% of each run, Pallas kernels for 0% -> 0%
where the time goes in v15:
time: 358 us; the launch traced here: 356 us
  waiting for transfers between devices  216 us (60%)
  starting transfers between devices  59.3 us (17%)
  other arithmetic  22.5 us (6%)
  local copies, waits for them, and re-layouts  22.2 us (6%)
  matrix products  21.3 us (6%)
  between operations  14.2 us (4%)
    reduce_scatter x1, waiting for transfers between devices, per_device(): reduced = lax.psum_scatter(stacked, 'mp', scatter_dimension=1, tiled=True)  91 us
    ppermute x3, waiting for transfers between devices, per_device(): other = lax.ppermute(held, 'dp', pairs)  26.8 us
    all_to_all x1, waiting for transfers between devices, per_device(): recv_buf = lax.all_to_all(send_buf, ('dp', 'group'), 0, 0, tiled=True)  22.2 us
    ppermute x5, waiting for transfers between devices, group_sum(): return x + lax.ppermute(x, 'group', swap)  19.6 us
    ppermute x3, waiting for transfers between devices, per_device(): other = lax.ppermute(held_rows, 'mp', pairs)  16.7 us
    ppermute x5, starting transfers between devices, group_sum(): return x + lax.ppermute(x, 'group', swap)  15.9 us
    ppermute x1, waiting for transfers between devices, per_device(): held = lax.ppermute(kv_piece, 'group', swap)[None]  14.7 us
    ppermute x3, starting transfers between devices, per_device(): other = lax.ppermute(held, 'dp', pairs)  14.6 us
  transfers between devices with their start and end apart: 19, of which 15 were waited for; matrix products, arithmetic and copies ran while one was open for 11% of the time, Pallas kernels for 0%

profile of v15, /device:TPU:192, one launch (start us, length us, event | category | flops | bytes accessed | tf_op | source)
XLA Modules:
  0.0 356.1 jit_solution(9898570484650482912)
XLA Ops:
  10.3 6.3 %all-to-all-start = ((f32[16,1,256]{2,1,0:T(1,128)}), f32[16,1,256]{2,1,0:T(1,128)S(1)}, u32[]{:S(2)}, u32[]{:S(2)}) async-start(f32[16,1,256]{2,1,0:T(1,128)} %broadcast_in_dim.21), calls=%async_computation | async-start | bytes 32768 | tf_op jit(solution)/shard_map/all_to_all | solution.py:87
  16.6 4.2 %all-to-all-done = f32[16,1,256]{2,1,0:T(1,128)S(1)} async-done(((f32[16,1,256]{2,1,0:T(1,128)}), f32[16,1,256]{2,1,0:T(1,128)S(1)}, u32[]{:S(2)}, u32[]{:S(2)}) %all-to-all-start) | async-done | bytes 16416 | tf_op jit(solution)/shard_map/all_to_all | solution.py:87
  22.3 7.9 %gather_fusion = bf16[1024,512]{1,0:T(8,128)(2,1)} fusion(bf16[4096,512]{1,0:T(8,128)(2,1)} %param.12, s32[1024]{0:T(1024)S(1)} %broadcast_clamp_fusion), kind=kCustom, calls=%fused_computation | custom fusion | bytes 2101248 | tf_op jit(solution)/shard_map/gather | solution.py:94
  30.1 7.2 %all-to-all-start.1 = ((bf16[16,64,512]{2,1,0:T(8,128)(2,1)}), bf16[16,64,512]{2,1,0:T(8,128)(2,1)S(1)}, u32[]{:S(2)}, u32[]{:S(2)}) async-start(bf16[16,64,512]{2,1,0:T(8,128)(2,1)} %bitcast.113), calls=%async_computation.1 | async-start | bytes 2097152 | tf_op jit(solution)/shard_map/all_to_all | solution.py:95
  38.3 22.2 %all-to-all-done.1 = bf16[16,64,512]{2,1,0:T(8,128)(2,1)S(1)} async-done(((bf16[16,64,512]{2,1,0:T(8,128)(2,1)}), bf16[16,64,512]{2,1,0:T(8,128)(2,1)S(1)}, u32[]{:S(2)}, u32[]{:S(2)}) %all-to-all-start.1) | async-done | bytes 1048608 | tf_op jit(solution)/shard_map/all_to_all | solution.py:95
  63.5 4.6 %collective-permute-start = (bf16[512,512]{1,0:T(8,128)(2,1)S(1)}, bf16[512,512]{1,0:T(8,128)(2,1)S(1)}, u32[]{:S(2)}, u32[]{:S(2)}) collective-permute-start(bf16[512,512]{1,0:T(8,128)(2,1)S(1)} %fusion.44), channel_id=1, source_target_pairs={{0,1},{1,0},{2,3},{3,2},{4,5},{5,4},{6,7},{7,6},{8,9},{9,8},{10,11... | collective-permute-start | bytes 1572872 | tf_op jit(solution)/shard_map/ppermute | solution.py:64
  68.1 14.7 %collective-permute-done = bf16[512,512]{1,0:T(8,128)(2,1)S(1)} collective-permute-done((bf16[512,512]{1,0:T(8,128)(2,1)S(1)}, bf16[512,512]{1,0:T(8,128)(2,1)S(1)}, u32[]{:S(2)}, u32[]{:S(2)}) %collective-permute-start) | collective-permute-done | bytes 524320 | tf_op jit(solution)/shard_map/ppermute | solution.py:64
  82.9 12.2 %collective-permute-start.1 = (bf16[1,512,512]{2,1,0:T(8,128)(2,1)S(1)}, bf16[1,512,512]{2,1,0:T(8,128)(2,1)}, u32[]{:S(2)}, u32[]{:S(2)}) collective-permute-start(bf16[1,512,512]{2,1,0:T(8,128)(2,1)S(1)} %bitcast.122), channel_id=1, source_target_pairs={{0,128},{32,160},{64,192},{96,224},{128,0},{160,32},{192,64},{224,... | collective-permute-start | bytes 1572872 | tf_op jit(solution)/shard_map/ppermute | solution.py:69
  95.1 22.1 %collective-permute-done.1 = bf16[1,512,512]{2,1,0:T(8,128)(2,1)} collective-permute-done((bf16[1,512,512]{2,1,0:T(8,128)(2,1)S(1)}, bf16[1,512,512]{2,1,0:T(8,128)(2,1)}, u32[]{:S(2)}, u32[]{:S(2)}) %collective-permute-start.1) | collective-permute-done | bytes 524320 | tf_op jit(solution)/shard_map/ppermute | solution.py:69
  118.9 2.4 collective-permute-start.2
  121.3 3.1 collective-permute-start.7
  124.4 6.9 %collective-permute-done.7 = bf16[128,512]{1,0:T(8,128)(2,1)S(1)} collective-permute-done((bf16[128,512]{1,0:T(8,128)(2,1)S(1)}, bf16[128,512]{1,0:T(8,128)(2,1)S(1)}, u32[]{:S(2)}, u32[]{:S(2)}) %collective-permute-start.7) | collective-permute-done | bytes 131104 | tf_op jit(solution)/shard_map/ppermute | solution.py:42
  132.6 4.0 %collective-permute-done.8 = bf16[1,128,512]{2,1,0:T(8,128)(2,1)} collective-permute-done((bf16[1,128,512]{2,1,0:T(8,128)(2,1)S(1)}, bf16[1,128,512]{2,1,0:T(8,128)(2,1)}, u32[]{:S(2)}, u32[]{:S(2)}) %collective-permute-start.8) | collective-permute-done | bytes 131104 | tf_op jit(solution)/shard_map/ppermute | solution.py:47
  137.6 2.5 collective-permute-start.9
  140.1 4.7 %collective-permute-done.2 = bf16[2,512,512]{2,1,0:T(8,128)(2,1)} collective-permute-done((bf16[2,512,512]{2,1,0:T(8,128)(2,1)S(1)}, bf16[2,512,512]{2,1,0:T(8,128)(2,1)}, u32[]{:S(2)}, u32[]{:S(2)}) %collective-permute-start.2) | collective-permute-done | bytes 1048608 | tf_op jit(solution)/shard_map/ppermute | solution.py:69
  144.7 3.3 maximum_select_fusion.2
  150.8 12.8 %collective-permute-done.10 = bf16[4,128,512]{2,1,0:T(8,128)(2,1)S(1)} collective-permute-done((bf16[4,128,512]{2,1,0:T(8,128)(2,1)S(1)}, bf16[4,128,512]{2,1,0:T(8,128)(2,1)S(1)}, u32[]{:S(2)}, u32[]{:S(2)}) %collective-permute-start.10) | collective-permute-done | bytes 524320 | tf_op jit(solution)/shard_map/ppermute | solution.py:47
  167.3 4.3 %collective-permute-start.11 = (f32[128,256]{1,0:T(8,128)S(1)}, f32[128,256]{1,0:T(8,128)S(1)}, u32[]{:S(2)}, u32[]{:S(2)}) collective-permute-start(f32[128,256]{1,0:T(8,128)S(1)} %fusion.80), channel_id=1, source_target_pairs={{0,1},{1,0},{2,3},{3,2},{4,5},{5,4},{6,7},{7,6},{8,9},{9,8},{10,11... | collective-permute-start | bytes 393224 | tf_op jit(solution)/shard_map/ppermute | solution.py:34
  178.1 9.1 %collective-permute-done.4 = f32[128,256]{1,0:T(8,128)S(1)} collective-permute-done((f32[128,256]{1,0:T(8,128)S(1)}, f32[128,256]{1,0:T(8,128)S(1)}, u32[]{:S(2)}, u32[]{:S(2)}) %collective-permute-start.4) | collective-permute-done | bytes 131104 | tf_op jit(solution)/shard_map/ppermute | solution.py:34
  187.2 4.0 %maximum_select_fusion.1 = bf16[8,512,512]{2,1,0:T(8,128)(2,1)S(1)} fusion(bf16[4,512,512]{2,1,0:T(8,128)(2,1)} %collective-permute-done.3, bf16[4,512,512]{2,1,0:T(8,128)(2,1)} %maximum_select_fusion.2, pred[]{:T(512)S(6)} %eq.77), kind=kLoop, calls=%fused_computation.11 | loop fusion | flops 6291456 | bytes 8388609 | tf_op jit(solution)/shard_map/jit(_where)/select_n | solution.py:71
  191.1 2.4 copy.80
  193.6 3.1 fusion.12
  197.0 2.4 fusion.25
  199.4 3.1 fusion.10
  205.6 2.7 collective-permute-start.6
  208.5 3.4 collective-permute-start.5
  213.7 4.9 %collective-permute-done.5 = f32[2,64,2,128]{3,1,2,0:T(8,128)S(1)} collective-permute-done((f32[2,64,2,128]{3,1,2,0:T(8,128)S(1)}, f32[2,64,2,128]{3,1,2,0:T(8,128)S(1)}, u32[]{:S(2)}, u32[]{:S(2)}) %collective-permute-start.5) | collective-permute-done | bytes 131104 | tf_op jit(solution)/shard_map/ppermute | solution.py:34
  219.5 2.5 fusion.4
  222.9 3.6 collective-permute-start.12
  234.2 3.6 %pad_maximum_fusion = bf16[512,8192]{1,0:T(8,128)(2,1)} fusion(bf16[256,8192]{1,0:T(8,128)(2,1)S(1)} %fusion, bf16[128,8192]{1,0:T(8,128)(2,1)S(1)} %get-tuple-element.28, bf16[128,8192]{1,0:T(8,128)(2,1)S(1)} %get-tuple-element.29), kind=kLoop, calls=%fused_computation.4 | loop fusion | flops 25165824 | bytes 16777216 | tf_op jit(solution)/shard_map/concatenate | solution.py:178
  237.8 91.0 %reduce-scatter.2.cloned.1.call-done = bf16[512,512]{1,0:T(8,128)(2,1)} async-done(((bf16[512,8192]{1,0:T(8,128)(2,1)}), bf16[512,512]{1,0:T(8,128)(2,1)}) %reduce-scatter.2.cloned.1.call-update) | async-done | bytes 524304 | tf_op jit(solution)/shard_map/reduce_scatter | solution.py:186
  331.9 14.2 %collective-permute-done.13 = bf16[256,512]{1,0:T(8,128)(2,1)S(1)} collective-permute-done((bf16[256,512]{1,0:T(8,128)(2,1)S(1)}, bf16[256,512]{1,0:T(8,128)(2,1)S(1)}, u32[]{:S(2)}, u32[]{:S(2)}) %collective-permute-start.13) | collective-permute-done | bytes 262176 | tf_op jit(solution)/shard_map/ppermute | solution.py:188
  (115 shorter events, 46.8 us)
Async XLA Ops:
  7.2 159.3 %copy-start = (bf16[256,4096]{1,0:T(8,128)(2,1)S(1)}, bf16[256,4096]{1,0:T(8,128)(2,1)}, u32[]{:S(2)}) copy-start(bf16[256,4096]{1,0:T(8,128)(2,1)} %param.16) | copy-start | bytes 6291460
  7.2 164.4 %all-gather.4.cloned.1.call-start = ((), (), s32[]{:S(2)}) async-start(), calls=%async_computation.3 | async-start | bytes 2228224 | tf_op jit(solution)/shard_map/all_gather | solution.py:39
  10.3 10.6 %all-to-all-start = ((f32[16,1,256]{2,1,0:T(1,128)}), f32[16,1,256]{2,1,0:T(1,128)S(1)}, u32[]{:S(2)}, u32[]{:S(2)}) async-start(f32[16,1,256]{2,1,0:T(1,128)} %broadcast_in_dim.21), calls=%async_computation | async-start | bytes 32768 | tf_op jit(solution)/shard_map/all_to_all | solution.py:87
  30.1 7.2 %copy-start.9 = (s32[2,1,128]{2,1,0:T(1,128)S(1)}, s32[2,1,128]{2,1,0:T(1,128)}, u32[]{:S(2)}) copy-start(s32[2,1,128]{2,1,0:T(1,128)} %param.10) | copy-start | bytes 3076
  30.1 30.4 %all-to-all-start.1 = ((bf16[16,64,512]{2,1,0:T(8,128)(2,1)}), bf16[16,64,512]{2,1,0:T(8,128)(2,1)S(1)}, u32[]{:S(2)}, u32[]{:S(2)}) async-start(bf16[16,64,512]{2,1,0:T(8,128)(2,1)} %bitcast.113), calls=%async_computation.1 | async-start | bytes 2097152 | tf_op jit(solution)/shard_map/all_to_all | solution.py:95
  37.3 156.3 %all-gather.6.cloned.1.call-start = ((), (), s32[]{:S(2)}) async-start(), calls=%async_computation.5 | async-start | bytes 4456448 | tf_op jit(solution)/shard_map/all_gather | solution.py:102
  62.4 266.4 %reduce-scatter.2.cloned.1.call-start = ((), (), s32[]{:S(2)}) async-start(), calls=%async_computation.4 | async-start | bytes 8912896 | tf_op jit(solution)/shard_map/reduce_scatter | solution.py:186
  63.5 57.8 %copy-start.8 = (bf16[128,512]{1,0:T(8,128)(2,1)S(1)}, bf16[128,512]{1,0:T(8,128)(2,1)}, u32[]{:S(2)}) copy-start(bf16[128,512]{1,0:T(8,128)(2,1)} %param.17) | copy-start | bytes 393220
  63.5 19.3 %collective-permute-start = (bf16[512,512]{1,0:T(8,128)(2,1)S(1)}, bf16[512,512]{1,0:T(8,128)(2,1)S(1)}, u32[]{:S(2)}, u32[]{:S(2)}) collective-permute-start(bf16[512,512]{1,0:T(8,128)(2,1)S(1)} %fusion.44), channel_id=1, source_target_pairs={{0,1},{1,0},{2,3},{3,2},{4,5},{5,4},{6,7},{7,6},{8,9},{9,8},{10,11... | collective-permute-start | bytes 1572872 | tf_op jit(solution)/shard_map/ppermute | solution.py:64
  82.9 12.2 %copy-start.7 = (bf16[512,512]{1,0:T(8,128)(2,1)}, bf16[512,512]{1,0:T(8,128)(2,1)S(1)}, u32[]{:S(2)}) copy-start(bf16[512,512]{1,0:T(8,128)(2,1)S(1)} %collective-permute-done) | copy-start | bytes 1572868
  82.9 34.3 %collective-permute-start.1 = (bf16[1,512,512]{2,1,0:T(8,128)(2,1)S(1)}, bf16[1,512,512]{2,1,0:T(8,128)(2,1)}, u32[]{:S(2)}, u32[]{:S(2)}) collective-permute-start(bf16[1,512,512]{2,1,0:T(8,128)(2,1)S(1)} %bitcast.122), channel_id=1, source_target_pairs={{0,128},{32,160},{64,192},{96,224},{128,0},{160,32},{192,64},{224,... | collective-permute-start | bytes 1572872 | tf_op jit(solution)/shard_map/ppermute | solution.py:69
  118.9 25.9 %collective-permute-start.2 = (bf16[2,512,512]{2,1,0:T(8,128)(2,1)S(1)}, bf16[2,512,512]{2,1,0:T(8,128)(2,1)}, u32[]{:S(2)}, u32[]{:S(2)}) collective-permute-start(bf16[2,512,512]{2,1,0:T(8,128)(2,1)S(1)} %maximum_select_fusion.3), channel_id=1, source_target_pairs={{0,64},{32,96},{64,0},{96,32},{128,192},{160,224},{192,128},{224,1... | collective-permute-start | bytes 3145736 | tf_op jit(solution)/shard_map/ppermute | solution.py:69
  121.3 10.0 %collective-permute-start.7 = (bf16[128,512]{1,0:T(8,128)(2,1)S(1)}, bf16[128,512]{1,0:T(8,128)(2,1)S(1)}, u32[]{:S(2)}, u32[]{:S(2)}) collective-permute-start(bf16[128,512]{1,0:T(8,128)(2,1)S(1)} %concatenate.82), channel_id=1, source_target_pairs={{0,16},{2,18},{4,20},{6,22},{8,24},{10,26},{12,28},{14,30},{16,0},... | collective-permute-start | bytes 393224 | tf_op jit(solution)/shard_map/ppermute | solution.py:42
  131.4 5.2 %collective-permute-start.8 = (bf16[1,128,512]{2,1,0:T(8,128)(2,1)S(1)}, bf16[1,128,512]{2,1,0:T(8,128)(2,1)}, u32[]{:S(2)}, u32[]{:S(2)}) collective-permute-start(bf16[1,128,512]{2,1,0:T(8,128)(2,1)S(1)} %select_bitcast_fusion), channel_id=1, source_target_pairs={{0,8},{2,10},{4,12},{6,14},{8,0},{10,2},{12,4},{14,6},{16,24},{18,... | collective-permute-start | bytes 393224 | tf_op jit(solution)/shard_map/ppermute | solution.py:47
  137.5 13.3 %copy-start.10 = (s32[2]{0:T(128)S(1)}, s32[2]{0:T(128)}, u32[]{:S(2)}) copy-start(s32[2]{0:T(128)} %param.11) | copy-start | bytes 28
  137.6 10.5 %collective-permute-start.9 = (bf16[2,128,512]{2,1,0:T(8,128)(2,1)S(1)}, bf16[2,128,512]{2,1,0:T(8,128)(2,1)}, u32[]{:S(2)}, u32[]{:S(2)}) collective-permute-start(bf16[2,128,512]{2,1,0:T(8,128)(2,1)S(1)} %maximum_select_fusion.6), channel_id=1, source_target_pairs={{0,4},{2,6},{4,0},{6,2},{8,12},{10,14},{12,8},{14,10},{16,20},{18,... | collective-permute-start | bytes 786440 | tf_op jit(solution)/shard_map/ppermute | solution.py:47
  148.0 39.1 %collective-permute-start.3 = (bf16[4,512,512]{2,1,0:T(8,128)(2,1)}, bf16[4,512,512]{2,1,0:T(8,128)(2,1)}, u32[]{:S(2)}, u32[]{:S(2)}) collective-permute-start(bf16[4,512,512]{2,1,0:T(8,128)(2,1)} %maximum_select_fusion.2), channel_id=1, source_target_pairs={{0,32},{32,0},{64,96},{96,64},{128,160},{160,128},{192,224},{224,1... | collective-permute-start | bytes 6291464 | tf_op jit(solution)/shard_map/ppermute | solution.py:69
  149.2 14.4 %collective-permute-start.10 = (bf16[4,128,512]{2,1,0:T(8,128)(2,1)S(1)}, bf16[4,128,512]{2,1,0:T(8,128)(2,1)S(1)}, u32[]{:S(2)}, u32[]{:S(2)}) collective-permute-start(bf16[4,128,512]{2,1,0:T(8,128)(2,1)S(1)} %maximum_select_fusion.5), channel_id=1, source_target_pairs={{0,2},{2,0},{4,6},{6,4},{8,10},{10,8},{12,14},{14,12},{16,18},{18,... | collective-permute-start | bytes 1572872 | tf_op jit(solution)/shard_map/ppermute | solution.py:47
  167.3 10.7 %collective-permute-start.11 = (f32[128,256]{1,0:T(8,128)S(1)}, f32[128,256]{1,0:T(8,128)S(1)}, u32[]{:S(2)}, u32[]{:S(2)}) collective-permute-start(f32[128,256]{1,0:T(8,128)S(1)} %fusion.80), channel_id=1, source_target_pairs={{0,1},{1,0},{2,3},{3,2},{4,5},{5,4},{6,7},{7,6},{8,9},{9,8},{10,11... | collective-permute-start | bytes 393224 | tf_op jit(solution)/shard_map/ppermute | solution.py:34
  174.0 13.1 %collective-permute-start.4 = (f32[128,256]{1,0:T(8,128)S(1)}, f32[128,256]{1,0:T(8,128)S(1)}, u32[]{:S(2)}, u32[]{:S(2)}) collective-permute-start(f32[128,256]{1,0:T(8,128)S(1)} %fusion.41), channel_id=1, source_target_pairs={{0,1},{1,0},{2,3},{3,2},{4,5},{5,4},{6,7},{7,6},{8,9},{9,8},{10,11... | collective-permute-start | bytes 393224 | tf_op jit(solution)/shard_map/ppermute | solution.py:34
  193.6 3.4 copy-start.3
  199.4 3.5 copy-start.4
  205.6 7.7 %collective-permute-start.6 = (f32[2,2,64]{2,1,0:T(2,128)S(1)}, f32[2,2,64]{2,1,0:T(2,128)S(1)}, u32[]{:S(2)}, u32[]{:S(2)}) collective-permute-start(f32[2,2,64]{2,1,0:T(2,128)S(1)} %get-tuple-element.26), channel_id=1, source_target_pairs={{0,1},{1,0},{2,3},{3,2},{4,5},{5,4},{6,7},{7,6},{8,9},{9,8},{10,11... | collective-permute-start | bytes 3080 | tf_op jit(solution)/shard_map/ppermute | solution.py:34
  208.5 10.1 %collective-permute-start.5 = (f32[2,64,2,128]{3,1,2,0:T(8,128)S(1)}, f32[2,64,2,128]{3,1,2,0:T(8,128)S(1)}, u32[]{:S(2)}, u32[]{:S(2)}) collective-permute-start(f32[2,64,2,128]{3,1,2,0:T(8,128)S(1)} %convolution_bitcast_fusion.1), channel_id=1, source_target_pairs={{0,1},{1,0},{2,3},{3,2},{4,5},{5,4},{6,7},{7,6},{8,9},{9,8},{10,11... | collective-permute-start | bytes 393224 | tf_op jit(solution)/shard_map/ppermute | solution.py:34
  219.5 2.5 copy-start.1
  222.0 4.4 %copy-start.5 = (bf16[2,2,2,512,512]{4,3,2,1,0:T(8,128)(2,1)S(1)}, bf16[2,2,2,512,512]{4,3,2,1,0:T(8,128)(2,1)}, u32[]{:S(2)}) copy-start(bf16[2,2,2,512,512]{4,3,2,1,0:T(8,128)(2,1)} %copy.80) | copy-start | bytes 12582916
  222.9 9.6 %collective-permute-start.12 = (f32[2,64,2,128]{3,1,2,0:T(8,128)S(1)}, f32[2,64,2,128]{3,1,2,0:T(8,128)S(1)}, u32[]{:S(2)}, u32[]{:S(2)}) collective-permute-start(f32[2,64,2,128]{3,1,2,0:T(8,128)S(1)} %convolution_bitcast_fusion), channel_id=1, source_target_pairs={{0,1},{1,0},{2,3},{3,2},{4,5},{5,4},{6,7},{7,6},{8,9},{9,8},{10,11... | collective-permute-start | bytes 393224 | tf_op jit(solution)/shard_map/ppermute | solution.py:34
  226.4 1.6 copy-start.2
  229.8 2.8 copy-start.6
  329.8 16.3 %collective-permute-start.13 = (bf16[256,512]{1,0:T(8,128)(2,1)S(1)}, bf16[256,512]{1,0:T(8,128)(2,1)S(1)}, u32[]{:S(2)}, u32[]{:S(2)}) collective-permute-start(bf16[256,512]{1,0:T(8,128)(2,1)S(1)} %slice.60), channel_id=1, source_target_pairs={{0,1},{1,0},{2,3},{3,2},{4,5},{5,4},{6,7},{7,6},{8,9},{9,8},{10,11... | collective-permute-start | bytes 786440 | tf_op jit(solution)/shard_map/ppermute | solution.py:188
Sparse Core Ops, SparseCore 0:
  11.0 53.4 all-gather.3
  67.5 64.8 all-gather.5
  237.9 90.8 reduce-scatter.1

commit v16 on v12

--- a/solution.py
+++ b/solution.py
@@ -36,7 +36,8 @@
     pad_rows = jnp.zeros((tail_rows, hidden.shape[1]), jnp.bfloat16)
     query_rows = jnp.concatenate([hidden[tail_rows:], pad_rows], 0)
     grad_rows = jnp.concatenate([grad_out[tail_rows:], pad_rows], 0)
-    full_query = lax.all_gather(query_rows, "mp", axis=1, tiled=True)
+    full_rows = lax.all_gather(jnp.stack([query_rows, grad_rows]), "mp", axis=2, tiled=True)
+    full_query, full_grad = full_rows[0], full_rows[1]
     piece_rows = half // lax.axis_size("dp")
     kv_local = jnp.concatenate([w_key, w_value], axis=1)
     kv_piece = lax.dynamic_slice_in_dim(kv_local, me_dp * piece_rows, piece_rows, 0)
@@ -79,8 +80,6 @@
     ) - 1
     own_cols = recv_buf.reshape(owners * cap, -1)[own_owner * cap + own_rank]
     neighbours = lax.all_gather(own_cols, "mp", axis=1, tiled=True)
-    grad_rows, neighbours = lax.optimization_barrier((grad_rows, neighbours))
-    full_grad = lax.all_gather(grad_rows, "mp", axis=1, tiled=True)
 
     def this_half(x):
         return lax.dynamic_slice_in_dim(x, me_group * half, half, 1)

time: 394 us -> 340 us (0.86)
  waiting for transfers between devices: 262 us -> 226 us
  starting transfers between devices: 47.6 us -> 33.6 us
  matrix products: 25.4 us -> 19.4 us
    all_gather x2 -> x1, waiting for transfers between devices: 52.5 us -> 0.01 us  [per_device(): lax.all_gather(jnp.stack([query_rows, grad_rows]), 'mp', axis=2, tiled=True)]
    ppermute x3, starting transfers between devices: 14.6 us -> 1.69 us  [per_device(): other = lax.ppermute(held, 'dp', pairs)]
    ppermute x1, waiting for transfers between devices: 14.7 us -> 23.4 us  [per_device(): held = lax.ppermute(kv_piece, 'group', swap)[None]]
    dot_general x6, matrix products: 14.5 us -> 6.36 us  [contract(): lax.dot_general(left, right, (((1,), (1,)), ((), ())), preferred_element_...]
    ppermute x3, waiting for transfers between devices: 45.6 us -> 52 us  [per_device(): other = lax.ppermute(held, 'dp', pairs)]
    reduce_scatter x1, waiting for transfers between devices: 90.5 us -> 96.2 us  [per_device(): reduced = lax.psum_scatter(stacked, 'mp', scatter_dimension=1, tiled=True)]
    unnamed x29 -> x21, local copies, waits for them, and re-layouts: 6.16 us -> 1.58 us
    all_to_all x1, waiting for transfers between devices: 22.2 us -> 18 us  [per_device(): recv_buf = lax.all_to_all(send_buf, ('dp', 'group'), 0, 0, tiled=True)]
  transfers between devices with their start and end apart: 16 -> 15, of which waited for: 11 -> 13; matrix products, arithmetic and copies ran while one was open for 8% -> 10% of each run, Pallas kernels for 0% -> 0%
where the time goes in v16:
time: 340 us; the launch traced here: 337 us
  waiting for transfers between devices  226 us (66%)
  starting transfers between devices  33.6 us (10%)
  local copies, waits for them, and re-layouts  22.5 us (7%)
  other arithmetic  21.8 us (6%)
  matrix products  19.4 us (6%)
  between operations  14.2 us (4%)
    reduce_scatter x1, waiting for transfers between devices, per_device(): reduced = lax.psum_scatter(stacked, 'mp', scatter_dimension=1, tiled=True)  96.2 us
    ppermute x3, waiting for transfers between devices, per_device(): other = lax.ppermute(held, 'dp', pairs)  52 us
    ppermute x1, waiting for transfers between devices, per_device(): held = lax.ppermute(kv_piece, 'group', swap)[None]  23.4 us
    all_to_all x1, waiting for transfers between devices, per_device(): recv_buf = lax.all_to_all(send_buf, ('dp', 'group'), 0, 0, tiled=True)  18 us
    ppermute x5, waiting for transfers between devices, group_sum(): return x + lax.ppermute(x, 'group', swap)  17.8 us
    ppermute x1, waiting for transfers between devices, per_device(): lax.ppermute(both_cols, 'group', swap)  14.3 us
    ppermute x5, starting transfers between devices, group_sum(): return x + lax.ppermute(x, 'group', swap)  14.1 us
    select_n x3, other arithmetic, per_device(): jnp.where(low, jnp.concatenate([held, other], 0), jnp.concatenate([other,...  8.85 us
  transfers between devices with their start and end apart: 15, of which 13 were waited for; matrix products, arithmetic and copies ran while one was open for 10% of the time, Pallas kernels for 0%

profile of v16, /device:TPU:192, one launch (start us, length us, event | category | flops | bytes accessed | tf_op | source)
XLA Modules:
  0.0 337.5 jit_solution(3007873271737682520)
XLA Ops:
  11.3 6.3 %all-to-all-start = ((f32[16,1,256]{2,1,0:T(1,128)}), f32[16,1,256]{2,1,0:T(1,128)S(1)}, u32[]{:S(2)}, u32[]{:S(2)}) async-start(f32[16,1,256]{2,1,0:T(1,128)} %broadcast_in_dim.19), calls=%async_computation | async-start | bytes 32768 | tf_op jit(solution)/shard_map/all_to_all | solution.py:67
  17.6 4.2 %all-to-all-done = f32[16,1,256]{2,1,0:T(1,128)S(1)} async-done(((f32[16,1,256]{2,1,0:T(1,128)}), f32[16,1,256]{2,1,0:T(1,128)S(1)}, u32[]{:S(2)}, u32[]{:S(2)}) %all-to-all-start) | async-done | bytes 16416 | tf_op jit(solution)/shard_map/all_to_all | solution.py:67
  23.3 7.9 %gather_fusion = bf16[1024,512]{1,0:T(8,128)(2,1)} fusion(bf16[4096,512]{1,0:T(8,128)(2,1)} %param.12, s32[1024]{0:T(1024)S(1)} %broadcast_clamp_fusion), kind=kCustom, calls=%fused_computation | custom fusion | bytes 2101248 | tf_op jit(solution)/shard_map/gather | solution.py:74
  31.2 7.0 %all-to-all-start.1 = ((bf16[16,64,512]{2,1,0:T(8,128)(2,1)}), bf16[16,64,512]{2,1,0:T(8,128)(2,1)S(1)}, u32[]{:S(2)}, u32[]{:S(2)}) async-start(bf16[16,64,512]{2,1,0:T(8,128)(2,1)} %bitcast.113), calls=%async_computation.1 | async-start | bytes 2097152 | tf_op jit(solution)/shard_map/all_to_all | solution.py:75
  38.2 1.9 fusion.48
  40.1 2.4 collective-permute-start
  43.4 18.0 %all-to-all-done.1 = bf16[16,64,512]{2,1,0:T(8,128)(2,1)S(1)} async-done(((bf16[16,64,512]{2,1,0:T(8,128)(2,1)}), bf16[16,64,512]{2,1,0:T(8,128)(2,1)S(1)}, u32[]{:S(2)}, u32[]{:S(2)}) %all-to-all-start.1) | async-done | bytes 1048608 | tf_op jit(solution)/shard_map/all_to_all | solution.py:75
  61.4 1.9 gather_fusion.1
  63.3 23.4 %collective-permute-done = bf16[512,512]{1,0:T(8,128)(2,1)} collective-permute-done((bf16[512,512]{1,0:T(8,128)(2,1)}, bf16[512,512]{1,0:T(8,128)(2,1)}, u32[]{:S(2)}, u32[]{:S(2)}) %collective-permute-start) | collective-permute-done | bytes 524320 | tf_op jit(solution)/shard_map/ppermute | solution.py:44
  86.8 23.7 %collective-permute-done.1 = bf16[1,512,512]{2,1,0:T(8,128)(2,1)} collective-permute-done((bf16[1,512,512]{2,1,0:T(8,128)(2,1)}, bf16[1,512,512]{2,1,0:T(8,128)(2,1)}, u32[]{:S(2)}, u32[]{:S(2)}) %collective-permute-start.1) | collective-permute-done | bytes 524320 | tf_op jit(solution)/shard_map/ppermute | solution.py:49
  113.9 23.9 %collective-permute-done.2 = bf16[2,512,512]{2,1,0:T(8,128)(2,1)} collective-permute-done((bf16[2,512,512]{2,1,0:T(8,128)(2,1)S(1)}, bf16[2,512,512]{2,1,0:T(8,128)(2,1)}, u32[]{:S(2)}, u32[]{:S(2)}) %collective-permute-start.2) | collective-permute-done | bytes 1048608 | tf_op jit(solution)/shard_map/ppermute | solution.py:49
  137.8 3.2 maximum_select_fusion.2
  141.0 4.5 %collective-permute-done.3 = bf16[4,512,512]{2,1,0:T(8,128)(2,1)} collective-permute-done((bf16[4,512,512]{2,1,0:T(8,128)(2,1)}, bf16[4,512,512]{2,1,0:T(8,128)(2,1)}, u32[]{:S(2)}, u32[]{:S(2)}) %collective-permute-start.3) | collective-permute-done | bytes 2097184 | tf_op jit(solution)/shard_map/ppermute | solution.py:49
  145.5 3.8 %maximum_select_fusion.1 = bf16[8,512,512]{2,1,0:T(8,128)(2,1)S(1)} fusion(bf16[4,512,512]{2,1,0:T(8,128)(2,1)} %collective-permute-done.3, bf16[4,512,512]{2,1,0:T(8,128)(2,1)} %maximum_select_fusion.2, pred[]{:T(512)S(6)} %eq.62), kind=kLoop, calls=%fused_computation.11 | loop fusion | flops 6291456 | bytes 8388609 | tf_op jit(solution)/shard_map/jit(_where)/select_n | solution.py:51
  149.4 2.4 copy.75
  151.8 2.6 fusion.82
  155.3 3.3 collective-permute-start.7
  159.1 2.8 collective-permute-start.4
  161.9 3.1 collective-permute-done.7
  165.0 4.7 %collective-permute-done.4 = f32[128,256]{1,0:T(8,128)S(1)} collective-permute-done((f32[128,256]{1,0:T(8,128)S(1)}, f32[128,256]{1,0:T(8,128)S(1)}, u32[]{:S(2)}, u32[]{:S(2)}) %collective-permute-start.4) | collective-permute-done | bytes 131104 | tf_op jit(solution)/shard_map/ppermute | solution.py:34
  169.8 3.1 fusion.12
  173.2 2.4 fusion.25
  175.7 3.1 fusion.10
  179.1 2.3 fusion.30
  181.8 4.6 %collective-permute-start.6 = (f32[2,2,64]{2,1,0:T(2,128)S(1)}, f32[2,2,64]{2,1,0:T(2,128)S(1)}, u32[]{:S(2)}, u32[]{:S(2)}) collective-permute-start(f32[2,2,64]{2,1,0:T(2,128)S(1)} %get-tuple-element.28), channel_id=1, source_target_pairs={{0,1},{1,0},{2,3},{3,2},{4,5},{5,4},{6,7},{7,6},{8,9},{9,8},{10,11... | collective-permute-start | bytes 3080 | tf_op jit(solution)/shard_map/ppermute | solution.py:34
  190.0 5.6 %collective-permute-done.5 = f32[2,64,2,128]{3,1,2,0:T(8,128)S(1)} collective-permute-done((f32[2,64,2,128]{3,1,2,0:T(8,128)S(1)}, f32[2,64,2,128]{3,1,2,0:T(8,128)S(1)}, u32[]{:S(2)}, u32[]{:S(2)}) %collective-permute-start.5) | collective-permute-done | bytes 131104 | tf_op jit(solution)/shard_map/ppermute | solution.py:34
  196.5 2.5 fusion.4
  205.8 3.0 collective-permute-done.8
  210.2 3.7 %pad_maximum_fusion = bf16[512,8192]{1,0:T(8,128)(2,1)} fusion(bf16[256,8192]{1,0:T(8,128)(2,1)S(1)} %fusion, bf16[128,8192]{1,0:T(8,128)(2,1)S(1)} %pad_select_fusion, bf16[128,8192]{1,0:T(8,128)(2,1)S(1)} %pad_select_fusion.1), kind=kLoop, calls=%fused_computation.4 | loop fusion | flops 25165824 | bytes 16777216 | tf_op jit(solution)/shard_map/concatenate | solution.py:158
  214.0 96.2 %reduce-scatter.2.cloned.1.call-done = bf16[512,512]{1,0:T(8,128)(2,1)} async-done(((bf16[512,8192]{1,0:T(8,128)(2,1)}), bf16[512,512]{1,0:T(8,128)(2,1)}) %reduce-scatter.2.cloned.1.call-update) | async-done | bytes 524304 | tf_op jit(solution)/shard_map/reduce_scatter | solution.py:166
  311.2 2.0 collective-permute-start.9
  313.2 14.3 %collective-permute-done.9 = bf16[256,512]{1,0:T(8,128)(2,1)S(1)} collective-permute-done((bf16[256,512]{1,0:T(8,128)(2,1)S(1)}, bf16[256,512]{1,0:T(8,128)(2,1)S(1)}, u32[]{:S(2)}, u32[]{:S(2)}) %collective-permute-start.9) | collective-permute-done | bytes 262176 | tf_op jit(solution)/shard_map/ppermute | solution.py:168
  (101 shorter events, 29.4 us)
Async XLA Ops:
  7.2 147.3 %copy-start = (bf16[256,4096]{1,0:T(8,128)(2,1)S(1)}, bf16[256,4096]{1,0:T(8,128)(2,1)}, u32[]{:S(2)}) copy-start(bf16[256,4096]{1,0:T(8,128)(2,1)} %param.16) | copy-start | bytes 6291460
  7.2 144.6 %all-gather.4.cloned.1.call-start = ((), (), s32[]{:S(2)}) async-start(), calls=%async_computation.3 | async-start | bytes 4456448 | tf_op jit(solution)/shard_map/all_gather | solution.py:39
  11.3 10.6 %all-to-all-start = ((f32[16,1,256]{2,1,0:T(1,128)}), f32[16,1,256]{2,1,0:T(1,128)S(1)}, u32[]{:S(2)}, u32[]{:S(2)}) async-start(f32[16,1,256]{2,1,0:T(1,128)} %broadcast_in_dim.19), calls=%async_computation | async-start | bytes 32768 | tf_op jit(solution)/shard_map/all_to_all | solution.py:67
  31.2 30.2 %all-to-all-start.1 = ((bf16[16,64,512]{2,1,0:T(8,128)(2,1)}), bf16[16,64,512]{2,1,0:T(8,128)(2,1)S(1)}, u32[]{:S(2)}, u32[]{:S(2)}) async-start(bf16[16,64,512]{2,1,0:T(8,128)(2,1)} %bitcast.113), calls=%async_computation.1 | async-start | bytes 2097152 | tf_op jit(solution)/shard_map/all_to_all | solution.py:75
  38.1 131.6 %all-gather.6.cloned.1.call-start = ((), (), s32[]{:S(2)}) async-start(), calls=%async_computation.5 | async-start | bytes 4456448 | tf_op jit(solution)/shard_map/all_gather | solution.py:82
  38.2 4.2 %copy-start.8 = (s32[2,1,128]{2,1,0:T(1,128)S(1)}, s32[2,1,128]{2,1,0:T(1,128)}, u32[]{:S(2)}) copy-start(s32[2,1,128]{2,1,0:T(1,128)} %param.10) | copy-start | bytes 3076
  40.1 46.7 %collective-permute-start = (bf16[512,512]{1,0:T(8,128)(2,1)}, bf16[512,512]{1,0:T(8,128)(2,1)}, u32[]{:S(2)}, u32[]{:S(2)}) collective-permute-start(bf16[512,512]{1,0:T(8,128)(2,1)} %fusion.48), channel_id=1, source_target_pairs={{0,1},{1,0},{2,3},{3,2},{4,5},{5,4},{6,7},{7,6},{8,9},{9,8},{10,11... | collective-permute-start | bytes 1572872 | tf_op jit(solution)/shard_map/ppermute | solution.py:44
  63.3 246.9 %reduce-scatter.2.cloned.1.call-start = ((), (), s32[]{:S(2)}) async-start(), calls=%async_computation.4 | async-start | bytes 8912896 | tf_op jit(solution)/shard_map/reduce_scatter | solution.py:166
  86.8 23.7 %collective-permute-start.1 = (bf16[1,512,512]{2,1,0:T(8,128)(2,1)}, bf16[1,512,512]{2,1,0:T(8,128)(2,1)}, u32[]{:S(2)}, u32[]{:S(2)}) collective-permute-start(bf16[1,512,512]{2,1,0:T(8,128)(2,1)} %bitcast.10), channel_id=1, source_target_pairs={{0,128},{32,160},{64,192},{96,224},{128,0},{160,32},{192,64},{224,... | collective-permute-start | bytes 1572872 | tf_op jit(solution)/shard_map/ppermute | solution.py:49
  112.2 25.6 %collective-permute-start.2 = (bf16[2,512,512]{2,1,0:T(8,128)(2,1)S(1)}, bf16[2,512,512]{2,1,0:T(8,128)(2,1)}, u32[]{:S(2)}, u32[]{:S(2)}) collective-permute-start(bf16[2,512,512]{2,1,0:T(8,128)(2,1)S(1)} %maximum_select_fusion.3), channel_id=1, source_target_pairs={{0,64},{32,96},{64,0},{96,32},{128,192},{160,224},{192,128},{224,1... | collective-permute-start | bytes 3145736 | tf_op jit(solution)/shard_map/ppermute | solution.py:49
  113.9 27.1 %copy-start.9 = (s32[2]{0:T(128)S(1)}, s32[2]{0:T(128)}, u32[]{:S(2)}) copy-start(s32[2]{0:T(128)} %param.11) | copy-start | bytes 28
  141.0 4.5 %collective-permute-start.3 = (bf16[4,512,512]{2,1,0:T(8,128)(2,1)}, bf16[4,512,512]{2,1,0:T(8,128)(2,1)}, u32[]{:S(2)}, u32[]{:S(2)}) collective-permute-start(bf16[4,512,512]{2,1,0:T(8,128)(2,1)} %maximum_select_fusion.2), channel_id=1, source_target_pairs={{0,32},{32,0},{64,96},{96,64},{128,160},{160,128},{192,224},{224,1... | collective-permute-start | bytes 6291464 | tf_op jit(solution)/shard_map/ppermute | solution.py:49
  154.5 4.2 %copy-start.6 = (bf16[4096,256]{1,0:T(8,128)(2,1)S(1)}, bf16[4096,256]{1,0:T(8,128)(2,1)}, u32[]{:S(2)}) copy-start(bf16[4096,256]{1,0:T(8,128)(2,1)} %param.13) | copy-start | bytes 6291460
  155.3 9.7 %collective-permute-start.7 = (f32[128,256]{1,0:T(8,128)S(1)}, f32[128,256]{1,0:T(8,128)S(1)}, u32[]{:S(2)}, u32[]{:S(2)}) collective-permute-start(f32[128,256]{1,0:T(8,128)S(1)} %fusion.41), channel_id=1, source_target_pairs={{0,1},{1,0},{2,3},{3,2},{4,5},{5,4},{6,7},{7,6},{8,9},{9,8},{10,11... | collective-permute-start | bytes 393224 | tf_op jit(solution)/shard_map/ppermute | solution.py:34
  159.1 10.6 %collective-permute-start.4 = (f32[128,256]{1,0:T(8,128)S(1)}, f32[128,256]{1,0:T(8,128)S(1)}, u32[]{:S(2)}, u32[]{:S(2)}) collective-permute-start(f32[128,256]{1,0:T(8,128)S(1)} %fusion.43), channel_id=1, source_target_pairs={{0,1},{1,0},{2,3},{3,2},{4,5},{5,4},{6,7},{7,6},{8,9},{9,8},{10,11... | collective-permute-start | bytes 393224 | tf_op jit(solution)/shard_map/ppermute | solution.py:34
  169.8 3.5 %copy-start.3 = (bf16[2,2,2,512,512]{4,3,2,1,0:T(8,128)(2,1)S(1)}, bf16[2,2,2,512,512]{4,3,2,1,0:T(8,128)(2,1)}, u32[]{:S(2)}) copy-start(bf16[2,2,2,512,512]{4,3,2,1,0:T(8,128)(2,1)} %copy.75) | copy-start | bytes 12582916
  175.7 3.5 %copy-start.4 = (bf16[2,2,2,512,512]{4,3,2,1,0:T(8,128)(2,1)S(1)}, bf16[2,2,2,512,512]{4,3,2,1,0:T(8,128)(2,1)}, u32[]{:S(2)}) copy-start(bf16[2,2,2,512,512]{4,3,2,1,0:T(8,128)(2,1)} %copy.75) | copy-start | bytes 12582916
  181.8 7.8 %collective-permute-start.6 = (f32[2,2,64]{2,1,0:T(2,128)S(1)}, f32[2,2,64]{2,1,0:T(2,128)S(1)}, u32[]{:S(2)}, u32[]{:S(2)}) collective-permute-start(f32[2,2,64]{2,1,0:T(2,128)S(1)} %get-tuple-element.28), channel_id=1, source_target_pairs={{0,1},{1,0},{2,3},{3,2},{4,5},{5,4},{6,7},{7,6},{8,9},{9,8},{10,11... | collective-permute-start | bytes 3080 | tf_op jit(solution)/shard_map/ppermute | solution.py:34
  186.6 9.0 %collective-permute-start.5 = (f32[2,64,2,128]{3,1,2,0:T(8,128)S(1)}, f32[2,64,2,128]{3,1,2,0:T(8,128)S(1)}, u32[]{:S(2)}, u32[]{:S(2)}) collective-permute-start(f32[2,64,2,128]{3,1,2,0:T(8,128)S(1)} %convolution_bitcast_fusion.1), channel_id=1, source_target_pairs={{0,1},{1,0},{2,3},{3,2},{4,5},{5,4},{6,7},{7,6},{8,9},{9,8},{10,11... | collective-permute-start | bytes 393224 | tf_op jit(solution)/shard_map/ppermute | solution.py:34
  196.5 2.5 copy-start.1
  199.0 3.0 copy-start.5
  199.9 9.0 %collective-permute-start.8 = (f32[2,64,2,128]{3,1,2,0:T(8,128)S(1)}, f32[2,64,2,128]{3,1,2,0:T(8,128)S(1)}, u32[]{:S(2)}, u32[]{:S(2)}) collective-permute-start(f32[2,64,2,128]{3,1,2,0:T(8,128)S(1)} %convolution_bitcast_fusion), channel_id=1, source_target_pairs={{0,1},{1,0},{2,3},{3,2},{4,5},{5,4},{6,7},{7,6},{8,9},{9,8},{10,11... | collective-permute-start | bytes 393224 | tf_op jit(solution)/shard_map/ppermute | solution.py:34
  202.1 1.6 copy-start.2
  205.4 3.6 %copy-start.7 = (bf16[4096,256]{1,0:T(8,128)(2,1)S(1)}, bf16[4096,256]{1,0:T(8,128)(2,1)}, u32[]{:S(2)}) copy-start(bf16[4096,256]{1,0:T(8,128)(2,1)} %param.13) | copy-start | bytes 6291460
  311.2 16.4 %collective-permute-start.9 = (bf16[256,512]{1,0:T(8,128)(2,1)S(1)}, bf16[256,512]{1,0:T(8,128)(2,1)S(1)}, u32[]{:S(2)}, u32[]{:S(2)}) collective-permute-start(bf16[256,512]{1,0:T(8,128)(2,1)S(1)} %slice.70), channel_id=1, source_target_pairs={{0,1},{1,0},{2,3},{3,2},{4,5},{5,4},{6,7},{7,6},{8,9},{9,8},{10,11... | collective-permute-start | bytes 786440 | tf_op jit(solution)/shard_map/ppermute | solution.py:168
Sparse Core Ops, SparseCore 0:
  11.0 63.3 all-gather.3
  77.4 73.6 all-gather.5
  214.1 96.0 reduce-scatter.1
